TPU v7x, 256 devices: a whole 4x4x8 slice. The times are simulated.
256 devices in a mesh: depth: 32 (over x, z_hi, core), filt: 8 (over z_lo, y).
Axes of the slice: x: 4, y: 4, z: 8 (z_hi: 4, z_lo: 2; z = z_hi * 2 + z_lo), core: 2. Of those that a mesh axis runs over, the one named last changes fastest.
Arguments:
- volume: bfloat16 [256, 32, 4096], P('filt', 'depth'), may hold values from -6 to 6
- kernel: bfloat16 [27, 256, 256], P(None, 'filt'), may hold values from -0.078125 to 0.078125
- bias: float32 [256], P('filt'), may hold values from -3 to 3
- cotangent: bfloat16 [256, 32, 4096], P('filt', 'depth'), may hold values from -6 to 6
Outputs:
- activated: bfloat16 [256, 32, 4096], P('filt', 'depth')
- input_grad: bfloat16 [256, 32, 4096], P('filt', 'depth')
- kernel_grad: float32 [27, 256, 256], P(None, 'filt')
- bias_grad: float32 [256], P('filt')
All inputs are finite; a program needn't handle non-finite values.
Results may differ from a plain program's by a relative error of at most 0.0055.
Values may be sent and summed in bfloat16 or wider, within the bound.
No kernel may reach another device: no remote copies, remote signals or barrier semaphores. Data moves between devices by JAX's collectives and lax.ppermute only.
A program may use at most 64 MiB of HBM per device.

v0:
```python
import jax
import jax.numpy as jnp
from jax import lax
from jax.sharding import PartitionSpec as P

WIDTH = 64


def extended(block, sides, width):
    for axis, dim in sides:
        count = lax.axis_size(axis)
        forward = [(i, i + 1) for i in range(count - 1)]
        backward = [(target, source) for source, target in forward]
        low = lax.ppermute(
            lax.slice_in_dim(block, block.shape[dim] - width, None, axis=dim), axis, forward
        )
        high = lax.ppermute(lax.slice_in_dim(block, 0, width, axis=dim), axis, backward)
        block = jnp.concatenate([low, block, high], axis=dim)
    return block


def shift_out(values, down_by, right_by):
    length = values.shape[-1]
    offset = down_by * WIDTH + right_by
    if offset > 0:
        filler = jnp.zeros(values.shape[:-1] + (offset,), values.dtype)
        moved = jnp.concatenate([values[..., offset:], filler], axis=-1)
    elif offset < 0:
        filler = jnp.zeros(values.shape[:-1] + (-offset,), values.dtype)
        moved = jnp.concatenate([filler, values[..., : length + offset]], axis=-1)
    else:
        moved = values
    column = jnp.arange(length, dtype=jnp.int32) % WIDTH
    inside = (column + right_by >= 0) & (column + right_by < WIDTH)
    return jnp.where(inside, moved, jnp.zeros((), values.dtype))


def smooth_gate(values):
    return jax.nn.gelu(values, approximate=True)


def data_grad(columns, grads):
    planes_dev = grads.shape[1] - 2
    shifted = []
    for depth_tap in range(3):
        grad_planes = grads[:, 2 - depth_tap : 2 - depth_tap + planes_dev]
        for plane_tap in range(9):
            shifted.append(shift_out(grad_planes, 1 - plane_tap // 3, 1 - plane_tap % 3))
    stacked = jnp.stack(shifted, axis=0)
    return jnp.einsum("koc,kodp->cdp", columns, stacked, preferred_element_type=jnp.float32)


def local(volume, kernel, bias, cotangent):
    planes_dev = volume.shape[1]
    rimmed = extended(volume, (("depth", 1),), 1)
    widened = lax.all_gather(rimmed, "filt", axis=0, tiled=True)
    preact = jnp.zeros(volume.shape, jnp.float32) + bias[:, None, None]
    for depth_tap in range(3):
        planes = widened[:, depth_tap : depth_tap + planes_dev]
        products = jnp.einsum(
            "koc,cdp->kodp",
            kernel[9 * depth_tap : 9 * depth_tap + 9],
            planes,
            preferred_element_type=jnp.float32,
        )
        for plane_tap in range(9):
            preact = preact + shift_out(products[plane_tap], plane_tap // 3 - 1, plane_tap % 3 - 1)
    activation, pullback = jax.vjp(smooth_gate, preact)
    activated = activation.astype(jnp.bfloat16)
    grad_pre = pullback(cotangent.astype(jnp.float32))[0].astype(jnp.bfloat16)
    padded_grad = extended(grad_pre, (("depth", 1),), 1)
    stacked = jnp.stack(
        [shift_out(grad_pre, 1 - plane_tap // 3, 1 - plane_tap % 3) for plane_tap in range(9)],
        axis=0,
    )
    partials = []
    for depth_tap in range(3):
        planes = widened[:, depth_tap : depth_tap + planes_dev]
        partials.append(
            jnp.einsum("kodp,cdp->koc", stacked, planes, preferred_element_type=jnp.float32)
        )
    local_kernel_grad = jnp.concatenate(partials, axis=0)
    local_bias_grad = jnp.sum(grad_pre.astype(jnp.float32), axis=(1, 2))
    kernel_grad, bias_grad = lax.psum((local_kernel_grad, local_bias_grad), "depth")
    input_grad = lax.psum_scatter(
        data_grad(kernel, padded_grad), "filt", scatter_dimension=0, tiled=True
    )
    return (activated, input_grad.astype(jnp.bfloat16), kernel_grad, bias_grad)


def solution(mesh):
    placed = (P("filt", "depth", None), P(None, "filt", None), P("filt"), P("filt", "depth", None))
    return jax.shard_map(
        local,
        mesh=mesh,
        in_specs=placed,
        out_specs=(
            P("filt", "depth", None),
            P("filt", "depth", None),
            P(None, "filt", None),
            P("filt"),
        ),
        check_vma=False,
    )
```

profile of v0, /device:TPU:32, one launch (start us, length us, event | category | flops | bytes accessed | tf_op | source)
XLA Modules:
  0.0 899.4 jit_solution(8102236298506291788)
XLA Ops:
  7.2 1.8 collective-permute-start
  9.0 1.3 collective-permute-start.1
  10.3 5.3 collective-permute-done.1
  15.7 1.9 pad_maximum_fusion.1
  17.6 1.3 dynamic-slice
  19.6 81.1 %all-gather.2.cloned.1.call-done = bf16[256,3,4096]{2,0,1:T(8,128)(2,1)} async-done(((bf16[32,3,4096]{2,0,1:T(8,128)(2,1)}), bf16[256,3,4096]{2,0,1:T(8,128)(2,1)}) %all-gather.2.cloned.1.call-update) | async-done | bytes 6291472 | tf_op jit(solution)/shard_map/all_gather | solution.py:56
  100.7 2.5 convolution_bitcast_fusion.2
  103.3 0.4 slice_bitcast_fusion.35
  103.7 0.2 slice.373
  103.9 0.2 slice.375
  104.1 0.2 slice.377
  104.3 0.2 slice.379
  104.6 0.4 slice-done.1
  105.0 0.8 convolution_bitcast_fusion.1
  105.7 0.4 slice_bitcast_fusion.26
  106.2 0.2 slice.391
  106.8 0.2 slice.397
  107.0 0.8 convolution_bitcast_fusion
  107.8 0.4 slice_bitcast_fusion.17
  108.3 0.2 slice.409
  108.5 0.2 slice.411
  108.7 0.2 slice.413
  108.9 0.2 slice.415
  109.1 2.2 convert_reduce_fusion
  111.3 1.3 collective-permute-start.2
  113.2 3.0 collective-permute-start.3
  116.3 0.9 multiply_convert_fusion
  117.1 75.8 %psum.15 = f32[32]{0:T(128)} all-reduce(f32[32]{0:T(128)S(1)} %get-tuple-element.12), channel_id=1, replica_groups=mesh['depth'=32,'filt'=8] {'depth'}, use_global_device_ids=true, to_apply=%region_3.4 | all-reduce | flops 32 | bytes 256 | tf_op jit(solution)/shard_map/psum | solution.py:84
  195.3 0.9 slice-done.3
  196.2 0.8 fusion.5
  197.0 0.8 fusion.7
  197.8 0.8 fusion.9
  198.7 1.0 pad_maximum_fusion
  199.8 0.7 bitcast_dynamic-update-slice_fusion.8
  200.7 0.8 bitcast_dynamic-update-slice_fusion.7
  201.6 0.8 bitcast_dynamic-update-slice_fusion.6
  202.5 0.8 bitcast_dynamic-update-slice_fusion.5
  203.3 0.8 bitcast_dynamic-update-slice_fusion.4
  204.1 0.9 bitcast_dynamic-update-slice_fusion.3
  204.9 0.8 bitcast_dynamic-update-slice_fusion.2
  205.8 0.9 bitcast_dynamic-update-slice_fusion.1
  206.6 0.8 bitcast_dynamic-update-slice_fusion
  207.5 7.5 fusion.2
  215.0 10.2 %copy.9 = f32[256,1,4096]{2,1,0:T(1,128)} copy(f32[256,1,4096]{0,2,1:T(8,128)} %fusion.2) | data formatting | bytes 8388608 | tf_op jit(solution)/shard_map/koc,kodp->cdp/dot_general | solution.py:50
  225.2 662.7 %all-reduce.53 = bf16[256,1,4096]{2,1,0:T(2,128)(2,1)} all-reduce(f32[256,1,4096]{2,1,0:T(1,128)} %copy.9), channel_id=2, replica_groups=mesh['depth'=32,'filt'=8] {'filt'}, use_global_device_ids=true, to_apply=%region_0.1.clone | all-reduce | flops 1048576 | bytes 6291456
  887.8 1.6 dynamic-slice_convert_fusion
  889.4 1.0 copy.10
  890.4 2.2 copy.48
  (58 shorter events, 4.0 us)
Async XLA Ops:
  7.2 93.6 %all-gather.2.cloned.1.call-start = ((), (), s32[]{:S(2)}) async-start(), calls=%async_computation | async-start | bytes 7077888 | tf_op jit(solution)/shard_map/all_gather | solution.py:56
  7.2 3.1 collective-permute-start
  9.0 6.7 collective-permute-start.1
  17.6 872.8 %all-reduce.52.cloned.1.call-start = ((), (), s32[]{:S(2)}) async-start(), calls=%async_computation.1 | async-start | bytes 1769472 | tf_op jit(solution)/shard_map/psum | solution.py:84
  100.7 3.8 slice-start
  103.3 1.7 slice-start.1
  103.3 1.7 copy-start.3
  107.8 1.3 copy-start
  107.8 1.3 copy-start.2
  111.3 81.6 %collective-permute-start.2 = (bf16[32,1,4096]{2,0,1:T(8,128)(2,1)S(1)}, bf16[32,1,4096]{2,0,1:T(8,128)(2,1)S(1)}, u32[]{:S(2)}, u32[]{:S(2)}) collective-permute-start(bf16[32,1,4096]{2,0,1:T(8,128)(2,1)S(1)} %get-tuple-element.13), channel_id=1, source_target_pairs={{8,0},{16,8},{24,16},{32,24},{40,32},{48,40},{56,48},{64,56},{72,6... | collective-permute-start | bytes 786440 | tf_op jit(solution)/shard_map/ppermute | solution.py:17
  113.2 86.5 %collective-permute-start.3 = (bf16[32,1,4096]{2,0,1:T(8,128)(2,1)S(1)}, bf16[32,1,4096]{2,0,1:T(8,128)(2,1)S(1)}, u32[]{:S(2)}, u32[]{:S(2)}) collective-permute-start(bf16[32,1,4096]{2,0,1:T(8,128)(2,1)S(1)} %get-tuple-element.13), channel_id=1, source_target_pairs={{0,8},{8,16},{16,24},{24,32},{32,40},{40,48},{48,56},{56,64},{64,7... | collective-permute-start | bytes 786440 | tf_op jit(solution)/shard_map/ppermute | solution.py:14
  193.1 2.2 slice-start.2
  194.3 2.0 slice-start.3
  195.3 3.3 copy-start.1
Sparse Core Ops, SparseCore 0:
  17.7 82.9 all-gather.1
  199.8 276.6 all-reduce.51
where the time goes:
time: 900 us; the launch traced here: 899 us
  blocking collectives  738 us (82%)
  waiting for transfers between devices  86.5 us (10%)
  local copies, waits for them, and re-layouts  23 us (3%)
  between operations  15.1 us (2%)
  other arithmetic  14.9 us (2%)
  matrix products  14 us (2%)
    unnamed x1, blocking collectives  663 us
    all_gather x1, waiting for transfers between devices, local(): widened = lax.all_gather(rimmed, 'filt', axis=0, tiled=True)  81.1 us
    psum x1, blocking collectives, local(): lax.psum((local_kernel_grad, local_bias_grad), 'depth')  75.8 us
  transfers between devices with their start and end apart: 6, of which 2 were waited for; matrix products, arithmetic and copies ran while one was open for 4% of the time, Pallas kernels for 0%

commit v1 on v0

v1 whole, which is shorter than its diff:
```python
import jax
import jax.numpy as jnp
from jax import lax
from jax.experimental import pallas as pl
from jax.experimental.pallas import tpu as pltpu
from jax.sharding import PartitionSpec as P


BF = jnp.bfloat16
F32 = jnp.float32
ROW = 64
OWN = 32 * ROW
GWIN = 34 * ROW
VWIN = 36 * ROW
VMEM = pl.BlockSpec(memory_space=pltpu.VMEM)
SMEM = pl.BlockSpec(memory_space=pltpu.SMEM)
HBM = pl.BlockSpec(memory_space=pltpu.HBM)
PEERS = (1, 3, 2)
STEPS = (0,) + PEERS


def peer(index, s):
    return 3 - index if s == 3 else index ^ s


def pairs(move):
    found = []
    for i in range(256):
        x, h, c, z, y = i // 64, i // 16 % 4, i // 8 % 2, i // 4 % 2, i % 4
        to = move(x, h, c, z, y)
        if to is not None:
            x, h, c, z, y = to
            found.append((i, (((x % 4) * 4 + h % 4) * 2 + c % 2) * 8 + z % 2 * 4 + y % 4))
    return found


def far_plane(x, h, c, z, y):
    plane = x * 8 + h * 2 + z + (1 if z else -1)
    return (plane // 8, plane // 2 % 4, c, plane % 2, y) if 0 <= plane < 32 else None


def straight(x, h, c, z, y):
    return x, h, z, c, y


def crossed_in(x, h, c, z, y):
    return x, h, 1 - z, c, y


def crossed_out(x, h, c, z, y):
    return x, h, z, 1 - c, y


def other_core(x, h, c, z, y):
    return x, h, 1 - c, z, y


def other_z(x, h, c, z, y):
    return x, h, c, 1 - z, y


def pair_h(x, h, c, z, y):
    return x, h ^ 1, c, z, y


def mirror_h(x, h, c, z, y):
    return x, 3 - h, c, z, y


def pair_zh(x, h, c, z, y):
    return x, h ^ 1, c, 1 - z, y


def peer_x(s):
    return lambda x, h, c, z, y: (peer(x, s), h, c, z, y)


def peer_y(s):
    return lambda x, h, c, z, y: (x, h, c, z, peer(y, s))


def exchange(value, move):
    return lax.ppermute(value, ("depth", "filt"), pairs(move))


def shape(*dims, dtype=BF):
    return jax.ShapeDtypeStruct(dims, dtype)


def call(body, outs, scratch, *args, flops=0, moved=2_000_000, room=4, hbm_in=(), hbm_out=()):
    return pl.pallas_call(
        body,
        out_shape=outs,
        in_specs=[SMEM] + [HBM if i in hbm_in else VMEM for i in range(1, len(args))],
        out_specs=tuple(HBM if i in hbm_out else VMEM for i in range(len(outs))),
        scratch_shapes=scratch,
        compiler_params=pltpu.CompilerParams(vmem_limit_bytes=room * 1024 * 1024),
        cost_estimate=pl.CostEstimate(flops=flops, bytes_accessed=moved, transcendentals=0),
    )(*args)


def at(index, size):
    return pl.ds(pl.multiple_of(index * size, size), size)


Z, Y, C, X = range(4)


def shifted_columns(values, by):
    if by == 0:
        return values
    moved = pltpu.roll(values, (-by) % values.shape[1], 1)
    column = lax.broadcasted_iota(jnp.int32, values.shape, 1) % ROW
    inside = column < ROW - 1 if by > 0 else column > 0
    return jnp.where(inside, moved, jnp.zeros_like(moved))


def prepare_body(place, mine, partner, partner_rest, forward, backward, filters):
    z, c = place[Z], place[C]
    for k in range(27):
        filters[k, at(z, 32), :] = mine[k]
        filters[k, at(1 - z, 32), at(c, 128)] = partner[k]
        filters[k, at(1 - z, 32), at(1 - c, 128)] = partner_rest[k]
    for k in range(27):
        a, b, d = k // 9, k // 3 % 3, k % 3
        row = (d * 3 + a) * 64
        forward[row : row + 64, 256 * b : 256 * b + 256] = filters[k]
    for k in range(0, 27, 2):
        two = filters[k : min(k + 2, 27)].reshape(-1, 256)
        backward[:, 64 * k : 64 * k + two.shape[0]] = two.T


def forward_body(place, *refs):
    shards, weights = refs[:4], refs[4]
    near, mid, far, own = refs[5:9]
    window, moved, sem = refs[9:]
    y, c = place[Y], place[C]
    window[:, pl.ds(pl.multiple_of(GWIN * c, 128), 128)] = jnp.zeros((256, 128), BF)
    start = pl.ds(pl.multiple_of(128 * (1 - c), 128), GWIN)
    for s, shard in zip(STEPS, shards, strict=True):
        for i in range(2):
            block = (c + i) % 2 * 4 + peer(y, s)
            window[at(block, 32), start] = shard[32 * i : 32 * i + 32, :]
    keep = pltpu.make_async_copy(window.at[:, 2 * ROW : 2 * ROW + OWN], own, sem)
    keep.start()

    def build(i, _):
        moved[at(i, 32), :] = window[at(i, 32), :][:, ROW : ROW + GWIN]
        return 0

    lax.fori_loop(0, 8, build, 0)
    for n in range(0, GWIN, 256):
        size = min(256, GWIN - n)
        planes = (window[:, n : n + size], moved[:, n : n + size], window[:, n + 128 : n + 128 + size])
        got = jnp.dot(weights[...], jnp.concatenate(planes), preferred_element_type=F32)
        total = shifted_columns(got[:192], -1) + got[192:384] + shifted_columns(got[384:], 1)
        cells = slice(n, n + size)
        to_next, to_last = total[:64].astype(BF), total[128:].astype(BF)
        near[:, cells] = jnp.where(place[Z] == 0, to_next, to_last)
        mid[:, cells] = total[64:128]
        far[:, cells] = jnp.where(place[Z] == 0, to_last, to_next)
    keep.wait()


def gelu_parts(mid, near, far, bias):
    v = mid[...] + bias[...] + near[...].astype(F32) + far[...].astype(F32)
    square = v * v
    t = jnp.tanh(0.7978845608028654 * (v + 0.044715 * (square * v)))
    return v, square, t


def grad_body(place, mid, near, far, bias, cot_own, cot_other, grad, sums, cot):
    c = place[C]
    cot[at(c, 32), :] = cot_own[...]
    cot[at(1 - c, 32), :] = cot_other[...]
    v, square, t = gelu_parts(mid, near, far, bias)
    inner = 0.7978845608028654 * (1.0 + 3 * 0.044715 * square)
    slope = 0.5 * (1.0 + t) + 0.5 * v * (1.0 - t * t) * inner
    g = (cot[...].astype(F32) * slope).astype(BF)
    grad[...] = g
    sums[...] = jnp.sum(g.astype(F32)[:, ROW : ROW + OWN], axis=1, keepdims=True)


def activated_body(place, mid, near, far, bias, mine, other, act):
    v, _, t = gelu_parts(mid, near, far, bias)
    act[...] = (v * (0.5 * (1.0 + t)))[:, ROW : ROW + OWN].astype(BF)
    mine[...] = act[at(place[C], 32), :]
    other[...] = act[at(1 - place[C], 32), :]


def shifted_grads(place, near, here, far, stack):
    lower = place[Z] == 0
    above, below = jnp.where(lower, near[...], far[...]), jnp.where(lower, far[...], near[...])
    for a, values in enumerate((above, here[...], below)):
        values = values.astype(F32)
        for c in range(3):
            moved = shifted_columns(values, 1 - c).astype(BF)
            for b in range(3):
                k = (9 * a + 3 * b + c) * 64
                start = ROW * (2 - b)
                stack[k : k + 64, :] = moved[:, start : start + OWN]


def split(values, out):
    high = values.astype(BF)
    out[...] = high
    n = values.shape[0] * 27 // 28
    low = (values[n:] - high[n:].astype(F32)).astype(BF)
    lane = lax.broadcasted_iota(jnp.int32, low.shape, 2)
    out[n:] = jnp.where(lane < 64, high[n:], low)


def join(ref):
    values = ref[...].astype(F32)
    n = values.shape[0] * 27 // 28
    last = values[n:]
    return jnp.concatenate([values[:n], last + pltpu.roll(last, 64, 2)])


def kernel_grad_body(place, near, here, far, own, sums, keep, send, stack, volume, sem):
    fetch = pltpu.make_async_copy(own, volume, sem)
    fetch.start()
    shifted_grads(place, near, here, far, stack)
    fetch.wait()
    core = place[C]
    for m in range(0, 27, 4):
        n = min(4, 27 - m)
        got = lax.dot_general(
            stack[64 * m : 64 * (m + n), :],
            volume[...],
            (((1,), (1,)), ((), ())),
            preferred_element_type=F32,
        )
        left, right = got[:, :128], got[:, 128:]
        taps = slice(2 * m, 2 * (m + n))
        keep[taps] = jnp.where(core == 0, left, right).reshape(2 * n, 32, 128)
        send[taps] = jnp.where(core == 0, right, left).reshape(2 * n, 32, 128).astype(BF)
    spread = jnp.broadcast_to(sums[...], (64, 128))
    keep[54:] = spread.reshape(2, 32, 128)
    split_last = spread.astype(BF)
    rest = (spread - split_last.astype(F32)).astype(BF)
    lane = lax.broadcasted_iota(jnp.int32, rest.shape, 1)
    send[54:] = jnp.where(lane < 64, split_last, rest).reshape(2, 32, 128)


def input_grad_body(place, near, here, far, weights, *refs):
    outs, (stack, full) = refs[:4], refs[4:]
    shifted_grads(place, near, here, far, stack)
    for n in range(0, OWN, 256):
        full[:, n : n + 256] = jnp.dot(
            weights[...], stack[:, n : n + 256], preferred_element_type=F32
        ).astype(BF)
    y, c = place[Y], place[C]
    for s, out in zip(STEPS, outs, strict=True):
        for i in range(2):
            block = (c + i) % 2 * 4 + peer(y, s)
            out[32 * i : 32 * i + 32, :] = full[at(block, 32), :]


def fold_y_body(place, one, two, three, four, act_own, act_other, straight_out, crossed_out):
    total = (one[...].astype(F32) + four[...].astype(F32)) + (two[...].astype(F32) + three[...].astype(F32))
    total = total.astype(BF)
    straight_out[:32, :] = act_own[...]
    crossed_out[:32, :] = act_other[...]
    straight_out[32:, :] = total[:32]
    crossed_out[32:, :] = total[32:]


def place_body(place, direct, crossed, activated, input_grad):
    z = place[Z]
    for part, half in ((direct, z), (crossed, 1 - z)):
        activated[:, at(half, OWN)] = part[:32, :]
        input_grad[:, at(half, OWN)] = part[32:, :]


def fold_core_body(place, keep, got, mine, *refs):
    outs, total = refs[:3], refs[3]
    total[...] = keep[...] + join(got)
    x = place[X]
    mine[...] = total[:, at(x, 8), :]
    for s, out in zip(PEERS, outs, strict=True):
        split(total[:, at(peer(x, s), 8), :], out)


def fold_x_body(place, mine, one, two, three, keep, send, total):
    total[...] = (mine[...] + join(one) + join(two) + join(three)).reshape(28, 2, 8, 128)
    split(total[:, pl.ds(place[Z], 1)].reshape(28, 8, 128), keep)
    split(total[:, pl.ds(1 - place[Z], 1)].reshape(28, 8, 128), send)


def fold_zh_body(place, mine, from_z, from_h, from_zh, out):
    split((join(mine) + join(from_z)) + (join(from_h) + join(from_zh)), out)


def fold_h_body(place, mine, got, out):
    split(join(mine) + join(got), out)


def quarters_body(place, *refs):
    parts, out, full = refs[:4], refs[4], refs[5]
    for s, part in zip(STEPS, parts, strict=True):
        full[:, at(peer(place[X], s), 8), :] = part[...].astype(F32)
    out[...] = full[...].astype(BF)


def whole_body(place, mine, other, taps, bias):
    taps[:, :, at(place[C], 128)] = mine[:27].astype(F32)
    taps[:, :, at(1 - place[C], 128)] = other[:27].astype(F32)
    last = mine[27].astype(F32)
    bias[...] = (last + pltpu.roll(last, 64, 1)).T[:1]


def local(volume, kernel, bias, cotangent):
    filt, depth = lax.axis_index("filt"), lax.axis_index("depth")
    z, c = filt // 4, depth % 2
    place = jnp.stack([z, filt % 4, c, depth // 8]).astype(jnp.int32)

    flat = volume.reshape(32, 64 * ROW)
    first, second = flat[:, :GWIN], flat[:, 30 * ROW :]
    direct = exchange(jnp.where(z == 0, first, second), straight)
    crossed = exchange(jnp.where(z == 0, second, first), crossed_in)
    column = jnp.concatenate([direct, crossed])
    shards = [column] + [exchange(column, peer_y(s)) for s in PEERS]

    taps = exchange(lax.dynamic_slice(kernel, (0, 0, 128 * c), (27, 32, 128)), other_z)
    forward_weights, backward_weights = call(
        prepare_body,
        (shape(576, 768), shape(256, 1728)),
        [pltpu.VMEM((27, 64, 256), BF)],
        place,
        kernel,
        taps,
        exchange(taps, other_core),
        room=8,
    )
    partner_bias = exchange(bias, other_z)
    biases = jnp.where(
        z == 0, jnp.concatenate([bias, partner_bias]), jnp.concatenate([partner_bias, bias])
    ).reshape(64, 1)
    padded = jnp.pad(cotangent.reshape(32, 64 * ROW), ((0, 0), (ROW, ROW)))
    first, second = padded[:, :GWIN], padded[:, OWN:]
    cot_own = exchange(jnp.where(z == 0, first, second), straight)
    cot_other = exchange(jnp.where(z == 0, second, first), crossed_in)

    near, mid, far, own = call(
        forward_body,
        (shape(64, GWIN), shape(64, GWIN, dtype=F32), shape(64, GWIN), shape(256, OWN)),
        [pltpu.VMEM((256, VWIN), BF), pltpu.VMEM((256, GWIN), BF), pltpu.SemaphoreType.DMA],
        place,
        *shards,
        forward_weights,
        flops=2 * 192 * 2304 * GWIN,
        room=12,
        hbm_out=(3,),
    )
    near, far = exchange(near, other_z), exchange(far, far_plane)
    grad, sums = call(
        grad_body,
        (shape(64, GWIN), shape(64, 1, dtype=F32)),
        [pltpu.VMEM((64, GWIN), BF)],
        place,
        mid,
        near,
        far,
        biases,
        cot_own,
        cot_other,
        room=12,
    )
    grad_near, grad_far = exchange(grad, other_z), exchange(grad, far_plane)
    act_own, act_other = call(
        activated_body,
        (shape(32, OWN), shape(32, OWN)),
        [pltpu.VMEM((64, OWN), BF)],
        place,
        mid,
        near,
        far,
        biases,
        room=12,
    )

    stack = pltpu.VMEM((27 * 64, OWN), BF)
    keep, send = call(
        kernel_grad_body,
        (shape(56, 32, 128, dtype=F32), shape(56, 32, 128)),
        [stack, pltpu.VMEM((256, OWN), BF), pltpu.SemaphoreType.DMA],
        place,
        grad_near,
        grad,
        grad_far,
        own,
        sums,
        flops=2 * 1728 * 256 * OWN,
        room=20,
        hbm_in=(4,),
    )
    pieces = call(
        input_grad_body,
        tuple(shape(64, OWN) for _ in STEPS),
        [stack, pltpu.VMEM((256, OWN), BF)],
        place,
        grad_near,
        grad,
        grad_far,
        backward_weights,
        flops=2 * 1728 * 256 * OWN,
        room=20,
    )

    parts = [pieces[0]] + [exchange(p, peer_y(s)) for s, p in zip(PEERS, pieces[1:])]
    direct, crossed = call(
        fold_y_body, (shape(64, OWN), shape(64, OWN)), [], place, *parts, act_own, act_other
    )
    activated, input_grad = call(
        place_body,
        (shape(32, 64 * ROW), shape(32, 64 * ROW)),
        [],
        place,
        exchange(direct, straight),
        exchange(crossed, crossed_out),
    )

    mine, *sends = call(
        fold_core_body,
        (shape(56, 8, 128, dtype=F32),) + (shape(56, 8, 128),) * 3,
        [pltpu.VMEM((56, 32, 128), F32)],
        place,
        keep,
        exchange(send, other_core),
    )
    got = [exchange(value, peer_x(s)) for s, value in zip(PEERS, sends)]
    eight = shape(28, 8, 128)
    keep, send = call(
        fold_x_body, (eight, eight), [pltpu.VMEM((28, 2, 8, 128), F32)], place, mine, *got
    )
    got = [exchange(send, other_z), exchange(keep, pair_h), exchange(send, pair_zh)]
    (part,) = call(fold_zh_body, (eight,), [], place, keep, *got)
    (part,) = call(fold_h_body, (eight,), [], place, part, exchange(part, mirror_h))
    got = [exchange(part, peer_x(s)) for s in PEERS]
    (part,) = call(
        quarters_body, (shape(28, 32, 128),), [pltpu.VMEM((28, 32, 128), F32)], place, part, *got
    )
    kernel_grad, bias_grad = call(
        whole_body,
        (shape(27, 32, 256, dtype=F32), shape(1, 32, dtype=F32)),
        [],
        place,
        part,
        exchange(part, other_core),
    )
    return (
        activated.reshape(32, 1, 64 * ROW),
        input_grad.reshape(32, 1, 64 * ROW),
        kernel_grad,
        bias_grad.reshape(32),
    )


def solution(mesh):
    placed = (P("filt", "depth", None), P(None, "filt", None), P("filt"), P("filt", "depth", None))
    return jax.shard_map(
        local,
        mesh=mesh,
        in_specs=placed,
        out_specs=(
            P("filt", "depth", None),
            P("filt", "depth", None),
            P(None, "filt", None),
            P("filt"),
        ),
        check_vma=False,
    )
```

time: 900 us -> 120 us (0.13)
  blocking collectives: 738 us -> 0 us
  waiting for transfers between devices: 86.5 us -> 36.5 us
  starting transfers between devices: 7.46 us -> 54.9 us
  Pallas kernels: 0 us -> 22.4 us
  local copies, waits for them, and re-layouts: 23 us -> 1.27 us
  between operations: 15.1 us -> 0.91 us
  matrix products: 14 us -> 0 us
  other arithmetic: 14.9 us -> 2.13 us
    unnamed x1 -> x0, blocking collectives: 663 us -> none
    all_gather x1 -> x0, waiting for transfers between devices: 81.1 us -> none  [local(): widened = lax.all_gather(rimmed, 'filt', axis=0, tiled=True)]
    psum x1 -> x0, blocking collectives: 75.8 us -> none  [local(): lax.psum((local_kernel_grad, local_bias_grad), 'depth')]
    ppermute x4 -> x31, starting transfers between devices: 7.38 us -> 54.9 us  [exchange(): return lax.ppermute(value, ('depth', 'filt'), pairs(move))]
    ppermute x4 -> x31, waiting for transfers between devices: 5.39 us -> 36.5 us  [exchange(): return lax.ppermute(value, ('depth', 'filt'), pairs(move))]
    pallas_call x0 -> x14, Pallas kernels: none -> 22.4 us  [call(): pl.pallas_call(body, out_shape=outs, in_specs=[SMEM] + [HBM if i in hbm_i...]
    dot_general x7 -> x0, matrix products: 14 us -> none  [the longest x1 7.51 us: data_grad(): jnp.einsum('koc,kodp->cdp', columns, stacked, preferred_element_type=jnp....]
    dot_general x1 -> x0, local copies, waits for them, and re-layouts: 10.2 us -> none  [data_grad(): jnp.einsum('koc,kodp->cdp', columns, stacked, preferred_element_type=jnp....]
  transfers between devices with their start and end apart: 6 -> 31, of which waited for: 2 -> 17; matrix products, arithmetic and copies ran while one was open for 4% -> 1% of each run, Pallas kernels for 0% -> 12%
where the time goes in v1:
time: 120 us; the launch traced here: 118 us
  starting transfers between devices  54.9 us (46%)
  waiting for transfers between devices  36.5 us (30%)
  Pallas kernels  22.4 us (19%)
  other arithmetic  2.13 us (2%)
  local copies, waits for them, and re-layouts  1.27 us (1%)
    ppermute x31, starting transfers between devices, exchange(): return lax.ppermute(value, ('depth', 'filt'), pairs(move))  54.9 us
    ppermute x31, waiting for transfers between devices, exchange(): return lax.ppermute(value, ('depth', 'filt'), pairs(move))  36.5 us
    pallas_call x14, Pallas kernels, call(): pl.pallas_call(body, out_shape=outs, in_specs=[SMEM] + [HBM if i in hbm_i...  22.4 us
  transfers between devices with their start and end apart: 31, of which 17 were waited for; matrix products, arithmetic and copies ran while one was open for 1% of the time, Pallas kernels for 12%

profile of v1, /device:TPU:32, one launch (start us, length us, event | category | flops | bytes accessed | tf_op | source)
XLA Modules:
  0.0 118.1 jit_solution(17056338488886529522)
XLA Ops:
  0.7 1.1 broadcast_select_fusion.2
  1.7 1.9 %collective-permute-start = (bf16[32,2176]{1,0:T(8,128)(2,1)S(1)}, bf16[32,2176]{1,0:T(8,128)(2,1)S(1)}, u32[]{:S(2)}, u32[]{:S(2)}) collective-permute-start(bf16[32,2176]{1,0:T(8,128)(2,1)S(1)} %get-tuple-element.63), channel_id=1, source_target_pairs={{0,0},{1,1},{2,2},{3,3},{4,8},{5,9},{6,10},{7,11},{8,4},{9,5},{10,... | collective-permute-start | bytes 417800 | tf_op jit(solution)/shard_map/ppermute | solution.py:83
  4.4 1.7 %collective-permute-start.5 = (bf16[27,32,128]{2,1,0:T(8,128)(2,1)S(1)}, bf16[27,32,128]{2,1,0:T(8,128)(2,1)S(1)}, u32[]{:S(2)}, u32[]{:S(2)}) collective-permute-start(bf16[27,32,128]{2,1,0:T(8,128)(2,1)S(1)} %constant_dynamic-slice_fusion), channel_id=1, source_target_pairs={{0,4},{1,5},{2,6},{3,7},{4,0},{5,1},{6,2},{7,3},{8,12},{9,13},{10,... | collective-permute-start | bytes 663560 | tf_op jit(solution)/shard_map/ppermute | solution.py:83
  6.5 1.6 %collective-permute-done = bf16[32,2176]{1,0:T(8,128)(2,1)S(1)} collective-permute-done((bf16[32,2176]{1,0:T(8,128)(2,1)S(1)}, bf16[32,2176]{1,0:T(8,128)(2,1)S(1)}, u32[]{:S(2)}, u32[]{:S(2)}) %collective-permute-start) | collective-permute-done | bytes 139296 | tf_op jit(solution)/shard_map/ppermute | solution.py:83
  8.2 1.0 collective-permute-done.1
  9.2 1.7 %collective-permute-start.2 = (bf16[64,2176]{1,0:T(8,128)(2,1)S(1)}, bf16[64,2176]{1,0:T(8,128)(2,1)S(1)}, u32[]{:S(2)}, u32[]{:S(2)}) collective-permute-start(bf16[64,2176]{1,0:T(8,128)(2,1)S(1)} %constant_dynamic-update-slice_fusion.refs_0_), channel_id=1, source_target_pairs={{0,1},{1,0},{2,3},{3,2},{4,5},{5,4},{6,7},{7,6},{8,9},{9,8},{10,11... | collective-permute-start | bytes 835592 | tf_op jit(solution)/shard_map/ppermute | solution.py:83
  10.9 2.2 %collective-permute-start.3 = (bf16[64,2176]{1,0:T(8,128)(2,1)S(1)}, bf16[64,2176]{1,0:T(8,128)(2,1)S(1)}, u32[]{:S(2)}, u32[]{:S(2)}) collective-permute-start(bf16[64,2176]{1,0:T(8,128)(2,1)S(1)} %constant_dynamic-update-slice_fusion.refs_0_), channel_id=1, source_target_pairs={{0,3},{1,2},{2,1},{3,0},{4,7},{5,6},{6,5},{7,4},{8,11},{9,10},{10,... | collective-permute-start | bytes 835592 | tf_op jit(solution)/shard_map/ppermute | solution.py:83
  13.8 2.0 %collective-permute-start.6 = (bf16[27,32,128]{2,1,0:T(8,128)(2,1)S(1)}, bf16[27,32,128]{2,1,0:T(8,128)(2,1)S(1)}, u32[]{:S(2)}, u32[]{:S(2)}) collective-permute-start(bf16[27,32,128]{2,1,0:T(8,128)(2,1)S(1)} %collective-permute-done.5.partner), channel_id=1, source_target_pairs={{0,8},{1,9},{2,10},{3,11},{4,12},{5,13},{6,14},{7,15},{8,0},{9,1},... | collective-permute-start | bytes 663560 | tf_op jit(solution)/shard_map/ppermute | solution.py:83
  15.8 0.9 broadcast_select_fusion
  16.9 2.5 %collective-permute-start.10 = (bf16[32,2176]{1,0:T(8,128)(2,1)}, bf16[32,2176]{1,0:T(8,128)(2,1)S(1)}, u32[]{:S(2)}, u32[]{:S(2)}) collective-permute-start(bf16[32,2176]{1,0:T(8,128)(2,1)} %get-tuple-element.61), channel_id=1, source_target_pairs={{0,0},{1,1},{2,2},{3,3},{4,8},{5,9},{6,10},{7,11},{8,4},{9,5},{10,... | collective-permute-start | bytes 417800 | tf_op jit(solution)/shard_map/ppermute | solution.py:83
  19.4 0.9 shard_map.75
  20.4 1.0 collective-permute-start.11
  21.3 3.3 %collective-permute-done.3.refs_2_ = bf16[64,2176]{1,0:T(8,128)(2,1)S(1)} collective-permute-done((bf16[64,2176]{1,0:T(8,128)(2,1)S(1)}, bf16[64,2176]{1,0:T(8,128)(2,1)S(1)}, u32[]{:S(2)}, u32[]{:S(2)}) %collective-permute-start.3) | collective-permute-done | bytes 278560 | tf_op jit(solution)/shard_map/ppermute | solution.py:83
  24.6 1.1 collective-permute-done.4.refs_3_
  25.8 4.7 %shard_map.76 = (bf16[64,2176]{1,0:T(8,128)(2,1)}, f32[64,2176]{1,0:T(8,128)S(1)}, bf16[64,2176]{1,0:T(8,128)(2,1)}, bf16[256,2048]{1,0:T(8,128)(2,1)S(1)}) custom-call(s32[4]{0:T(128)S(1)} %pad_add_fusion.place, bf16[64,2176]{1,0:T(8,128)(2,1)S(1)} %constant_dynamic-update-slice_fusion.refs_0_, bf16[64,2176]{1,0:T(8,128)(2,1)S(1)} %collective-permute-done.2.refs_1_, ...), custom_call_target="tpu_custom_call" | custom-call | flops 1925185536 | bytes 2000000 | tf_op jit(solution)/shard_map/pallas_call | solution.py:91
  30.5 1.0 copy-done.1
  31.5 2.6 %collective-permute-start.7 = (bf16[64,2176]{1,0:T(8,128)(2,1)}, bf16[64,2176]{1,0:T(8,128)(2,1)S(1)}, u32[]{:S(2)}, u32[]{:S(2)}) collective-permute-start(bf16[64,2176]{1,0:T(8,128)(2,1)} %get-tuple-element.34), channel_id=1, source_target_pairs={{0,4},{1,5},{2,6},{3,7},{4,0},{5,1},{6,2},{7,3},{8,12},{9,13},{10,... | collective-permute-start | bytes 835592 | tf_op jit(solution)/shard_map/ppermute | solution.py:83
  34.1 3.7 %collective-permute-start.8 = (bf16[64,2176]{1,0:T(8,128)(2,1)}, bf16[64,2176]{1,0:T(8,128)(2,1)S(1)}, u32[]{:S(2)}, u32[]{:S(2)}) collective-permute-start(bf16[64,2176]{1,0:T(8,128)(2,1)} %get-tuple-element.35), channel_id=1, source_target_pairs={{4,16},{5,17},{6,18},{7,19},{12,24},{13,25},{14,26},{15,27},{16,4}... | collective-permute-start | bytes 835592 | tf_op jit(solution)/shard_map/ppermute | solution.py:83
  38.2 3.6 %collective-permute-done.7.near = bf16[64,2176]{1,0:T(8,128)(2,1)S(1)} collective-permute-done((bf16[64,2176]{1,0:T(8,128)(2,1)}, bf16[64,2176]{1,0:T(8,128)(2,1)S(1)}, u32[]{:S(2)}, u32[]{:S(2)}) %collective-permute-start.7) | collective-permute-done | bytes 278560 | tf_op jit(solution)/shard_map/ppermute | solution.py:83
  41.8 3.8 %collective-permute-done.8.far = bf16[64,2176]{1,0:T(8,128)(2,1)S(1)} collective-permute-done((bf16[64,2176]{1,0:T(8,128)(2,1)}, bf16[64,2176]{1,0:T(8,128)(2,1)S(1)}, u32[]{:S(2)}, u32[]{:S(2)}) %collective-permute-start.8) | collective-permute-done | bytes 278560 | tf_op jit(solution)/shard_map/ppermute | solution.py:83
  45.6 1.2 %shard_map.77 = (bf16[64,2176]{1,0:T(8,128)(2,1)S(1)}, f32[64,1]{1,0:T(8,128)S(1)}) custom-call(s32[4]{0:T(128)S(1)} %pad_add_fusion.place, f32[64,2176]{1,0:T(8,128)S(1)} %get-tuple-element.33.mid, bf16[64,2176]{1,0:T(8,128)(2,1)S(1)} %collective-permute-done.7.near, bf16[64,2176]{1,0:T(8,128)(2,1)S(1)} %collective-permute-done.8.far, ...), custom_call_target="tpu_custom_call" | custom-call | bytes 2000000 | tf_op jit(solution)/shard_map/pallas_call | solution.py:91
  46.9 7.3 %collective-permute-start.13 = (bf16[64,2176]{1,0:T(8,128)(2,1)S(1)}, bf16[64,2176]{1,0:T(8,128)(2,1)S(1)}, u32[]{:S(2)}, u32[]{:S(2)}) collective-permute-start(bf16[64,2176]{1,0:T(8,128)(2,1)S(1)} %get-tuple-element.36.here), channel_id=1, source_target_pairs={{4,16},{5,17},{6,18},{7,19},{12,24},{13,25},{14,26},{15,27},{16,4}... | collective-permute-start | bytes 835592 | tf_op jit(solution)/shard_map/ppermute | solution.py:83
  54.2 1.2 collective-permute-done.12.near
  55.4 4.4 %collective-permute-done.13.far = bf16[64,2176]{1,0:T(8,128)(2,1)S(1)} collective-permute-done((bf16[64,2176]{1,0:T(8,128)(2,1)S(1)}, bf16[64,2176]{1,0:T(8,128)(2,1)S(1)}, u32[]{:S(2)}, u32[]{:S(2)}) %collective-permute-start.13) | collective-permute-done | bytes 278560 | tf_op jit(solution)/shard_map/ppermute | solution.py:83
  59.8 4.4 %shard_map.82 = (f32[56,32,128]{2,1,0:T(8,128)S(1)}, bf16[56,32,128]{2,1,0:T(8,128)(2,1)S(1)}) custom-call(s32[4]{0:T(128)S(1)} %pad_add_fusion.place, bf16[64,2176]{1,0:T(8,128)(2,1)S(1)} %collective-permute-done.12.near, bf16[64,2176]{1,0:T(8,128)(2,1)S(1)} %get-tuple-element.36.here, bf16[64,2176]{1,0:T(8,128)(2,1)S(1)} %collective-permute-done.13.far, ...), custom_call_target="tpu_custom_call" | custom-call | flops 1811939328 | bytes 2000000 | tf_op jit(solution)/shard_map/pallas_call | solution.py:91
  64.3 1.8 %collective-permute-done.19.got = bf16[56,32,128]{2,1,0:T(8,128)(2,1)S(1)} collective-permute-done((bf16[56,32,128]{2,1,0:T(8,128)(2,1)S(1)}, bf16[56,32,128]{2,1,0:T(8,128)(2,1)S(1)}, u32[]{:S(2)}, u32[]{:S(2)}) %collective-permute-start.19) | collective-permute-done | bytes 458784 | tf_op jit(solution)/shard_map/ppermute | solution.py:83
  66.1 0.8 shard_map.83
  66.9 1.8 %collective-permute-start.20 = (bf16[56,8,128]{2,1,0:T(8,128)(2,1)S(1)}, bf16[56,8,128]{2,1,0:T(8,128)(2,1)S(1)}, u32[]{:S(2)}, u32[]{:S(2)}) collective-permute-start(bf16[56,8,128]{2,1,0:T(8,128)(2,1)S(1)} %get-tuple-element.53), channel_id=1, source_target_pairs={{0,64},{1,65},{2,66},{3,67},{4,68},{5,69},{6,70},{7,71},{8,72},{9,... | collective-permute-start | bytes 344072 | tf_op jit(solution)/shard_map/ppermute | solution.py:83
  68.7 2.1 %collective-permute-start.21 = (bf16[56,8,128]{2,1,0:T(8,128)(2,1)S(1)}, bf16[56,8,128]{2,1,0:T(8,128)(2,1)S(1)}, u32[]{:S(2)}, u32[]{:S(2)}) collective-permute-start(bf16[56,8,128]{2,1,0:T(8,128)(2,1)S(1)} %get-tuple-element.54), channel_id=1, source_target_pairs={{0,192},{1,193},{2,194},{3,195},{4,196},{5,197},{6,198},{7,199},{8... | collective-permute-start | bytes 344072 | tf_op jit(solution)/shard_map/ppermute | solution.py:83
  70.8 0.9 collective-permute-start.22
  71.8 3.3 %shard_map.78 = (bf16[64,2048]{1,0:T(8,128)(2,1)S(1)}, bf16[64,2048]{1,0:T(8,128)(2,1)S(1)}, bf16[64,2048]{1,0:T(8,128)(2,1)S(1)}, bf16[64,2048]{1,0:T(8,128)(2,1)S(1)}) custom-call(s32[4]{0:T(128)S(1)} %pad_add_fusion.place, bf16[64,2176]{1,0:T(8,128)(2,1)S(1)} %collective-permute-done.12.near, bf16[64,2176]{1,0:T(8,128)(2,1)S(1)} %get-tuple-element.36.here, ...), custom_call_target="tpu_custom_call" | custom-call | flops 1811939328 | bytes 2000000 | tf_op jit(solution)/shard_map/pallas_call | solution.py:91
  75.1 2.3 %collective-permute-start.15 = (bf16[64,2048]{1,0:T(8,128)(2,1)S(1)}, bf16[64,2048]{1,0:T(8,128)(2,1)S(1)}, u32[]{:S(2)}, u32[]{:S(2)}) collective-permute-start(bf16[64,2048]{1,0:T(8,128)(2,1)S(1)} %get-tuple-element.40), channel_id=1, source_target_pairs={{0,3},{1,2},{2,1},{3,0},{4,7},{5,6},{6,5},{7,4},{8,11},{9,10},{10,... | collective-permute-start | bytes 786440 | tf_op jit(solution)/shard_map/ppermute | solution.py:83
  77.4 1.8 %collective-permute-start.16 = (bf16[64,2048]{1,0:T(8,128)(2,1)S(1)}, bf16[64,2048]{1,0:T(8,128)(2,1)S(1)}, u32[]{:S(2)}, u32[]{:S(2)}) collective-permute-start(bf16[64,2048]{1,0:T(8,128)(2,1)S(1)} %get-tuple-element.41), channel_id=1, source_target_pairs={{0,2},{1,3},{2,0},{3,1},{4,6},{5,7},{6,4},{7,5},{8,10},{9,11},{10,... | collective-permute-start | bytes 786440 | tf_op jit(solution)/shard_map/ppermute | solution.py:83
  79.9 2.5 %collective-permute-start.23 = (bf16[28,8,128]{2,1,0:T(8,128)(2,1)S(1)}, bf16[28,8,128]{2,1,0:T(8,128)(2,1)S(1)}, u32[]{:S(2)}, u32[]{:S(2)}) collective-permute-start(bf16[28,8,128]{2,1,0:T(8,128)(2,1)S(1)} %get-tuple-element.57), channel_id=1, source_target_pairs={{0,4},{1,5},{2,6},{3,7},{4,0},{5,1},{6,2},{7,3},{8,12},{9,13},{10,... | collective-permute-start | bytes 172040 | tf_op jit(solution)/shard_map/ppermute | solution.py:83
  82.6 1.9 %collective-permute-done.23.from_z = bf16[28,8,128]{2,1,0:T(8,128)(2,1)S(1)} collective-permute-done((bf16[28,8,128]{2,1,0:T(8,128)(2,1)S(1)}, bf16[28,8,128]{2,1,0:T(8,128)(2,1)S(1)}, u32[]{:S(2)}, u32[]{:S(2)}) %collective-permute-start.23) | collective-permute-done | bytes 57376 | tf_op jit(solution)/shard_map/ppermute | solution.py:83
  84.5 1.2 %collective-permute-start.25 = (bf16[28,8,128]{2,1,0:T(8,128)(2,1)S(1)}, bf16[28,8,128]{2,1,0:T(8,128)(2,1)S(1)}, u32[]{:S(2)}, u32[]{:S(2)}) collective-permute-start(bf16[28,8,128]{2,1,0:T(8,128)(2,1)S(1)} %get-tuple-element.57), channel_id=1, source_target_pairs={{0,20},{1,21},{2,22},{3,23},{4,16},{5,17},{6,18},{7,19},{8,28},{9,... | collective-permute-start | bytes 172040 | tf_op jit(solution)/shard_map/ppermute | solution.py:83
  85.8 1.8 %collective-permute-done.24.from_h = bf16[28,8,128]{2,1,0:T(8,128)(2,1)S(1)} collective-permute-done((bf16[28,8,128]{2,1,0:T(8,128)(2,1)S(1)}, bf16[28,8,128]{2,1,0:T(8,128)(2,1)S(1)}, u32[]{:S(2)}, u32[]{:S(2)}) %collective-permute-start.24) | collective-permute-done | bytes 57376 | tf_op jit(solution)/shard_map/ppermute | solution.py:83
  87.5 1.2 collective-permute-done.25.from_zh
  89.3 6.7 %collective-permute-start.26 = (bf16[28,8,128]{2,1,0:T(8,128)(2,1)S(1)}, bf16[28,8,128]{2,1,0:T(8,128)(2,1)S(1)}, u32[]{:S(2)}, u32[]{:S(2)}) collective-permute-start(bf16[28,8,128]{2,1,0:T(8,128)(2,1)S(1)} %shard_map.85.mine), channel_id=1, source_target_pairs={{0,48},{1,49},{2,50},{3,51},{4,52},{5,53},{6,54},{7,55},{8,56},{9,... | collective-permute-start | bytes 172040 | tf_op jit(solution)/shard_map/ppermute | solution.py:83
  96.0 2.2 %collective-permute-done.26.got = bf16[28,8,128]{2,1,0:T(8,128)(2,1)S(1)} collective-permute-done((bf16[28,8,128]{2,1,0:T(8,128)(2,1)S(1)}, bf16[28,8,128]{2,1,0:T(8,128)(2,1)S(1)}, u32[]{:S(2)}, u32[]{:S(2)}) %collective-permute-start.26) | collective-permute-done | bytes 57376 | tf_op jit(solution)/shard_map/ppermute | solution.py:83
  98.8 1.5 %collective-permute-start.27 = (bf16[28,8,128]{2,1,0:T(8,128)(2,1)S(1)}, bf16[28,8,128]{2,1,0:T(8,128)(2,1)S(1)}, u32[]{:S(2)}, u32[]{:S(2)}) collective-permute-start(bf16[28,8,128]{2,1,0:T(8,128)(2,1)S(1)} %shard_map.86.refs_0_), channel_id=1, source_target_pairs={{0,64},{1,65},{2,66},{3,67},{4,68},{5,69},{6,70},{7,71},{8,72},{9,... | collective-permute-start | bytes 172040 | tf_op jit(solution)/shard_map/ppermute | solution.py:83
  100.4 2.1 %collective-permute-start.28 = (bf16[28,8,128]{2,1,0:T(8,128)(2,1)S(1)}, bf16[28,8,128]{2,1,0:T(8,128)(2,1)S(1)}, u32[]{:S(2)}, u32[]{:S(2)}) collective-permute-start(bf16[28,8,128]{2,1,0:T(8,128)(2,1)S(1)} %shard_map.86.refs_0_), channel_id=1, source_target_pairs={{0,192},{1,193},{2,194},{3,195},{4,196},{5,197},{6,198},{7,199},{8... | collective-permute-start | bytes 172040 | tf_op jit(solution)/shard_map/ppermute | solution.py:83
  103.0 1.0 shard_map.79
  104.6 1.9 %collective-permute-start.17 = (bf16[64,2048]{1,0:T(8,128)(2,1)S(1)}, bf16[64,2048]{1,0:T(8,128)(2,1)S(1)}, u32[]{:S(2)}, u32[]{:S(2)}) collective-permute-start(bf16[64,2048]{1,0:T(8,128)(2,1)S(1)} %get-tuple-element.44), channel_id=1, source_target_pairs={{0,0},{1,1},{2,2},{3,3},{4,8},{5,9},{6,10},{7,11},{8,4},{9,5},{10,... | collective-permute-start | bytes 786440 | tf_op jit(solution)/shard_map/ppermute | solution.py:83
  106.7 1.5 %collective-permute-done.29.refs_3_ = bf16[28,8,128]{2,1,0:T(8,128)(2,1)S(1)} collective-permute-done((bf16[28,8,128]{2,1,0:T(8,128)(2,1)S(1)}, bf16[28,8,128]{2,1,0:T(8,128)(2,1)S(1)}, u32[]{:S(2)}, u32[]{:S(2)}) %collective-permute-start.29) | collective-permute-done | bytes 57376 | tf_op jit(solution)/shard_map/ppermute | solution.py:83
  109.2 5.2 %collective-permute-done.17.direct = bf16[64,2048]{1,0:T(8,128)(2,1)S(1)} collective-permute-done((bf16[64,2048]{1,0:T(8,128)(2,1)S(1)}, bf16[64,2048]{1,0:T(8,128)(2,1)S(1)}, u32[]{:S(2)}, u32[]{:S(2)}) %collective-permute-start.17) | collective-permute-done | bytes 262176 | tf_op jit(solution)/shard_map/ppermute | solution.py:83
  115.1 1.4 %shard_map.81 = (bf16[32,4096]{1,0:T(8,128)(2,1)}, bf16[32,4096]{1,0:T(8,128)(2,1)}) custom-call(s32[4]{0:T(128)S(1)} %pad_add_fusion.place, bf16[64,2048]{1,0:T(8,128)(2,1)S(1)} %collective-permute-done.17.direct, bf16[64,2048]{1,0:T(8,128)(2,1)S(1)} %collective-permute-done.18.crossed), custom_call_target="tpu_custom_call" | custom-call | bytes 2000000 | tf_op jit(solution)/shard_map/pallas_call | solution.py:91
  116.5 1.6 %shard_map.88 = (f32[27,32,256]{2,1,0:T(8,128)}, f32[1,32]{1,0:T(1,128)}) custom-call(s32[4]{0:T(128)S(1)} %pad_add_fusion.place, bf16[28,32,128]{2,1,0:T(8,128)(2,1)S(1)} %shard_map.87.mine, bf16[28,32,128]{2,1,0:T(8,128)(2,1)S(1)} %collective-permute-done.30.other), custom_call_target="tpu_custom_call" | custom-call | bytes 2000000 | tf_op jit(solution)/shard_map/pallas_call | solution.py:91
  (48 shorter events, 7.8 us)
Async XLA Ops:
  0.6 3.7 %copy-start = (bf16[27,32,256]{2,1,0:T(8,128)(2,1)S(1)}, bf16[27,32,256]{2,1,0:T(8,128)(2,1)}, u32[]{:S(2)}) copy-start(bf16[27,32,256]{2,1,0:T(8,128)(2,1)} %mine.1) | copy-start | bytes 1327108
  1.7 6.5 %collective-permute-start = (bf16[32,2176]{1,0:T(8,128)(2,1)S(1)}, bf16[32,2176]{1,0:T(8,128)(2,1)S(1)}, u32[]{:S(2)}, u32[]{:S(2)}) collective-permute-start(bf16[32,2176]{1,0:T(8,128)(2,1)S(1)} %get-tuple-element.63), channel_id=1, source_target_pairs={{0,0},{1,1},{2,2},{3,3},{4,8},{5,9},{6,10},{7,11},{8,4},{9,5},{10,... | collective-permute-start | bytes 417800 | tf_op jit(solution)/shard_map/ppermute | solution.py:83
  3.6 5.5 %collective-permute-start.1 = (bf16[32,2176]{1,0:T(8,128)(2,1)S(1)}, bf16[32,2176]{1,0:T(8,128)(2,1)S(1)}, u32[]{:S(2)}, u32[]{:S(2)}) collective-permute-start(bf16[32,2176]{1,0:T(8,128)(2,1)S(1)} %get-tuple-element.62), channel_id=1, source_target_pairs={{0,8},{1,9},{2,10},{3,11},{4,0},{5,1},{6,2},{7,3},{8,12},{9,13},{1... | collective-permute-start | bytes 417800 | tf_op jit(solution)/shard_map/ppermute | solution.py:83
  4.3 1.7 %copy-start.4 = (f32[32]{0:T(128)S(1)}, f32[32]{0:T(128)}, u32[]{:S(2)}) copy-start(f32[32]{0:T(128)} %param.6) | copy-start | bytes 388
  4.3 11.4 %copy-start.3 = (bf16[32,1,4096]{2,0,1:T(8,128)(2,1)S(1)}, bf16[32,1,4096]{2,0,1:T(8,128)(2,1)}, u32[]{:S(2)}) copy-start(bf16[32,1,4096]{2,0,1:T(8,128)(2,1)} %param.7) | copy-start | bytes 786436
  4.4 9.4 %collective-permute-start.5 = (bf16[27,32,128]{2,1,0:T(8,128)(2,1)S(1)}, bf16[27,32,128]{2,1,0:T(8,128)(2,1)S(1)}, u32[]{:S(2)}, u32[]{:S(2)}) collective-permute-start(bf16[27,32,128]{2,1,0:T(8,128)(2,1)S(1)} %constant_dynamic-slice_fusion), channel_id=1, source_target_pairs={{0,4},{1,5},{2,6},{3,7},{4,0},{5,1},{6,2},{7,3},{8,12},{9,13},{10,... | collective-permute-start | bytes 663560 | tf_op jit(solution)/shard_map/ppermute | solution.py:83
  6.0 31.8 %collective-permute-start.9 = (f32[32]{0:T(128)S(1)}, f32[32]{0:T(128)S(1)}, u32[]{:S(2)}, u32[]{:S(2)}) collective-permute-start(f32[32]{0:T(128)S(1)} %copy-done.4), channel_id=1, source_target_pairs={{0,4},{1,5},{2,6},{3,7},{4,0},{5,1},{6,2},{7,3},{8,12},{9,13},{10,... | collective-permute-start | bytes 392 | tf_op jit(solution)/shard_map/ppermute | solution.py:83
  9.2 11.1 %collective-permute-start.2 = (bf16[64,2176]{1,0:T(8,128)(2,1)S(1)}, bf16[64,2176]{1,0:T(8,128)(2,1)S(1)}, u32[]{:S(2)}, u32[]{:S(2)}) collective-permute-start(bf16[64,2176]{1,0:T(8,128)(2,1)S(1)} %constant_dynamic-update-slice_fusion.refs_0_), channel_id=1, source_target_pairs={{0,1},{1,0},{2,3},{3,2},{4,5},{5,4},{6,7},{7,6},{8,9},{9,8},{10,11... | collective-permute-start | bytes 835592 | tf_op jit(solution)/shard_map/ppermute | solution.py:83
  10.9 13.8 %collective-permute-start.3 = (bf16[64,2176]{1,0:T(8,128)(2,1)S(1)}, bf16[64,2176]{1,0:T(8,128)(2,1)S(1)}, u32[]{:S(2)}, u32[]{:S(2)}) collective-permute-start(bf16[64,2176]{1,0:T(8,128)(2,1)S(1)} %constant_dynamic-update-slice_fusion.refs_0_), channel_id=1, source_target_pairs={{0,3},{1,2},{2,1},{3,0},{4,7},{5,6},{6,5},{7,4},{8,11},{9,10},{10,... | collective-permute-start | bytes 835592 | tf_op jit(solution)/shard_map/ppermute | solution.py:83
  13.1 12.7 %collective-permute-start.4 = (bf16[64,2176]{1,0:T(8,128)(2,1)S(1)}, bf16[64,2176]{1,0:T(8,128)(2,1)S(1)}, u32[]{:S(2)}, u32[]{:S(2)}) collective-permute-start(bf16[64,2176]{1,0:T(8,128)(2,1)S(1)} %constant_dynamic-update-slice_fusion.refs_0_), channel_id=1, source_target_pairs={{0,2},{1,3},{2,0},{3,1},{4,6},{5,7},{6,4},{7,5},{8,10},{9,11},{10,... | collective-permute-start | bytes 835592 | tf_op jit(solution)/shard_map/ppermute | solution.py:83
  13.8 3.1 %collective-permute-start.6 = (bf16[27,32,128]{2,1,0:T(8,128)(2,1)S(1)}, bf16[27,32,128]{2,1,0:T(8,128)(2,1)S(1)}, u32[]{:S(2)}, u32[]{:S(2)}) collective-permute-start(bf16[27,32,128]{2,1,0:T(8,128)(2,1)S(1)} %collective-permute-done.5.partner), channel_id=1, source_target_pairs={{0,8},{1,9},{2,10},{3,11},{4,12},{5,13},{6,14},{7,15},{8,0},{9,1},... | collective-permute-start | bytes 663560 | tf_op jit(solution)/shard_map/ppermute | solution.py:83
  16.9 21.3 %collective-permute-start.10 = (bf16[32,2176]{1,0:T(8,128)(2,1)}, bf16[32,2176]{1,0:T(8,128)(2,1)S(1)}, u32[]{:S(2)}, u32[]{:S(2)}) collective-permute-start(bf16[32,2176]{1,0:T(8,128)(2,1)} %get-tuple-element.61), channel_id=1, source_target_pairs={{0,0},{1,1},{2,2},{3,3},{4,8},{5,9},{6,10},{7,11},{8,4},{9,5},{10,... | collective-permute-start | bytes 417800 | tf_op jit(solution)/shard_map/ppermute | solution.py:83
  20.4 17.8 %collective-permute-start.11 = (bf16[32,2176]{1,0:T(8,128)(2,1)}, bf16[32,2176]{1,0:T(8,128)(2,1)S(1)}, u32[]{:S(2)}, u32[]{:S(2)}) collective-permute-start(bf16[32,2176]{1,0:T(8,128)(2,1)} %get-tuple-element.60), channel_id=1, source_target_pairs={{0,8},{1,9},{2,10},{3,11},{4,0},{5,1},{6,2},{7,3},{8,12},{9,13},{1... | collective-permute-start | bytes 417800 | tf_op jit(solution)/shard_map/ppermute | solution.py:83
  30.5 1.0 copy-start.1
  31.5 10.3 %collective-permute-start.7 = (bf16[64,2176]{1,0:T(8,128)(2,1)}, bf16[64,2176]{1,0:T(8,128)(2,1)S(1)}, u32[]{:S(2)}, u32[]{:S(2)}) collective-permute-start(bf16[64,2176]{1,0:T(8,128)(2,1)} %get-tuple-element.34), channel_id=1, source_target_pairs={{0,4},{1,5},{2,6},{3,7},{4,0},{5,1},{6,2},{7,3},{8,12},{9,13},{10,... | collective-permute-start | bytes 835592 | tf_op jit(solution)/shard_map/ppermute | solution.py:83
  34.1 11.5 %collective-permute-start.8 = (bf16[64,2176]{1,0:T(8,128)(2,1)}, bf16[64,2176]{1,0:T(8,128)(2,1)S(1)}, u32[]{:S(2)}, u32[]{:S(2)}) collective-permute-start(bf16[64,2176]{1,0:T(8,128)(2,1)} %get-tuple-element.35), channel_id=1, source_target_pairs={{4,16},{5,17},{6,18},{7,19},{12,24},{13,25},{14,26},{15,27},{16,4}... | collective-permute-start | bytes 835592 | tf_op jit(solution)/shard_map/ppermute | solution.py:83
  38.1 21.7 %copy-start.2 = (bf16[256,2048]{1,0:T(8,128)(2,1)S(1)}, bf16[256,2048]{1,0:T(8,128)(2,1)}, u32[]{:S(2)}) copy-start(bf16[256,2048]{1,0:T(8,128)(2,1)} %copy-done.1) | copy-start | bytes 3145732
  46.8 8.5 %collective-permute-start.12 = (bf16[64,2176]{1,0:T(8,128)(2,1)S(1)}, bf16[64,2176]{1,0:T(8,128)(2,1)S(1)}, u32[]{:S(2)}, u32[]{:S(2)}) collective-permute-start(bf16[64,2176]{1,0:T(8,128)(2,1)S(1)} %get-tuple-element.36.here), channel_id=1, source_target_pairs={{0,4},{1,5},{2,6},{3,7},{4,0},{5,1},{6,2},{7,3},{8,12},{9,13},{10,... | collective-permute-start | bytes 835592 | tf_op jit(solution)/shard_map/ppermute | solution.py:83
  46.9 13.0 %collective-permute-start.13 = (bf16[64,2176]{1,0:T(8,128)(2,1)S(1)}, bf16[64,2176]{1,0:T(8,128)(2,1)S(1)}, u32[]{:S(2)}, u32[]{:S(2)}) collective-permute-start(bf16[64,2176]{1,0:T(8,128)(2,1)S(1)} %get-tuple-element.36.here), channel_id=1, source_target_pairs={{4,16},{5,17},{6,18},{7,19},{12,24},{13,25},{14,26},{15,27},{16,4}... | collective-permute-start | bytes 835592 | tf_op jit(solution)/shard_map/ppermute | solution.py:83
  64.2 1.9 %collective-permute-start.19 = (bf16[56,32,128]{2,1,0:T(8,128)(2,1)S(1)}, bf16[56,32,128]{2,1,0:T(8,128)(2,1)S(1)}, u32[]{:S(2)}, u32[]{:S(2)}) collective-permute-start(bf16[56,32,128]{2,1,0:T(8,128)(2,1)S(1)} %get-tuple-element.51), channel_id=1, source_target_pairs={{0,8},{1,9},{2,10},{3,11},{4,12},{5,13},{6,14},{7,15},{8,0},{9,1},... | collective-permute-start | bytes 1376264 | tf_op jit(solution)/shard_map/ppermute | solution.py:83
  66.9 10.5 %collective-permute-start.20 = (bf16[56,8,128]{2,1,0:T(8,128)(2,1)S(1)}, bf16[56,8,128]{2,1,0:T(8,128)(2,1)S(1)}, u32[]{:S(2)}, u32[]{:S(2)}) collective-permute-start(bf16[56,8,128]{2,1,0:T(8,128)(2,1)S(1)} %get-tuple-element.53), channel_id=1, source_target_pairs={{0,64},{1,65},{2,66},{3,67},{4,68},{5,69},{6,70},{7,71},{8,72},{9,... | collective-permute-start | bytes 344072 | tf_op jit(solution)/shard_map/ppermute | solution.py:83
  68.7 10.5 %collective-permute-start.21 = (bf16[56,8,128]{2,1,0:T(8,128)(2,1)S(1)}, bf16[56,8,128]{2,1,0:T(8,128)(2,1)S(1)}, u32[]{:S(2)}, u32[]{:S(2)}) collective-permute-start(bf16[56,8,128]{2,1,0:T(8,128)(2,1)S(1)} %get-tuple-element.54), channel_id=1, source_target_pairs={{0,192},{1,193},{2,194},{3,195},{4,196},{5,197},{6,198},{7,199},{8... | collective-permute-start | bytes 344072 | tf_op jit(solution)/shard_map/ppermute | solution.py:83
  70.8 8.4 %collective-permute-start.22 = (bf16[56,8,128]{2,1,0:T(8,128)(2,1)S(1)}, bf16[56,8,128]{2,1,0:T(8,128)(2,1)S(1)}, u32[]{:S(2)}, u32[]{:S(2)}) collective-permute-start(bf16[56,8,128]{2,1,0:T(8,128)(2,1)S(1)} %get-tuple-element.55), channel_id=1, source_target_pairs={{0,128},{1,129},{2,130},{3,131},{4,132},{5,133},{6,134},{7,135},{8... | collective-permute-start | bytes 344072 | tf_op jit(solution)/shard_map/ppermute | solution.py:83
  75.0 27.4 %collective-permute-start.14 = (bf16[64,2048]{1,0:T(8,128)(2,1)S(1)}, bf16[64,2048]{1,0:T(8,128)(2,1)S(1)}, u32[]{:S(2)}, u32[]{:S(2)}) collective-permute-start(bf16[64,2048]{1,0:T(8,128)(2,1)S(1)} %get-tuple-element.39), channel_id=1, source_target_pairs={{0,1},{1,0},{2,3},{3,2},{4,5},{5,4},{6,7},{7,6},{8,9},{9,8},{10,11... | collective-permute-start | bytes 786440 | tf_op jit(solution)/shard_map/ppermute | solution.py:83
  75.1 28.8 %collective-permute-start.15 = (bf16[64,2048]{1,0:T(8,128)(2,1)S(1)}, bf16[64,2048]{1,0:T(8,128)(2,1)S(1)}, u32[]{:S(2)}, u32[]{:S(2)}) collective-permute-start(bf16[64,2048]{1,0:T(8,128)(2,1)S(1)} %get-tuple-element.40), channel_id=1, source_target_pairs={{0,3},{1,2},{2,1},{3,0},{4,7},{5,6},{6,5},{7,4},{8,11},{9,10},{10,... | collective-permute-start | bytes 786440 | tf_op jit(solution)/shard_map/ppermute | solution.py:83
  77.4 26.5 %collective-permute-start.16 = (bf16[64,2048]{1,0:T(8,128)(2,1)S(1)}, bf16[64,2048]{1,0:T(8,128)(2,1)S(1)}, u32[]{:S(2)}, u32[]{:S(2)}) collective-permute-start(bf16[64,2048]{1,0:T(8,128)(2,1)S(1)} %get-tuple-element.41), channel_id=1, source_target_pairs={{0,2},{1,3},{2,0},{3,1},{4,6},{5,7},{6,4},{7,5},{8,10},{9,11},{10,... | collective-permute-start | bytes 786440 | tf_op jit(solution)/shard_map/ppermute | solution.py:83
  79.9 4.7 %collective-permute-start.23 = (bf16[28,8,128]{2,1,0:T(8,128)(2,1)S(1)}, bf16[28,8,128]{2,1,0:T(8,128)(2,1)S(1)}, u32[]{:S(2)}, u32[]{:S(2)}) collective-permute-start(bf16[28,8,128]{2,1,0:T(8,128)(2,1)S(1)} %get-tuple-element.57), channel_id=1, source_target_pairs={{0,4},{1,5},{2,6},{3,7},{4,0},{5,1},{6,2},{7,3},{8,12},{9,13},{10,... | collective-permute-start | bytes 172040 | tf_op jit(solution)/shard_map/ppermute | solution.py:83
  82.4 5.2 %collective-permute-start.24 = (bf16[28,8,128]{2,1,0:T(8,128)(2,1)S(1)}, bf16[28,8,128]{2,1,0:T(8,128)(2,1)S(1)}, u32[]{:S(2)}, u32[]{:S(2)}) collective-permute-start(bf16[28,8,128]{2,1,0:T(8,128)(2,1)S(1)} %get-tuple-element.56.mine), channel_id=1, source_target_pairs={{0,16},{1,17},{2,18},{3,19},{4,20},{5,21},{6,22},{7,23},{8,24},{9,... | collective-permute-start | bytes 172040 | tf_op jit(solution)/shard_map/ppermute | solution.py:83
  84.5 4.2 %collective-permute-start.25 = (bf16[28,8,128]{2,1,0:T(8,128)(2,1)S(1)}, bf16[28,8,128]{2,1,0:T(8,128)(2,1)S(1)}, u32[]{:S(2)}, u32[]{:S(2)}) collective-permute-start(bf16[28,8,128]{2,1,0:T(8,128)(2,1)S(1)} %get-tuple-element.57), channel_id=1, source_target_pairs={{0,20},{1,21},{2,22},{3,23},{4,16},{5,17},{6,18},{7,19},{8,28},{9,... | collective-permute-start | bytes 172040 | tf_op jit(solution)/shard_map/ppermute | solution.py:83
  89.3 8.9 %collective-permute-start.26 = (bf16[28,8,128]{2,1,0:T(8,128)(2,1)S(1)}, bf16[28,8,128]{2,1,0:T(8,128)(2,1)S(1)}, u32[]{:S(2)}, u32[]{:S(2)}) collective-permute-start(bf16[28,8,128]{2,1,0:T(8,128)(2,1)S(1)} %shard_map.85.mine), channel_id=1, source_target_pairs={{0,48},{1,49},{2,50},{3,51},{4,52},{5,53},{6,54},{7,55},{8,56},{9,... | collective-permute-start | bytes 172040 | tf_op jit(solution)/shard_map/ppermute | solution.py:83
  98.8 7.9 %collective-permute-start.27 = (bf16[28,8,128]{2,1,0:T(8,128)(2,1)S(1)}, bf16[28,8,128]{2,1,0:T(8,128)(2,1)S(1)}, u32[]{:S(2)}, u32[]{:S(2)}) collective-permute-start(bf16[28,8,128]{2,1,0:T(8,128)(2,1)S(1)} %shard_map.86.refs_0_), channel_id=1, source_target_pairs={{0,64},{1,65},{2,66},{3,67},{4,68},{5,69},{6,70},{7,71},{8,72},{9,... | collective-permute-start | bytes 172040 | tf_op jit(solution)/shard_map/ppermute | solution.py:83
  100.4 6.3 %collective-permute-start.28 = (bf16[28,8,128]{2,1,0:T(8,128)(2,1)S(1)}, bf16[28,8,128]{2,1,0:T(8,128)(2,1)S(1)}, u32[]{:S(2)}, u32[]{:S(2)}) collective-permute-start(bf16[28,8,128]{2,1,0:T(8,128)(2,1)S(1)} %shard_map.86.refs_0_), channel_id=1, source_target_pairs={{0,192},{1,193},{2,194},{3,195},{4,196},{5,197},{6,198},{7,199},{8... | collective-permute-start | bytes 172040 | tf_op jit(solution)/shard_map/ppermute | solution.py:83
  102.5 5.7 %collective-permute-start.29 = (bf16[28,8,128]{2,1,0:T(8,128)(2,1)S(1)}, bf16[28,8,128]{2,1,0:T(8,128)(2,1)S(1)}, u32[]{:S(2)}, u32[]{:S(2)}) collective-permute-start(bf16[28,8,128]{2,1,0:T(8,128)(2,1)S(1)} %shard_map.86.refs_0_), channel_id=1, source_target_pairs={{0,128},{1,129},{2,130},{3,131},{4,132},{5,133},{6,134},{7,135},{8... | collective-permute-start | bytes 172040 | tf_op jit(solution)/shard_map/ppermute | solution.py:83
  104.6 9.8 %collective-permute-start.17 = (bf16[64,2048]{1,0:T(8,128)(2,1)S(1)}, bf16[64,2048]{1,0:T(8,128)(2,1)S(1)}, u32[]{:S(2)}, u32[]{:S(2)}) collective-permute-start(bf16[64,2048]{1,0:T(8,128)(2,1)S(1)} %get-tuple-element.44), channel_id=1, source_target_pairs={{0,0},{1,1},{2,2},{3,3},{4,8},{5,9},{6,10},{7,11},{8,4},{9,5},{10,... | collective-permute-start | bytes 786440 | tf_op jit(solution)/shard_map/ppermute | solution.py:83
  106.6 8.6 %collective-permute-start.18 = (bf16[64,2048]{1,0:T(8,128)(2,1)S(1)}, bf16[64,2048]{1,0:T(8,128)(2,1)S(1)}, u32[]{:S(2)}, u32[]{:S(2)}) collective-permute-start(bf16[64,2048]{1,0:T(8,128)(2,1)S(1)} %get-tuple-element.45), channel_id=1, source_target_pairs={{0,4},{1,5},{2,6},{3,7},{4,12},{5,13},{6,14},{7,15},{8,0},{9,1},{1... | collective-permute-start | bytes 786440 | tf_op jit(solution)/shard_map/ppermute | solution.py:83
  108.8 7.7 %collective-permute-start.30 = (bf16[28,32,128]{2,1,0:T(8,128)(2,1)S(1)}, bf16[28,32,128]{2,1,0:T(8,128)(2,1)S(1)}, u32[]{:S(2)}, u32[]{:S(2)}) collective-permute-start(bf16[28,32,128]{2,1,0:T(8,128)(2,1)S(1)} %shard_map.87.mine), channel_id=1, source_target_pairs={{0,8},{1,9},{2,10},{3,11},{4,12},{5,13},{6,14},{7,15},{8,0},{9,1},... | collective-permute-start | bytes 688136 | tf_op jit(solution)/shard_map/ppermute | solution.py:83

commit v2 on v1

v2 whole, which is shorter than its diff:
```python
import jax
import jax.numpy as jnp
from jax import lax
from jax.experimental import pallas as pl
from jax.experimental.pallas import tpu as pltpu
from jax.sharding import PartitionSpec as P


BF = jnp.bfloat16
F32 = jnp.float32
ROW = 64
OWN = 32 * ROW
GWIN = 34 * ROW
VWIN = 36 * ROW
VMEM = pl.BlockSpec(memory_space=pltpu.VMEM)
SMEM = pl.BlockSpec(memory_space=pltpu.SMEM)
HBM = pl.BlockSpec(memory_space=pltpu.HBM)
PEERS = (1, 3, 2)
STEPS = (0,) + PEERS
ARRIVAL = (0, 1, 3, 2)


def peer(index, s):
    return 3 - index if s == 3 else index ^ s


def pairs(move):
    found = []
    for i in range(256):
        x, h, c, z, y = i // 64, i // 16 % 4, i // 8 % 2, i // 4 % 2, i % 4
        x, h, c, z, y = move(x, h, c, z, y)
        found.append((i, ((x * 4 + h) * 2 + c) * 8 + z * 4 + y))
    return found


def far_plane(x, h, c, z, y):
    plane = (x * 8 + h * 2 + z + (1 if z else -1)) % 32
    return plane // 8, plane // 2 % 4, c, plane % 2, y


def straight(x, h, c, z, y):
    return x, h, z, c, y


def crossed_in(x, h, c, z, y):
    return x, h, 1 - z, c, y


def crossed_out(x, h, c, z, y):
    return x, h, z, 1 - c, y


def other_core(x, h, c, z, y):
    return x, h, 1 - c, z, y


def other_z(x, h, c, z, y):
    return x, h, c, 1 - z, y


def pair_h(x, h, c, z, y):
    return x, h ^ 1, c, z, y


def mirror_h(x, h, c, z, y):
    return x, 3 - h, c, z, y


def ring_z(x, h, c, z, y):
    return (x, (h + 1) % 4, c, 0, y) if z else (x, (h + 3) % 4, c, 1, y)


def pair_zh(x, h, c, z, y):
    return x, h ^ 1, c, 1 - z, y


def peer_x(s):
    return lambda x, h, c, z, y: (peer(x, s), h, c, z, y)


def peer_y(s):
    return lambda x, h, c, z, y: (x, h, c, z, peer(y, s))


def exchange(value, move):
    return lax.ppermute(value, ("depth", "filt"), pairs(move))


def shape(*dims, dtype=BF):
    return jax.ShapeDtypeStruct(dims, dtype)


def call(body, outs, scratch, *args, flops=0, moved=2_000_000, room=4, hbm_in=(), hbm_out=()):
    return pl.pallas_call(
        body,
        out_shape=outs,
        in_specs=[SMEM] + [HBM if i in hbm_in else VMEM for i in range(1, len(args))],
        out_specs=tuple(HBM if i in hbm_out else VMEM for i in range(len(outs))),
        scratch_shapes=scratch,
        compiler_params=pltpu.CompilerParams(vmem_limit_bytes=room * 1024 * 1024),
        cost_estimate=pl.CostEstimate(flops=flops, bytes_accessed=moved, transcendentals=0),
    )(*args)


def at(index, size):
    return pl.ds(pl.multiple_of(index * size, size), size)


Z, Y, C, X, INNER = range(5)


def shifted_columns(values, by):
    if by == 0:
        return values
    moved = pltpu.roll(values, (-by) % values.shape[1], 1)
    column = lax.broadcasted_iota(jnp.int32, values.shape, 1) % ROW
    inside = column < ROW - 1 if by > 0 else column > 0
    return jnp.where(inside, moved, jnp.zeros_like(moved))


def prepare_body(
    place, mine, partner, partner_rest, bias, early, late, middle, backward, biases, filters
):
    z, y, c = place[Z], place[Y], place[C]
    biases[at(z, 32), :] = jnp.broadcast_to(bias[...], (128, 32)).T
    thirds = partner[27].astype(F32)
    biases[at(1 - z, 32), :] = jnp.broadcast_to(
        (thirds[:, :1] + thirds[:, 1:2]) + thirds[:, 2:3], (32, 128)
    )
    for k in range(27):
        filters[k, at(z, 32), :] = mine[k]
        filters[k, at(1 - z, 32), at(c, 128)] = partner[k]
        filters[k, at(1 - z, 32), at(1 - c, 128)] = partner_rest[k]
    blocks = [(c + i) % 2 * 4 + peer(y, s) for s in ARRIVAL for i in range(2)]
    for k in range(0, 27, 2):
        two = filters[k : min(k + 2, 27)].reshape(-1, 256)
        lanes = slice(64 * k, 64 * k + two.shape[0])
        backward[:, lanes] = two.T
        by_arrival = jnp.concatenate([backward[at(block, 32), lanes] for block in blocks]).T
        for j in range(two.shape[0] // 64):
            a, b, d = (k + j) // 9, (k + j) // 3 % 3, (k + j) % 3
            if a == 1:
                middle[64 * d : 64 * d + 64, 256 * b : 256 * b + 256] = filters[k + j]
            else:
                rows, values = slice(128 * d + 32 * a, 128 * d + 32 * a + 64), by_arrival[64 * j : 64 * j + 64]
                early[rows, 192 * b : 192 * b + 192] = values[:, :192]
                late[rows, 64 * b : 64 * b + 64] = values[:, 192:]


def by_arrival(place, shards, window):
    c = place[C]
    n = window.shape[0]
    window[:, pl.ds(pl.multiple_of(GWIN * c, 128), 128)] = jnp.zeros((n, 128), BF)
    start = pl.ds(pl.multiple_of(128 * (1 - c), 128), GWIN)
    at_row = 0
    for shard in shards:
        window[at_row : at_row + shard.shape[0], start] = shard[...]
        at_row += shard.shape[0]


def gather_window(place, shards, window):
    y, c = place[Y], place[C]
    window[:, pl.ds(pl.multiple_of(GWIN * c, 128), 128)] = jnp.zeros((256, 128), BF)
    start = pl.ds(pl.multiple_of(128 * (1 - c), 128), GWIN)
    for n, part in enumerate(shards):
        block = (c + n % 2) % 2 * 4 + peer(y, ARRIVAL[n // 2])
        window[at(block, 32), start] = part[...]


def convolve(window, moved, weights, rows):
    def build(i, _):
        moved[at(i, 32), :] = window[at(i, 32), :][:, ROW : ROW + GWIN]
        return 0

    lax.fori_loop(0, window.shape[0] // 32, build, 0)
    for n in range(0, GWIN, 256):
        size = min(256, GWIN - n)
        planes = (window[:, n : n + size], moved[:, n : n + size], window[:, n + 128 : n + 128 + size])
        got = jnp.dot(weights[...], jnp.concatenate(planes), preferred_element_type=F32)
        left, right = shifted_columns(got[:rows], -1), shifted_columns(got[2 * rows :], 1)
        yield slice(n, n + size), left + got[rows : 2 * rows] + right


def early_body(place, *refs):
    shards, weights, part, window, moved = refs[:6], *refs[6:]
    by_arrival(place, shards, window)
    for cells, total in convolve(window, moved, weights, 128):
        part[:, cells] = total


def late_body(place, one, two, weights, part, near, far, window, moved):
    by_arrival(place, (one, two), window)
    lower = place[Z] == 0
    for cells, total in convolve(window, moved, weights, 128):
        total = total + part[:, cells]
        to_next, to_last = total[:64].astype(BF), total[64:].astype(BF)
        near[:, cells] = jnp.where(lower, to_next, to_last)
        far[:, cells] = jnp.where(lower, to_last, to_next)


def middle_body(place, *refs):
    shards, weights, mid, own, window, moved = refs[:8], *refs[8:]
    gather_window(place, shards, window)
    own[...] = window[:, 2 * ROW : 2 * ROW + OWN]
    for cells, total in convolve(window, moved, weights, 64):
        mid[:, cells] = total


def if_inner(place, values):
    return jnp.where(place[INNER] > 0, values, jnp.zeros_like(values))


def gelu_parts(place, mid, near, far, bias):
    v = mid[...] + bias[:, :1] + near[...].astype(F32) + if_inner(place, far[...].astype(F32))
    square = v * v
    t = jnp.tanh(0.7978845608028654 * (v + 0.044715 * (square * v)))
    return v, square, t


def grad_body(place, mid, near, far, bias, cot_own, cot_other, grad, sums, cot):
    c = place[C]
    cot[at(c, 32), :] = cot_own[...]
    cot[at(1 - c, 32), :] = cot_other[...]
    moved = pltpu.roll(cot[...].astype(F32), jnp.where(c == 0, ROW, GWIN - ROW), 1)
    cell = lax.broadcasted_iota(jnp.int32, moved.shape, 1)
    inside = (cell >= ROW * (1 - c)) & (cell < GWIN - ROW * c)
    cotangent = jnp.where(inside, moved, 0.0)
    v, square, t = gelu_parts(place, mid, near, far, bias)
    inner = 0.7978845608028654 * (1.0 + 3 * 0.044715 * square)
    slope = 0.5 * (1.0 + t) + 0.5 * v * (1.0 - t * t) * inner
    g = (cotangent * slope).astype(BF)
    grad[...] = g
    sums[...] = jnp.sum(g.astype(F32)[:, ROW : ROW + OWN], axis=1, keepdims=True)


def activated_body(place, mid, near, far, bias, mine, other, act):
    v, _, t = gelu_parts(place, mid, near, far, bias)
    act[...] = (v * (0.5 * (1.0 + t)))[:, ROW : ROW + OWN].astype(BF)
    mine[...] = act[at(place[C], 32), :]
    other[...] = act[at(1 - place[C], 32), :]


def shifted_grads(values, stack):
    values = values.astype(F32)
    for c in range(3):
        moved = shifted_columns(values, 1 - c).astype(BF)
        for b in range(3):
            k = (3 * b + c) * 64
            start = ROW * (2 - b)
            stack[k : k + 64, :] = moved[:, start : start + OWN]


def halves(values):
    high = values.astype(BF)
    low = (values - high.astype(F32)).astype(BF)
    lane = lax.broadcasted_iota(jnp.int32, values.shape, values.ndim - 1)
    return jnp.where(lane < 64, high, low)


def whole(values):
    values = values.astype(F32)
    return values + pltpu.roll(values, 64, values.ndim - 1)


def split(values, out):
    n = values.shape[0] * 27 // 28
    out[:n] = values[:n].astype(BF)
    out[n:] = halves(values[n:])


def join(ref):
    n = ref.shape[0] * 27 // 28
    return jnp.concatenate([ref[:n].astype(F32), whole(ref[n:])])


def kernel_grads(place, values, own, keep, send, stack):
    shifted_grads(values, stack)
    lower = place[C] == 0
    got = lax.dot_general(
        stack[...], own[...], (((1,), (1,)), ((), ())), preferred_element_type=F32
    )
    left, right = got[:, :128], got[:, 128:]
    keep[:18] = jnp.where(lower, left, right).reshape(18, 32, 128)
    send[:18] = jnp.where(lower, right, left).reshape(18, 32, 128).astype(BF)


def here_body(place, here, own, sums, keep, send, stack):
    kernel_grads(place, here[...], own, keep, send, stack)
    spread = jnp.broadcast_to(sums[...], (64, 128)).reshape(2, 32, 128)
    keep[18:] = spread
    send[18:] = halves(spread)


def near_body(place, near, own, keep, send, stack):
    kernel_grads(place, near[...], own, keep, send, stack)


def far_body(place, far, own, keep, send, stack):
    kernel_grads(place, if_inner(place, far[...]), own, keep, send, stack)


def input_grad_body(place, near, here, far, weights, *refs):
    outs, (stack, full) = refs[:4], refs[4:]
    lower = place[Z] == 0
    there, here, far = near[...], here[...], if_inner(place, far[...])
    shifted_grads(jnp.where(lower, there, far), stack.at[:576])
    shifted_grads(here, stack.at[576:1152])
    shifted_grads(jnp.where(lower, far, there), stack.at[1152:])
    for n in range(0, OWN, 256):
        full[:, n : n + 256] = jnp.dot(
            weights[...], stack[:, n : n + 256], preferred_element_type=F32
        ).astype(BF)
    y, c = place[Y], place[C]
    for s, out in zip(STEPS, outs, strict=True):
        for i in range(2):
            block = (c + i) % 2 * 4 + peer(y, s)
            out[32 * i : 32 * i + 32, :] = full[at(block, 32), :]


def fold_y_body(place, one, two, three, four, act_own, act_other, straight_out, crossed_out):
    total = (one[...].astype(F32) + four[...].astype(F32)) + (two[...].astype(F32) + three[...].astype(F32))
    total = total.astype(BF)
    straight_out[:32, :] = act_own[...]
    crossed_out[:32, :] = act_other[...]
    straight_out[32:, :] = total[:32]
    crossed_out[32:, :] = total[32:]


def place_body(place, direct, crossed, activated, input_grad):
    z = place[Z]
    for part, half in ((direct, z), (crossed, 1 - z)):
        activated[:, at(half, OWN)] = part[:32, :]
        input_grad[:, at(half, OWN)] = part[32:, :]


def fold_core_body(place, here, near, far, got_here, got_near, got_far, mine, *refs):
    outs, total = refs[:3], refs[3]
    x, z = place[X], place[Z]
    total[18:36] = here[:18] + got_here[:18].astype(F32)
    total[54:] = here[18:] + whole(got_here[18:])
    total[pl.ds(36 * z, 18)] = near[...] + got_near[...].astype(F32)
    total[pl.ds(36 * (1 - z), 18)] = far[...] + got_far[...].astype(F32)
    mine[...] = total[:, at(x, 8), :]
    for s, out in zip(PEERS, outs, strict=True):
        split(total[:, at(peer(x, s), 8), :], out)


def fold_x_body(place, mine, one, two, three, keep, send, total):
    total[...] = (mine[...] + join(one) + join(two) + join(three)).reshape(28, 2, 8, 128)
    split(total[:, pl.ds(place[Z], 1)].reshape(28, 8, 128), keep)
    split(total[:, pl.ds(1 - place[Z], 1)].reshape(28, 8, 128), send)


def fold_zh_body(place, mine, from_z, from_h, from_zh, out):
    split((join(mine) + join(from_z)) + (join(from_h) + join(from_zh)), out)


def fold_h_body(place, mine, got, out):
    split(join(mine) + join(got), out)


def quarters_body(place, *refs):
    parts, out, full = refs[:4], refs[4], refs[5]
    for s, part in zip(STEPS, parts, strict=True):
        full[:, at(peer(place[X], s), 8), :] = part[...].astype(F32)
    out[...] = full[...].astype(BF)


def whole_body(place, mine, other, taps, bias):
    taps[:, :, at(place[C], 128)] = mine[:27].astype(F32)
    taps[:, :, at(1 - place[C], 128)] = other[:27].astype(F32)
    bias[...] = whole(mine[27]).T[:1]


def local(volume, kernel, bias, cotangent):
    filt, depth = lax.axis_index("filt"), lax.axis_index("depth")
    z, c = filt // 4, depth % 2
    plane = depth // 2 * 2 + z
    inner = (plane > 0) & (plane < 31)
    place = jnp.stack([z, filt % 4, c, depth // 8, inner]).astype(jnp.int32)

    def halves_of(value):
        flat = value.reshape(32, 64 * ROW)
        first, second = flat[:, :GWIN], flat[:, 30 * ROW :]
        return jnp.where(z == 0, first, second), jnp.where(z == 0, second, first)

    direct, crossed = halves_of(volume)
    cot_direct, cot_crossed = halves_of(cotangent)

    direct, crossed = exchange(direct, straight), exchange(crossed, crossed_in)
    shards = [direct, crossed]
    shards += [exchange(shards[i], peer_y(s)) for s in PEERS[:2] for i in range(2)]
    last = [exchange(shards[4], peer_y(1)), exchange(shards[3], peer_y(3))]

    high = lax.reduce_precision(bias, 8, 7)
    middle = lax.reduce_precision(bias - high, 8, 7)
    lane = lax.broadcasted_iota(jnp.int32, (1, 32, 128), 2)
    parts = jnp.where(lane == 0, high[:, None], jnp.where(lane == 1, middle[:, None], (bias - high - middle)[:, None]))
    taps = lax.dynamic_slice(kernel, (0, 0, 128 * c), (27, 32, 128))
    taps = exchange(jnp.concatenate([taps, parts.astype(BF)]), ring_z)
    early_weights, late_weights, middle_weights, backward_weights, biases = call(
        prepare_body,
        (shape(384, 576), shape(384, 192), shape(192, 768), shape(256, 1728), shape(64, 128, dtype=F32)),
        [pltpu.VMEM((27, 64, 256), BF)],
        place,
        kernel,
        taps,
        exchange(taps, other_core),
        bias.reshape(1, 32),
        room=8,
    )
    cot_own, cot_other = exchange(cot_direct, straight), exchange(cot_crossed, crossed_in)

    def windows(channels):
        return [pltpu.VMEM((channels, VWIN), BF), pltpu.VMEM((channels, GWIN), BF)]

    (part,) = call(
        early_body,
        (shape(128, GWIN, dtype=F32),),
        windows(192),
        place,
        *shards,
        early_weights,
        flops=2 * 384 * 576 * GWIN,
        room=10,
    )
    near, far = call(
        late_body,
        (shape(64, GWIN), shape(64, GWIN)),
        windows(64),
        place,
        *last,
        late_weights,
        part,
        flops=2 * 384 * 192 * GWIN,
        room=10,
    )
    near, far = exchange(near, other_z), exchange(far, far_plane)
    mid, own = call(
        middle_body,
        (shape(64, GWIN, dtype=F32), shape(256, OWN)),
        windows(256),
        place,
        *shards,
        *last,
        middle_weights,
        flops=2 * 192 * 768 * GWIN,
        room=12,
    )
    grad, sums = call(
        grad_body,
        (shape(64, GWIN), shape(64, 1, dtype=F32)),
        [pltpu.VMEM((64, GWIN), BF)],
        place,
        mid,
        near,
        far,
        biases,
        cot_own,
        cot_other,
        room=12,
    )
    grad_near, grad_far = exchange(grad, other_z), exchange(grad, far_plane)
    act_own, act_other = call(
        activated_body,
        (shape(32, OWN), shape(32, OWN)),
        [pltpu.VMEM((64, OWN), BF)],
        place,
        mid,
        near,
        far,
        biases,
        room=12,
    )

    def wgrad(body, taps, *args):
        keep, send = call(
            body,
            (shape(taps, 32, 128, dtype=F32), shape(taps, 32, 128)),
            [pltpu.VMEM((9 * 64, OWN), BF)],
            place,
            *args,
            flops=2 * 576 * 256 * OWN,
            room=8,
        )
        return keep, exchange(send, other_core)

    grads = [
        wgrad(here_body, 20, grad, own, sums), wgrad(near_body, 18, grad_near, own), wgrad(far_body, 18, grad_far, own)
    ]
    pieces = call(
        input_grad_body,
        tuple(shape(64, OWN) for _ in STEPS),
        [pltpu.VMEM((27 * 64, OWN), BF), pltpu.VMEM((256, OWN), BF)],
        place,
        grad_near,
        grad,
        grad_far,
        backward_weights,
        flops=2 * 1728 * 256 * OWN,
        room=20,
    )

    parts = [pieces[0]] + [exchange(p, peer_y(s)) for s, p in zip(PEERS, pieces[1:])]
    direct, crossed = call(fold_y_body, (shape(64, OWN), shape(64, OWN)), [], place, *parts, act_own, act_other)
    activated, input_grad = call(
        place_body,
        (shape(32, 64 * ROW), shape(32, 64 * ROW)),
        [],
        place,
        exchange(direct, straight),
        exchange(crossed, crossed_out),
    )

    mine, *sends = call(
        fold_core_body,
        (shape(56, 8, 128, dtype=F32),) + (shape(56, 8, 128),) * 3,
        [pltpu.VMEM((56, 32, 128), F32)],
        place,
        *[keep for keep, _ in grads],
        *[got for _, got in grads],
    )
    got = [exchange(value, peer_x(s)) for s, value in zip(PEERS, sends)]
    eight = shape(28, 8, 128)
    keep, send = call(fold_x_body, (eight, eight), [pltpu.VMEM((28, 2, 8, 128), F32)], place, mine, *got)
    got = [exchange(send, other_z), exchange(keep, pair_h), exchange(send, pair_zh)]
    (part,) = call(fold_zh_body, (eight,), [], place, keep, *got)
    (part,) = call(fold_h_body, (eight,), [], place, part, exchange(part, mirror_h))
    got = [exchange(part, peer_x(s)) for s in PEERS]
    (part,) = call(quarters_body, (shape(28, 32, 128),), [pltpu.VMEM((28, 32, 128), F32)], place, part, *got)
    kernel_grad, bias_grad = call(
        whole_body,
        (shape(27, 32, 256, dtype=F32), shape(1, 32, dtype=F32)),
        [],
        place,
        part,
        exchange(part, other_core),
    )
    return (
        activated.reshape(32, 1, 64 * ROW),
        input_grad.reshape(32, 1, 64 * ROW),
        kernel_grad,
        bias_grad.reshape(32),
    )


def solution(mesh):
    placed = (P("filt", "depth", None), P(None, "filt", None), P("filt"), P("filt", "depth", None))
    return jax.shard_map(
        local,
        mesh=mesh,
        in_specs=placed,
        out_specs=(
            P("filt", "depth", None),
            P("filt", "depth", None),
            P(None, "filt", None),
            P("filt"),
        ),
        check_vma=False,
    )
```

time: 120 us -> 109 us (0.908)
  waiting for transfers between devices: 36.5 us -> 20.9 us
  Pallas kernels: 22.4 us -> 25.9 us
  starting transfers between devices: 54.9 us -> 58 us
  other arithmetic: 2.13 us -> 0.92 us
    ppermute x31 -> x35, waiting for transfers between devices: 36.5 us -> 20.9 us  [exchange(): return lax.ppermute(value, ('depth', 'filt'), pairs(move))]
    pallas_call x14 -> x18, Pallas kernels: 22.4 us -> 25.9 us  [call(): pl.pallas_call(body, out_shape=outs, in_specs=[SMEM] + [HBM if i in hbm_i...]
    ppermute x31 -> x35, starting transfers between devices: 54.9 us -> 58 us  [exchange(): return lax.ppermute(value, ('depth', 'filt'), pairs(move))]
    select_n x3 -> x2, other arithmetic: 1.98 us -> 0.06 us  [halves_of(): return (jnp.where(z == 0, first, second), jnp.where(z == 0, second, first))]
  transfers between devices with their start and end apart: 31 -> 35, of which waited for: 17 -> 11; matrix products, arithmetic and copies ran while one was open for 1% -> 0% of each run, Pallas kernels for 12% -> 19%
where the time goes in v2:
time: 109 us; the launch traced here: 108 us
  starting transfers between devices  58 us (53%)
  Pallas kernels  25.9 us (24%)
  waiting for transfers between devices  20.9 us (19%)
    ppermute x35, starting transfers between devices, exchange(): return lax.ppermute(value, ('depth', 'filt'), pairs(move))  58 us
    pallas_call x18, Pallas kernels, call(): pl.pallas_call(body, out_shape=outs, in_specs=[SMEM] + [HBM if i in hbm_i...  25.9 us
    ppermute x35, waiting for transfers between devices, exchange(): return lax.ppermute(value, ('depth', 'filt'), pairs(move))  20.9 us
  transfers between devices with their start and end apart: 35, of which 11 were waited for; matrix products, arithmetic and copies ran while one was open for 0% of the time, Pallas kernels for 19%

profile of v2, /device:TPU:32, one launch (start us, length us, event | category | flops | bytes accessed | tf_op | source)
XLA Modules:
  0.0 107.8 jit_solution(11834750138318417847)
XLA Ops:
  0.7 0.7 fusion
  1.4 0.9 constant_dynamic-slice_fusion
  2.5 2.0 %collective-permute-start.8 = (bf16[28,32,128]{2,1,0:T(8,128)(2,1)S(1)}, bf16[28,32,128]{2,1,0:T(8,128)(2,1)S(1)}, u32[]{:S(2)}, u32[]{:S(2)}) collective-permute-start(bf16[28,32,128]{2,1,0:T(8,128)(2,1)S(1)} %pad_maximum_fusion), channel_id=1, source_target_pairs={{0,52},{1,53},{2,54},{3,55},{4,16},{5,17},{6,18},{7,19},{8,60},{9,... | collective-permute-start | bytes 688136 | tf_op jit(solution)/shard_map/ppermute | solution.py:86
  4.6 4.1 %collective-permute-start.1 = (bf16[32,2176]{1,0:T(8,128)(2,1)S(1)}, bf16[32,2176]{1,0:T(8,128)(2,1)S(1)}, u32[]{:S(2)}, u32[]{:S(2)}) collective-permute-start(bf16[32,2176]{1,0:T(8,128)(2,1)S(1)} %get-tuple-element.76), channel_id=1, source_target_pairs={{0,8},{1,9},{2,10},{3,11},{4,0},{5,1},{6,2},{7,3},{8,12},{9,13},{1... | collective-permute-start | bytes 417800 | tf_op jit(solution)/shard_map/ppermute | solution.py:86
  8.7 1.9 %collective-permute-start = (bf16[32,2176]{1,0:T(8,128)(2,1)S(1)}, bf16[32,2176]{1,0:T(8,128)(2,1)S(1)}, u32[]{:S(2)}, u32[]{:S(2)}) collective-permute-start(bf16[32,2176]{1,0:T(8,128)(2,1)S(1)} %get-tuple-element.77), channel_id=1, source_target_pairs={{0,0},{1,1},{2,2},{3,3},{4,8},{5,9},{6,10},{7,11},{8,4},{9,5},{10,... | collective-permute-start | bytes 417800 | tf_op jit(solution)/shard_map/ppermute | solution.py:86
  11.3 1.6 %collective-permute-start.3 = (bf16[32,2176]{1,0:T(8,128)(2,1)S(1)}, bf16[32,2176]{1,0:T(8,128)(2,1)S(1)}, u32[]{:S(2)}, u32[]{:S(2)}) collective-permute-start(bf16[32,2176]{1,0:T(8,128)(2,1)S(1)} %collective-permute-done.1.refs_1_), channel_id=1, source_target_pairs={{0,1},{1,0},{2,3},{3,2},{4,5},{5,4},{6,7},{7,6},{8,9},{9,8},{10,11... | collective-permute-start | bytes 417800 | tf_op jit(solution)/shard_map/ppermute | solution.py:86
  12.9 2.2 %collective-permute-done.refs_0_ = bf16[32,2176]{1,0:T(8,128)(2,1)S(1)} collective-permute-done((bf16[32,2176]{1,0:T(8,128)(2,1)S(1)}, bf16[32,2176]{1,0:T(8,128)(2,1)S(1)}, u32[]{:S(2)}, u32[]{:S(2)}) %collective-permute-start) | collective-permute-done | bytes 139296 | tf_op jit(solution)/shard_map/ppermute | solution.py:86
  15.1 3.0 %collective-permute-start.4 = (bf16[32,2176]{1,0:T(8,128)(2,1)S(1)}, bf16[32,2176]{1,0:T(8,128)(2,1)S(1)}, u32[]{:S(2)}, u32[]{:S(2)}) collective-permute-start(bf16[32,2176]{1,0:T(8,128)(2,1)S(1)} %collective-permute-done.refs_0_), channel_id=1, source_target_pairs={{0,3},{1,2},{2,1},{3,0},{4,7},{5,6},{6,5},{7,4},{8,11},{9,10},{10,... | collective-permute-start | bytes 417800 | tf_op jit(solution)/shard_map/ppermute | solution.py:86
  18.7 2.7 %collective-permute-start.7 = (bf16[32,2176]{1,0:T(8,128)(2,1)S(1)}, bf16[32,2176]{1,0:T(8,128)(2,1)S(1)}, u32[]{:S(2)}, u32[]{:S(2)}) collective-permute-start(bf16[32,2176]{1,0:T(8,128)(2,1)S(1)} %collective-permute-done.3.refs_3_), channel_id=1, source_target_pairs={{0,3},{1,2},{2,1},{3,0},{4,7},{5,6},{6,5},{7,4},{8,11},{9,10},{10,... | collective-permute-start | bytes 417800 | tf_op jit(solution)/shard_map/ppermute | solution.py:86
  21.3 1.4 %collective-permute-done.4.refs_4_ = bf16[32,2176]{1,0:T(8,128)(2,1)S(1)} collective-permute-done((bf16[32,2176]{1,0:T(8,128)(2,1)S(1)}, bf16[32,2176]{1,0:T(8,128)(2,1)S(1)}, u32[]{:S(2)}, u32[]{:S(2)}) %collective-permute-start.4) | collective-permute-done | bytes 139296 | tf_op jit(solution)/shard_map/ppermute | solution.py:86
  23.1 1.8 %shard_map.75 = (bf16[384,576]{1,0:T(8,128)(2,1)S(1)}, bf16[384,192]{1,0:T(8,128)(2,1)S(1)}, bf16[192,768]{1,0:T(8,128)(2,1)S(1)}, bf16[256,1728]{1,0:T(8,128)(2,1)S(1)}, f32[64,128]{1,0:T(8,128)S(1)}) custom-call(s32[5]{0:T(128)S(1)} %stack.27.place, bf16[27,32,256]{2,1,0:T(8,128)(2,1)S(1)} %copy-done, ...), custom_call_target="tpu_custom_call" | custom-call | bytes 2000000 | tf_op jit(solution)/shard_map/pallas_call | solution.py:94
  24.9 2.8 %shard_map.77.part = f32[128,2176]{1,0:T(8,128)S(1)} custom-call(s32[5]{0:T(128)S(1)} %stack.27.place, bf16[32,2176]{1,0:T(8,128)(2,1)S(1)} %collective-permute-done.refs_0_, bf16[32,2176]{1,0:T(8,128)(2,1)S(1)} %collective-permute-done.1.refs_1_, bf16[32,2176]{1,0:T(8,128)(2,1)S(1)} %collective-permute-done.2.refs_2_, ...), custom_call_target="tpu_custom_call" | custom-call | flops 962592768 | bytes 2000000 | tf_op jit(solution)/shard_map/pallas_call | solution.py:94
  27.8 1.6 %shard_map.78 = (bf16[64,2176]{1,0:T(8,128)(2,1)S(1)}, bf16[64,2176]{1,0:T(8,128)(2,1)S(1)}) custom-call(s32[5]{0:T(128)S(1)} %stack.27.place, bf16[32,2176]{1,0:T(8,128)(2,1)S(1)} %collective-permute-done.6.refs_6_.one, bf16[32,2176]{1,0:T(8,128)(2,1)S(1)} %collective-permute-done.7.refs_7_.two, bf16[384,192]{1,0:T(8,128)(2,1)S(1)} %get-tuple-element.41.weights, ...), custom_call_target="tpu_custom_call" | custom-call | flops 320864256 | bytes 2000000 | tf_op jit(solution)/shard_map/pallas_call | solution.py:94
  29.5 1.6 %collective-permute-start.10 = (bf16[64,2176]{1,0:T(8,128)(2,1)S(1)}, bf16[64,2176]{1,0:T(8,128)(2,1)S(1)}, u32[]{:S(2)}, u32[]{:S(2)}) collective-permute-start(bf16[64,2176]{1,0:T(8,128)(2,1)S(1)} %get-tuple-element.43), channel_id=1, source_target_pairs={{0,4},{1,5},{2,6},{3,7},{4,0},{5,1},{6,2},{7,3},{8,12},{9,13},{10,... | collective-permute-start | bytes 835592 | tf_op jit(solution)/shard_map/ppermute | solution.py:86
  31.1 1.0 collective-permute-start.11
  32.1 4.3 %collective-permute-start.13 = (bf16[32,2176]{1,0:T(8,128)(2,1)S(1)}, bf16[32,2176]{1,0:T(8,128)(2,1)S(1)}, u32[]{:S(2)}, u32[]{:S(2)}) collective-permute-start(bf16[32,2176]{1,0:T(8,128)(2,1)S(1)} %get-tuple-element.74), channel_id=1, source_target_pairs={{0,8},{1,9},{2,10},{3,11},{4,0},{5,1},{6,2},{7,3},{8,12},{9,13},{1... | collective-permute-start | bytes 417800 | tf_op jit(solution)/shard_map/ppermute | solution.py:86
  36.5 2.1 %collective-permute-start.12 = (bf16[32,2176]{1,0:T(8,128)(2,1)S(1)}, bf16[32,2176]{1,0:T(8,128)(2,1)S(1)}, u32[]{:S(2)}, u32[]{:S(2)}) collective-permute-start(bf16[32,2176]{1,0:T(8,128)(2,1)S(1)} %get-tuple-element.75), channel_id=1, source_target_pairs={{0,0},{1,1},{2,2},{3,3},{4,8},{5,9},{6,10},{7,11},{8,4},{9,5},{10,... | collective-permute-start | bytes 417800 | tf_op jit(solution)/shard_map/ppermute | solution.py:86
  38.6 2.5 %shard_map.76 = (f32[64,2176]{1,0:T(8,128)S(1)}, bf16[256,2048]{1,0:T(8,128)(2,1)S(1)}) custom-call(s32[5]{0:T(128)S(1)} %stack.27.place, bf16[32,2176]{1,0:T(8,128)(2,1)S(1)} %collective-permute-done.refs_0_, bf16[32,2176]{1,0:T(8,128)(2,1)S(1)} %collective-permute-done.1.refs_1_, bf16[32,2176]{1,0:T(8,128)(2,1)S(1)} %collective-permute-done.2.refs_2_, ...), custom_call_target="tpu_custom_call" | custom-call | flops 641728512 | bytes 2000000 | tf_op jit(solution)/shard_map/pallas_call | solution.py:94
  41.1 1.8 %collective-permute-done.12.cot_own = bf16[32,2176]{1,0:T(8,128)(2,1)S(1)} collective-permute-done((bf16[32,2176]{1,0:T(8,128)(2,1)S(1)}, bf16[32,2176]{1,0:T(8,128)(2,1)S(1)}, u32[]{:S(2)}, u32[]{:S(2)}) %collective-permute-start.12) | collective-permute-done | bytes 139296 | tf_op jit(solution)/shard_map/ppermute | solution.py:86
  42.8 1.5 %shard_map.79 = (bf16[64,2176]{1,0:T(8,128)(2,1)S(1)}, f32[64,1]{1,0:T(8,128)S(1)}) custom-call(s32[5]{0:T(128)S(1)} %stack.27.place, f32[64,2176]{1,0:T(8,128)S(1)} %get-tuple-element.40.mid, bf16[64,2176]{1,0:T(8,128)(2,1)S(1)} %collective-permute-done.10.near, bf16[64,2176]{1,0:T(8,128)(2,1)S(1)} %collective-permute-done.11.far, ...), custom_call_target="tpu_custom_call" | custom-call | bytes 2000000 | tf_op jit(solution)/shard_map/pallas_call | solution.py:94
  44.3 4.1 %collective-permute-start.14 = (bf16[64,2176]{1,0:T(8,128)(2,1)S(1)}, bf16[64,2176]{1,0:T(8,128)(2,1)S(1)}, u32[]{:S(2)}, u32[]{:S(2)}) collective-permute-start(bf16[64,2176]{1,0:T(8,128)(2,1)S(1)} %get-tuple-element.46.here), channel_id=1, source_target_pairs={{0,4},{1,5},{2,6},{3,7},{4,0},{5,1},{6,2},{7,3},{8,12},{9,13},{10,... | collective-permute-start | bytes 835592 | tf_op jit(solution)/shard_map/ppermute | solution.py:86
  48.4 1.5 %shard_map.84 = (f32[20,32,128]{2,1,0:T(8,128)S(1)}, bf16[20,32,128]{2,1,0:T(8,128)(2,1)S(1)}) custom-call(s32[5]{0:T(128)S(1)} %stack.27.place, bf16[64,2176]{1,0:T(8,128)(2,1)S(1)} %get-tuple-element.46.here, bf16[256,2048]{1,0:T(8,128)(2,1)S(1)} %get-tuple-element.58.own, f32[64,1]{1,0:T(8,128)S(1)} %get-tuple-element.59.sums), custom_call_target="tpu_custom_call" | custom-call | flops 603979776 | bytes 2000000 | tf_op jit(solution)/shard_map/pallas_call | solution.py:94
  50.1 0.8 collective-permute-done.15.far
  50.9 1.6 %shard_map.86 = (f32[18,32,128]{2,1,0:T(8,128)S(1)}, bf16[18,32,128]{2,1,0:T(8,128)(2,1)S(1)}) custom-call(s32[5]{0:T(128)S(1)} %stack.27.place, bf16[64,2176]{1,0:T(8,128)(2,1)S(1)} %collective-permute-done.15.far, bf16[256,2048]{1,0:T(8,128)(2,1)S(1)} %get-tuple-element.58.own), custom_call_target="tpu_custom_call" | custom-call | flops 603979776 | bytes 2000000 | tf_op jit(solution)/shard_map/pallas_call | solution.py:94
  53.0 1.5 %shard_map.85 = (f32[18,32,128]{2,1,0:T(8,128)S(1)}, bf16[18,32,128]{2,1,0:T(8,128)(2,1)S(1)}) custom-call(s32[5]{0:T(128)S(1)} %stack.27.place, bf16[64,2176]{1,0:T(8,128)(2,1)S(1)} %collective-permute-done.14.near, bf16[256,2048]{1,0:T(8,128)(2,1)S(1)} %get-tuple-element.58.own), custom_call_target="tpu_custom_call" | custom-call | flops 603979776 | bytes 2000000 | tf_op jit(solution)/shard_map/pallas_call | solution.py:94
  54.7 1.3 %collective-permute-done.22.got_near = bf16[18,32,128]{2,1,0:T(8,128)(2,1)S(1)} collective-permute-done((bf16[18,32,128]{2,1,0:T(8,128)(2,1)S(1)}, bf16[18,32,128]{2,1,0:T(8,128)(2,1)S(1)}, u32[]{:S(2)}, u32[]{:S(2)}) %collective-permute-start.22) | collective-permute-done | bytes 147488 | tf_op jit(solution)/shard_map/ppermute | solution.py:86
  56.0 0.8 shard_map.87
  56.9 2.0 %collective-permute-start.25 = (bf16[56,8,128]{2,1,0:T(8,128)(2,1)S(1)}, bf16[56,8,128]{2,1,0:T(8,128)(2,1)S(1)}, u32[]{:S(2)}, u32[]{:S(2)}) collective-permute-start(bf16[56,8,128]{2,1,0:T(8,128)(2,1)S(1)} %get-tuple-element.68), channel_id=1, source_target_pairs={{0,192},{1,193},{2,194},{3,195},{4,196},{5,197},{6,198},{7,199},{8... | collective-permute-start | bytes 344072 | tf_op jit(solution)/shard_map/ppermute | solution.py:86
  58.8 2.1 %collective-permute-start.26 = (bf16[56,8,128]{2,1,0:T(8,128)(2,1)S(1)}, bf16[56,8,128]{2,1,0:T(8,128)(2,1)S(1)}, u32[]{:S(2)}, u32[]{:S(2)}) collective-permute-start(bf16[56,8,128]{2,1,0:T(8,128)(2,1)S(1)} %get-tuple-element.69), channel_id=1, source_target_pairs={{0,128},{1,129},{2,130},{3,131},{4,132},{5,133},{6,134},{7,135},{8... | collective-permute-start | bytes 344072 | tf_op jit(solution)/shard_map/ppermute | solution.py:86
  61.0 3.2 %shard_map.80 = (bf16[64,2048]{1,0:T(8,128)(2,1)S(1)}, bf16[64,2048]{1,0:T(8,128)(2,1)S(1)}, bf16[64,2048]{1,0:T(8,128)(2,1)S(1)}, bf16[64,2048]{1,0:T(8,128)(2,1)S(1)}) custom-call(s32[5]{0:T(128)S(1)} %stack.27.place, bf16[64,2176]{1,0:T(8,128)(2,1)S(1)} %collective-permute-done.14.near, bf16[64,2176]{1,0:T(8,128)(2,1)S(1)} %get-tuple-element.46.here, ...), custom_call_target="tpu_custom_call" | custom-call | flops 1811939328 | bytes 2000000 | tf_op jit(solution)/shard_map/pallas_call | solution.py:94
  64.2 1.4 %collective-permute-start.16 = (bf16[64,2048]{1,0:T(8,128)(2,1)S(1)}, bf16[64,2048]{1,0:T(8,128)(2,1)S(1)}, u32[]{:S(2)}, u32[]{:S(2)}) collective-permute-start(bf16[64,2048]{1,0:T(8,128)(2,1)S(1)} %get-tuple-element.49), channel_id=1, source_target_pairs={{0,1},{1,0},{2,3},{3,2},{4,5},{5,4},{6,7},{7,6},{8,9},{9,8},{10,11... | collective-permute-start | bytes 786440 | tf_op jit(solution)/shard_map/ppermute | solution.py:86
  65.6 1.8 %collective-permute-start.17 = (bf16[64,2048]{1,0:T(8,128)(2,1)S(1)}, bf16[64,2048]{1,0:T(8,128)(2,1)S(1)}, u32[]{:S(2)}, u32[]{:S(2)}) collective-permute-start(bf16[64,2048]{1,0:T(8,128)(2,1)S(1)} %get-tuple-element.50), channel_id=1, source_target_pairs={{0,3},{1,2},{2,1},{3,0},{4,7},{5,6},{6,5},{7,4},{8,11},{9,10},{10,... | collective-permute-start | bytes 786440 | tf_op jit(solution)/shard_map/ppermute | solution.py:86
  67.3 1.3 %collective-permute-start.18 = (bf16[64,2048]{1,0:T(8,128)(2,1)S(1)}, bf16[64,2048]{1,0:T(8,128)(2,1)S(1)}, u32[]{:S(2)}, u32[]{:S(2)}) collective-permute-start(bf16[64,2048]{1,0:T(8,128)(2,1)S(1)} %get-tuple-element.51), channel_id=1, source_target_pairs={{0,2},{1,3},{2,0},{3,1},{4,6},{5,7},{6,4},{7,5},{8,10},{9,11},{10,... | collective-permute-start | bytes 786440 | tf_op jit(solution)/shard_map/ppermute | solution.py:86
  69.2 2.0 %collective-permute-start.28 = (bf16[28,8,128]{2,1,0:T(8,128)(2,1)S(1)}, bf16[28,8,128]{2,1,0:T(8,128)(2,1)S(1)}, u32[]{:S(2)}, u32[]{:S(2)}) collective-permute-start(bf16[28,8,128]{2,1,0:T(8,128)(2,1)S(1)} %get-tuple-element.70.mine), channel_id=1, source_target_pairs={{0,16},{1,17},{2,18},{3,19},{4,20},{5,21},{6,22},{7,23},{8,24},{9,... | collective-permute-start | bytes 172040 | tf_op jit(solution)/shard_map/ppermute | solution.py:86
  71.2 4.6 %collective-permute-start.29 = (bf16[28,8,128]{2,1,0:T(8,128)(2,1)S(1)}, bf16[28,8,128]{2,1,0:T(8,128)(2,1)S(1)}, u32[]{:S(2)}, u32[]{:S(2)}) collective-permute-start(bf16[28,8,128]{2,1,0:T(8,128)(2,1)S(1)} %get-tuple-element.71), channel_id=1, source_target_pairs={{0,20},{1,21},{2,22},{3,23},{4,16},{5,17},{6,18},{7,19},{8,28},{9,... | collective-permute-start | bytes 172040 | tf_op jit(solution)/shard_map/ppermute | solution.py:86
  75.7 3.6 %collective-permute-start.27 = (bf16[28,8,128]{2,1,0:T(8,128)(2,1)S(1)}, bf16[28,8,128]{2,1,0:T(8,128)(2,1)S(1)}, u32[]{:S(2)}, u32[]{:S(2)}) collective-permute-start(bf16[28,8,128]{2,1,0:T(8,128)(2,1)S(1)} %get-tuple-element.71), channel_id=1, source_target_pairs={{0,4},{1,5},{2,6},{3,7},{4,0},{5,1},{6,2},{7,3},{8,12},{9,13},{10,... | collective-permute-start | bytes 172040 | tf_op jit(solution)/shard_map/ppermute | solution.py:86
  79.4 2.2 %collective-permute-done.27.from_z = bf16[28,8,128]{2,1,0:T(8,128)(2,1)S(1)} collective-permute-done((bf16[28,8,128]{2,1,0:T(8,128)(2,1)S(1)}, bf16[28,8,128]{2,1,0:T(8,128)(2,1)S(1)}, u32[]{:S(2)}, u32[]{:S(2)}) %collective-permute-start.27) | collective-permute-done | bytes 57376 | tf_op jit(solution)/shard_map/ppermute | solution.py:86
  82.1 2.0 %collective-permute-start.30 = (bf16[28,8,128]{2,1,0:T(8,128)(2,1)S(1)}, bf16[28,8,128]{2,1,0:T(8,128)(2,1)S(1)}, u32[]{:S(2)}, u32[]{:S(2)}) collective-permute-start(bf16[28,8,128]{2,1,0:T(8,128)(2,1)S(1)} %shard_map.89.mine), channel_id=1, source_target_pairs={{0,48},{1,49},{2,50},{3,51},{4,52},{5,53},{6,54},{7,55},{8,56},{9,... | collective-permute-start | bytes 172040 | tf_op jit(solution)/shard_map/ppermute | solution.py:86
  84.2 4.3 %collective-permute-done.30.got = bf16[28,8,128]{2,1,0:T(8,128)(2,1)S(1)} collective-permute-done((bf16[28,8,128]{2,1,0:T(8,128)(2,1)S(1)}, bf16[28,8,128]{2,1,0:T(8,128)(2,1)S(1)}, u32[]{:S(2)}, u32[]{:S(2)}) %collective-permute-start.30) | collective-permute-done | bytes 57376 | tf_op jit(solution)/shard_map/ppermute | solution.py:86
  89.1 0.8 collective-permute-start.33
  89.9 2.1 %collective-permute-start.32 = (bf16[28,8,128]{2,1,0:T(8,128)(2,1)S(1)}, bf16[28,8,128]{2,1,0:T(8,128)(2,1)S(1)}, u32[]{:S(2)}, u32[]{:S(2)}) collective-permute-start(bf16[28,8,128]{2,1,0:T(8,128)(2,1)S(1)} %shard_map.90.refs_0_), channel_id=1, source_target_pairs={{0,192},{1,193},{2,194},{3,195},{4,196},{5,197},{6,198},{7,199},{8... | collective-permute-start | bytes 172040 | tf_op jit(solution)/shard_map/ppermute | solution.py:86
  92.6 1.0 shard_map.81
  94.3 1.9 %collective-permute-start.19 = (bf16[64,2048]{1,0:T(8,128)(2,1)S(1)}, bf16[64,2048]{1,0:T(8,128)(2,1)S(1)}, u32[]{:S(2)}, u32[]{:S(2)}) collective-permute-start(bf16[64,2048]{1,0:T(8,128)(2,1)S(1)} %get-tuple-element.54), channel_id=1, source_target_pairs={{0,0},{1,1},{2,2},{3,3},{4,8},{5,9},{6,10},{7,11},{8,4},{9,5},{10,... | collective-permute-start | bytes 786440 | tf_op jit(solution)/shard_map/ppermute | solution.py:86
  97.0 1.9 %collective-permute-start.34 = (bf16[28,32,128]{2,1,0:T(8,128)(2,1)S(1)}, bf16[28,32,128]{2,1,0:T(8,128)(2,1)S(1)}, u32[]{:S(2)}, u32[]{:S(2)}) collective-permute-start(bf16[28,32,128]{2,1,0:T(8,128)(2,1)S(1)} %shard_map.91.mine), channel_id=1, source_target_pairs={{0,8},{1,9},{2,10},{3,11},{4,12},{5,13},{6,14},{7,15},{8,0},{9,1},... | collective-permute-start | bytes 688136 | tf_op jit(solution)/shard_map/ppermute | solution.py:86
  98.9 5.2 %collective-permute-done.19.direct = bf16[64,2048]{1,0:T(8,128)(2,1)S(1)} collective-permute-done((bf16[64,2048]{1,0:T(8,128)(2,1)S(1)}, bf16[64,2048]{1,0:T(8,128)(2,1)S(1)}, u32[]{:S(2)}, u32[]{:S(2)}) %collective-permute-start.19) | collective-permute-done | bytes 262176 | tf_op jit(solution)/shard_map/ppermute | solution.py:86
  104.1 0.7 collective-permute-done.20.crossed
  104.8 1.4 %shard_map.83 = (bf16[32,4096]{1,0:T(8,128)(2,1)}, bf16[32,4096]{1,0:T(8,128)(2,1)}) custom-call(s32[5]{0:T(128)S(1)} %stack.27.place, bf16[64,2048]{1,0:T(8,128)(2,1)S(1)} %collective-permute-done.19.direct, bf16[64,2048]{1,0:T(8,128)(2,1)S(1)} %collective-permute-done.20.crossed), custom_call_target="tpu_custom_call" | custom-call | bytes 2000000 | tf_op jit(solution)/shard_map/pallas_call | solution.py:94
  106.2 1.6 %shard_map.92 = (f32[27,32,256]{2,1,0:T(8,128)}, f32[1,32]{1,0:T(1,128)}) custom-call(s32[5]{0:T(128)S(1)} %stack.27.place, bf16[28,32,128]{2,1,0:T(8,128)(2,1)S(1)} %shard_map.91.mine, bf16[28,32,128]{2,1,0:T(8,128)(2,1)S(1)} %collective-permute-done.34.other), custom_call_target="tpu_custom_call" | custom-call | bytes 2000000 | tf_op jit(solution)/shard_map/pallas_call | solution.py:94
  (56 shorter events, 6.7 us)
Async XLA Ops:
  0.6 22.5 %copy-start.1 = (f32[32]{0:T(128)S(1)}, f32[32]{0:T(128)}, u32[]{:S(2)}) copy-start(f32[32]{0:T(128)} %param.6) | copy-start | bytes 388
  0.6 22.5 %copy-start = (bf16[27,32,256]{2,1,0:T(8,128)(2,1)S(1)}, bf16[27,32,256]{2,1,0:T(8,128)(2,1)}, u32[]{:S(2)}) copy-start(bf16[27,32,256]{2,1,0:T(8,128)(2,1)} %mine.1) | copy-start | bytes 1327108
  0.7 3.9 %copy-start.2 = (bf16[32,1,4096]{2,0,1:T(8,128)(2,1)S(1)}, bf16[32,1,4096]{2,0,1:T(8,128)(2,1)}, u32[]{:S(2)}) copy-start(bf16[32,1,4096]{2,0,1:T(8,128)(2,1)} %param.4) | copy-start | bytes 786436
  2.5 8.1 %collective-permute-start.8 = (bf16[28,32,128]{2,1,0:T(8,128)(2,1)S(1)}, bf16[28,32,128]{2,1,0:T(8,128)(2,1)S(1)}, u32[]{:S(2)}, u32[]{:S(2)}) collective-permute-start(bf16[28,32,128]{2,1,0:T(8,128)(2,1)S(1)} %pad_maximum_fusion), channel_id=1, source_target_pairs={{0,52},{1,53},{2,54},{3,55},{4,16},{5,17},{6,18},{7,19},{8,60},{9,... | collective-permute-start | bytes 688136 | tf_op jit(solution)/shard_map/ppermute | solution.py:86
  4.6 6.7 %collective-permute-start.1 = (bf16[32,2176]{1,0:T(8,128)(2,1)S(1)}, bf16[32,2176]{1,0:T(8,128)(2,1)S(1)}, u32[]{:S(2)}, u32[]{:S(2)}) collective-permute-start(bf16[32,2176]{1,0:T(8,128)(2,1)S(1)} %get-tuple-element.76), channel_id=1, source_target_pairs={{0,8},{1,9},{2,10},{3,11},{4,0},{5,1},{6,2},{7,3},{8,12},{9,13},{1... | collective-permute-start | bytes 417800 | tf_op jit(solution)/shard_map/ppermute | solution.py:86
  8.7 6.4 %collective-permute-start = (bf16[32,2176]{1,0:T(8,128)(2,1)S(1)}, bf16[32,2176]{1,0:T(8,128)(2,1)S(1)}, u32[]{:S(2)}, u32[]{:S(2)}) collective-permute-start(bf16[32,2176]{1,0:T(8,128)(2,1)S(1)} %get-tuple-element.77), channel_id=1, source_target_pairs={{0,0},{1,1},{2,2},{3,3},{4,8},{5,9},{6,10},{7,11},{8,4},{9,5},{10,... | collective-permute-start | bytes 417800 | tf_op jit(solution)/shard_map/ppermute | solution.py:86
  10.6 12.5 %collective-permute-start.9 = (bf16[28,32,128]{2,1,0:T(8,128)(2,1)S(1)}, bf16[28,32,128]{2,1,0:T(8,128)(2,1)S(1)}, u32[]{:S(2)}, u32[]{:S(2)}) collective-permute-start(bf16[28,32,128]{2,1,0:T(8,128)(2,1)S(1)} %collective-permute-done.8.partner), channel_id=1, source_target_pairs={{0,8},{1,9},{2,10},{3,11},{4,12},{5,13},{6,14},{7,15},{8,0},{9,1},... | collective-permute-start | bytes 688136 | tf_op jit(solution)/shard_map/ppermute | solution.py:86
  11.3 7.4 %collective-permute-start.3 = (bf16[32,2176]{1,0:T(8,128)(2,1)S(1)}, bf16[32,2176]{1,0:T(8,128)(2,1)S(1)}, u32[]{:S(2)}, u32[]{:S(2)}) collective-permute-start(bf16[32,2176]{1,0:T(8,128)(2,1)S(1)} %collective-permute-done.1.refs_1_), channel_id=1, source_target_pairs={{0,1},{1,0},{2,3},{3,2},{4,5},{5,4},{6,7},{7,6},{8,9},{9,8},{10,11... | collective-permute-start | bytes 417800 | tf_op jit(solution)/shard_map/ppermute | solution.py:86
  15.1 7.7 %collective-permute-start.4 = (bf16[32,2176]{1,0:T(8,128)(2,1)S(1)}, bf16[32,2176]{1,0:T(8,128)(2,1)S(1)}, u32[]{:S(2)}, u32[]{:S(2)}) collective-permute-start(bf16[32,2176]{1,0:T(8,128)(2,1)S(1)} %collective-permute-done.refs_0_), channel_id=1, source_target_pairs={{0,3},{1,2},{2,1},{3,0},{4,7},{5,6},{6,5},{7,4},{8,11},{9,10},{10,... | collective-permute-start | bytes 417800 | tf_op jit(solution)/shard_map/ppermute | solution.py:86
  18.1 6.9 %collective-permute-start.5 = (bf16[32,2176]{1,0:T(8,128)(2,1)S(1)}, bf16[32,2176]{1,0:T(8,128)(2,1)S(1)}, u32[]{:S(2)}, u32[]{:S(2)}) collective-permute-start(bf16[32,2176]{1,0:T(8,128)(2,1)S(1)} %collective-permute-done.1.refs_1_), channel_id=1, source_target_pairs={{0,3},{1,2},{2,1},{3,0},{4,7},{5,6},{6,5},{7,4},{8,11},{9,10},{10,... | collective-permute-start | bytes 417800 | tf_op jit(solution)/shard_map/ppermute | solution.py:86
  18.3 6.6 %collective-permute-start.2 = (bf16[32,2176]{1,0:T(8,128)(2,1)S(1)}, bf16[32,2176]{1,0:T(8,128)(2,1)S(1)}, u32[]{:S(2)}, u32[]{:S(2)}) collective-permute-start(bf16[32,2176]{1,0:T(8,128)(2,1)S(1)} %collective-permute-done.refs_0_), channel_id=1, source_target_pairs={{0,1},{1,0},{2,3},{3,2},{4,5},{5,4},{6,7},{7,6},{8,9},{9,8},{10,11... | collective-permute-start | bytes 417800 | tf_op jit(solution)/shard_map/ppermute | solution.py:86
  18.7 9.1 %collective-permute-start.7 = (bf16[32,2176]{1,0:T(8,128)(2,1)S(1)}, bf16[32,2176]{1,0:T(8,128)(2,1)S(1)}, u32[]{:S(2)}, u32[]{:S(2)}) collective-permute-start(bf16[32,2176]{1,0:T(8,128)(2,1)S(1)} %collective-permute-done.3.refs_3_), channel_id=1, source_target_pairs={{0,3},{1,2},{2,1},{3,0},{4,7},{5,6},{6,5},{7,4},{8,11},{9,10},{10,... | collective-permute-start | bytes 417800 | tf_op jit(solution)/shard_map/ppermute | solution.py:86
  22.7 5.1 %collective-permute-start.6 = (bf16[32,2176]{1,0:T(8,128)(2,1)S(1)}, bf16[32,2176]{1,0:T(8,128)(2,1)S(1)}, u32[]{:S(2)}, u32[]{:S(2)}) collective-permute-start(bf16[32,2176]{1,0:T(8,128)(2,1)S(1)} %collective-permute-done.4.refs_4_), channel_id=1, source_target_pairs={{0,1},{1,0},{2,3},{3,2},{4,5},{5,4},{6,7},{7,6},{8,9},{9,8},{10,11... | collective-permute-start | bytes 417800 | tf_op jit(solution)/shard_map/ppermute | solution.py:86
  27.8 4.3 %copy-start.3 = (bf16[32,1,4096]{2,0,1:T(8,128)(2,1)S(1)}, bf16[32,1,4096]{2,0,1:T(8,128)(2,1)}, u32[]{:S(2)}) copy-start(bf16[32,1,4096]{2,0,1:T(8,128)(2,1)} %param.7) | copy-start | bytes 786436
  29.5 13.4 %collective-permute-start.10 = (bf16[64,2176]{1,0:T(8,128)(2,1)S(1)}, bf16[64,2176]{1,0:T(8,128)(2,1)S(1)}, u32[]{:S(2)}, u32[]{:S(2)}) collective-permute-start(bf16[64,2176]{1,0:T(8,128)(2,1)S(1)} %get-tuple-element.43), channel_id=1, source_target_pairs={{0,4},{1,5},{2,6},{3,7},{4,0},{5,1},{6,2},{7,3},{8,12},{9,13},{10,... | collective-permute-start | bytes 835592 | tf_op jit(solution)/shard_map/ppermute | solution.py:86
  31.1 11.7 %collective-permute-start.11 = (bf16[64,2176]{1,0:T(8,128)(2,1)S(1)}, bf16[64,2176]{1,0:T(8,128)(2,1)S(1)}, u32[]{:S(2)}, u32[]{:S(2)}) collective-permute-start(bf16[64,2176]{1,0:T(8,128)(2,1)S(1)} %get-tuple-element.44), channel_id=1, source_target_pairs={{0,244},{1,245},{2,246},{3,247},{4,16},{5,17},{6,18},{7,19},{8,252... | collective-permute-start | bytes 835592 | tf_op jit(solution)/shard_map/ppermute | solution.py:86
  32.1 8.9 %collective-permute-start.13 = (bf16[32,2176]{1,0:T(8,128)(2,1)S(1)}, bf16[32,2176]{1,0:T(8,128)(2,1)S(1)}, u32[]{:S(2)}, u32[]{:S(2)}) collective-permute-start(bf16[32,2176]{1,0:T(8,128)(2,1)S(1)} %get-tuple-element.74), channel_id=1, source_target_pairs={{0,8},{1,9},{2,10},{3,11},{4,0},{5,1},{6,2},{7,3},{8,12},{9,13},{1... | collective-permute-start | bytes 417800 | tf_op jit(solution)/shard_map/ppermute | solution.py:86
  36.5 6.4 %collective-permute-start.12 = (bf16[32,2176]{1,0:T(8,128)(2,1)S(1)}, bf16[32,2176]{1,0:T(8,128)(2,1)S(1)}, u32[]{:S(2)}, u32[]{:S(2)}) collective-permute-start(bf16[32,2176]{1,0:T(8,128)(2,1)S(1)} %get-tuple-element.75), channel_id=1, source_target_pairs={{0,0},{1,1},{2,2},{3,3},{4,8},{5,9},{6,10},{7,11},{8,4},{9,5},{10,... | collective-permute-start | bytes 417800 | tf_op jit(solution)/shard_map/ppermute | solution.py:86
  44.3 6.6 %collective-permute-start.15 = (bf16[64,2176]{1,0:T(8,128)(2,1)S(1)}, bf16[64,2176]{1,0:T(8,128)(2,1)S(1)}, u32[]{:S(2)}, u32[]{:S(2)}) collective-permute-start(bf16[64,2176]{1,0:T(8,128)(2,1)S(1)} %get-tuple-element.46.here), channel_id=1, source_target_pairs={{0,244},{1,245},{2,246},{3,247},{4,16},{5,17},{6,18},{7,19},{8,252... | collective-permute-start | bytes 835592 | tf_op jit(solution)/shard_map/ppermute | solution.py:86
  44.3 8.6 %collective-permute-start.14 = (bf16[64,2176]{1,0:T(8,128)(2,1)S(1)}, bf16[64,2176]{1,0:T(8,128)(2,1)S(1)}, u32[]{:S(2)}, u32[]{:S(2)}) collective-permute-start(bf16[64,2176]{1,0:T(8,128)(2,1)S(1)} %get-tuple-element.46.here), channel_id=1, source_target_pairs={{0,4},{1,5},{2,6},{3,7},{4,0},{5,1},{6,2},{7,3},{8,12},{9,13},{10,... | collective-permute-start | bytes 835592 | tf_op jit(solution)/shard_map/ppermute | solution.py:86
  50.0 4.7 %collective-permute-start.21 = (bf16[20,32,128]{2,1,0:T(8,128)(2,1)S(1)}, bf16[20,32,128]{2,1,0:T(8,128)(2,1)S(1)}, u32[]{:S(2)}, u32[]{:S(2)}) collective-permute-start(bf16[20,32,128]{2,1,0:T(8,128)(2,1)S(1)} %get-tuple-element.63), channel_id=1, source_target_pairs={{0,8},{1,9},{2,10},{3,11},{4,12},{5,13},{6,14},{7,15},{8,0},{9,1},... | collective-permute-start | bytes 491528 | tf_op jit(solution)/shard_map/ppermute | solution.py:86
  52.4 2.2 %collective-permute-start.23 = (bf16[18,32,128]{2,1,0:T(8,128)(2,1)S(1)}, bf16[18,32,128]{2,1,0:T(8,128)(2,1)S(1)}, u32[]{:S(2)}, u32[]{:S(2)}) collective-permute-start(bf16[18,32,128]{2,1,0:T(8,128)(2,1)S(1)} %get-tuple-element.65), channel_id=1, source_target_pairs={{0,8},{1,9},{2,10},{3,11},{4,12},{5,13},{6,14},{7,15},{8,0},{9,1},... | collective-permute-start | bytes 442376 | tf_op jit(solution)/shard_map/ppermute | solution.py:86
  54.5 1.5 %collective-permute-start.22 = (bf16[18,32,128]{2,1,0:T(8,128)(2,1)S(1)}, bf16[18,32,128]{2,1,0:T(8,128)(2,1)S(1)}, u32[]{:S(2)}, u32[]{:S(2)}) collective-permute-start(bf16[18,32,128]{2,1,0:T(8,128)(2,1)S(1)} %get-tuple-element.64), channel_id=1, source_target_pairs={{0,8},{1,9},{2,10},{3,11},{4,12},{5,13},{6,14},{7,15},{8,0},{9,1},... | collective-permute-start | bytes 442376 | tf_op jit(solution)/shard_map/ppermute | solution.py:86
  56.8 10.5 %collective-permute-start.24 = (bf16[56,8,128]{2,1,0:T(8,128)(2,1)S(1)}, bf16[56,8,128]{2,1,0:T(8,128)(2,1)S(1)}, u32[]{:S(2)}, u32[]{:S(2)}) collective-permute-start(bf16[56,8,128]{2,1,0:T(8,128)(2,1)S(1)} %get-tuple-element.67), channel_id=1, source_target_pairs={{0,64},{1,65},{2,66},{3,67},{4,68},{5,69},{6,70},{7,71},{8,72},{9,... | collective-permute-start | bytes 344072 | tf_op jit(solution)/shard_map/ppermute | solution.py:86
  56.9 11.7 %collective-permute-start.25 = (bf16[56,8,128]{2,1,0:T(8,128)(2,1)S(1)}, bf16[56,8,128]{2,1,0:T(8,128)(2,1)S(1)}, u32[]{:S(2)}, u32[]{:S(2)}) collective-permute-start(bf16[56,8,128]{2,1,0:T(8,128)(2,1)S(1)} %get-tuple-element.68), channel_id=1, source_target_pairs={{0,192},{1,193},{2,194},{3,195},{4,196},{5,197},{6,198},{7,199},{8... | collective-permute-start | bytes 344072 | tf_op jit(solution)/shard_map/ppermute | solution.py:86
  58.8 9.7 %collective-permute-start.26 = (bf16[56,8,128]{2,1,0:T(8,128)(2,1)S(1)}, bf16[56,8,128]{2,1,0:T(8,128)(2,1)S(1)}, u32[]{:S(2)}, u32[]{:S(2)}) collective-permute-start(bf16[56,8,128]{2,1,0:T(8,128)(2,1)S(1)} %get-tuple-element.69), channel_id=1, source_target_pairs={{0,128},{1,129},{2,130},{3,131},{4,132},{5,133},{6,134},{7,135},{8... | collective-permute-start | bytes 344072 | tf_op jit(solution)/shard_map/ppermute | solution.py:86
  64.2 27.9 %collective-permute-start.16 = (bf16[64,2048]{1,0:T(8,128)(2,1)S(1)}, bf16[64,2048]{1,0:T(8,128)(2,1)S(1)}, u32[]{:S(2)}, u32[]{:S(2)}) collective-permute-start(bf16[64,2048]{1,0:T(8,128)(2,1)S(1)} %get-tuple-element.49), channel_id=1, source_target_pairs={{0,1},{1,0},{2,3},{3,2},{4,5},{5,4},{6,7},{7,6},{8,9},{9,8},{10,11... | collective-permute-start | bytes 786440 | tf_op jit(solution)/shard_map/ppermute | solution.py:86
  65.6 28.1 %collective-permute-start.17 = (bf16[64,2048]{1,0:T(8,128)(2,1)S(1)}, bf16[64,2048]{1,0:T(8,128)(2,1)S(1)}, u32[]{:S(2)}, u32[]{:S(2)}) collective-permute-start(bf16[64,2048]{1,0:T(8,128)(2,1)S(1)} %get-tuple-element.50), channel_id=1, source_target_pairs={{0,3},{1,2},{2,1},{3,0},{4,7},{5,6},{6,5},{7,4},{8,11},{9,10},{10,... | collective-permute-start | bytes 786440 | tf_op jit(solution)/shard_map/ppermute | solution.py:86
  67.3 26.3 %collective-permute-start.18 = (bf16[64,2048]{1,0:T(8,128)(2,1)S(1)}, bf16[64,2048]{1,0:T(8,128)(2,1)S(1)}, u32[]{:S(2)}, u32[]{:S(2)}) collective-permute-start(bf16[64,2048]{1,0:T(8,128)(2,1)S(1)} %get-tuple-element.51), channel_id=1, source_target_pairs={{0,2},{1,3},{2,0},{3,1},{4,6},{5,7},{6,4},{7,5},{8,10},{9,11},{10,... | collective-permute-start | bytes 786440 | tf_op jit(solution)/shard_map/ppermute | solution.py:86
  69.2 6.5 %collective-permute-start.28 = (bf16[28,8,128]{2,1,0:T(8,128)(2,1)S(1)}, bf16[28,8,128]{2,1,0:T(8,128)(2,1)S(1)}, u32[]{:S(2)}, u32[]{:S(2)}) collective-permute-start(bf16[28,8,128]{2,1,0:T(8,128)(2,1)S(1)} %get-tuple-element.70.mine), channel_id=1, source_target_pairs={{0,16},{1,17},{2,18},{3,19},{4,20},{5,21},{6,22},{7,23},{8,24},{9,... | collective-permute-start | bytes 172040 | tf_op jit(solution)/shard_map/ppermute | solution.py:86
  71.2 8.2 %collective-permute-start.29 = (bf16[28,8,128]{2,1,0:T(8,128)(2,1)S(1)}, bf16[28,8,128]{2,1,0:T(8,128)(2,1)S(1)}, u32[]{:S(2)}, u32[]{:S(2)}) collective-permute-start(bf16[28,8,128]{2,1,0:T(8,128)(2,1)S(1)} %get-tuple-element.71), channel_id=1, source_target_pairs={{0,20},{1,21},{2,22},{3,23},{4,16},{5,17},{6,18},{7,19},{8,28},{9,... | collective-permute-start | bytes 172040 | tf_op jit(solution)/shard_map/ppermute | solution.py:86
  75.7 5.8 %collective-permute-start.27 = (bf16[28,8,128]{2,1,0:T(8,128)(2,1)S(1)}, bf16[28,8,128]{2,1,0:T(8,128)(2,1)S(1)}, u32[]{:S(2)}, u32[]{:S(2)}) collective-permute-start(bf16[28,8,128]{2,1,0:T(8,128)(2,1)S(1)} %get-tuple-element.71), channel_id=1, source_target_pairs={{0,4},{1,5},{2,6},{3,7},{4,0},{5,1},{6,2},{7,3},{8,12},{9,13},{10,... | collective-permute-start | bytes 172040 | tf_op jit(solution)/shard_map/ppermute | solution.py:86
  82.1 6.3 %collective-permute-start.30 = (bf16[28,8,128]{2,1,0:T(8,128)(2,1)S(1)}, bf16[28,8,128]{2,1,0:T(8,128)(2,1)S(1)}, u32[]{:S(2)}, u32[]{:S(2)}) collective-permute-start(bf16[28,8,128]{2,1,0:T(8,128)(2,1)S(1)} %shard_map.89.mine), channel_id=1, source_target_pairs={{0,48},{1,49},{2,50},{3,51},{4,52},{5,53},{6,54},{7,55},{8,56},{9,... | collective-permute-start | bytes 172040 | tf_op jit(solution)/shard_map/ppermute | solution.py:86
  89.1 7.3 %collective-permute-start.33 = (bf16[28,8,128]{2,1,0:T(8,128)(2,1)S(1)}, bf16[28,8,128]{2,1,0:T(8,128)(2,1)S(1)}, u32[]{:S(2)}, u32[]{:S(2)}) collective-permute-start(bf16[28,8,128]{2,1,0:T(8,128)(2,1)S(1)} %shard_map.90.refs_0_), channel_id=1, source_target_pairs={{0,128},{1,129},{2,130},{3,131},{4,132},{5,133},{6,134},{7,135},{8... | collective-permute-start | bytes 172040 | tf_op jit(solution)/shard_map/ppermute | solution.py:86
  89.9 6.5 %collective-permute-start.32 = (bf16[28,8,128]{2,1,0:T(8,128)(2,1)S(1)}, bf16[28,8,128]{2,1,0:T(8,128)(2,1)S(1)}, u32[]{:S(2)}, u32[]{:S(2)}) collective-permute-start(bf16[28,8,128]{2,1,0:T(8,128)(2,1)S(1)} %shard_map.90.refs_0_), channel_id=1, source_target_pairs={{0,192},{1,193},{2,194},{3,195},{4,196},{5,197},{6,198},{7,199},{8... | collective-permute-start | bytes 172040 | tf_op jit(solution)/shard_map/ppermute | solution.py:86
  92.0 4.3 %collective-permute-start.31 = (bf16[28,8,128]{2,1,0:T(8,128)(2,1)S(1)}, bf16[28,8,128]{2,1,0:T(8,128)(2,1)S(1)}, u32[]{:S(2)}, u32[]{:S(2)}) collective-permute-start(bf16[28,8,128]{2,1,0:T(8,128)(2,1)S(1)} %shard_map.90.refs_0_), channel_id=1, source_target_pairs={{0,64},{1,65},{2,66},{3,67},{4,68},{5,69},{6,70},{7,71},{8,72},{9,... | collective-permute-start | bytes 172040 | tf_op jit(solution)/shard_map/ppermute | solution.py:86
  94.3 9.8 %collective-permute-start.19 = (bf16[64,2048]{1,0:T(8,128)(2,1)S(1)}, bf16[64,2048]{1,0:T(8,128)(2,1)S(1)}, u32[]{:S(2)}, u32[]{:S(2)}) collective-permute-start(bf16[64,2048]{1,0:T(8,128)(2,1)S(1)} %get-tuple-element.54), channel_id=1, source_target_pairs={{0,0},{1,1},{2,2},{3,3},{4,8},{5,9},{6,10},{7,11},{8,4},{9,5},{10,... | collective-permute-start | bytes 786440 | tf_op jit(solution)/shard_map/ppermute | solution.py:86
  96.3 8.6 %collective-permute-start.20 = (bf16[64,2048]{1,0:T(8,128)(2,1)S(1)}, bf16[64,2048]{1,0:T(8,128)(2,1)S(1)}, u32[]{:S(2)}, u32[]{:S(2)}) collective-permute-start(bf16[64,2048]{1,0:T(8,128)(2,1)S(1)} %get-tuple-element.55), channel_id=1, source_target_pairs={{0,4},{1,5},{2,6},{3,7},{4,12},{5,13},{6,14},{7,15},{8,0},{9,1},{1... | collective-permute-start | bytes 786440 | tf_op jit(solution)/shard_map/ppermute | solution.py:86
  97.0 9.2 %collective-permute-start.34 = (bf16[28,32,128]{2,1,0:T(8,128)(2,1)S(1)}, bf16[28,32,128]{2,1,0:T(8,128)(2,1)S(1)}, u32[]{:S(2)}, u32[]{:S(2)}) collective-permute-start(bf16[28,32,128]{2,1,0:T(8,128)(2,1)S(1)} %shard_map.91.mine), channel_id=1, source_target_pairs={{0,8},{1,9},{2,10},{3,11},{4,12},{5,13},{6,14},{7,15},{8,0},{9,1},... | collective-permute-start | bytes 688136 | tf_op jit(solution)/shard_map/ppermute | solution.py:86

commit v3 on v2

--- a/solution.py
+++ b/solution.py
@@ -199,11 +199,18 @@
 
 
 def middle_body(place, *refs):
-    shards, weights, mid, own, window, moved = refs[:8], *refs[8:]
+    shards, weights, cot_own, cot_other, mid, own, cotangent, window, moved, cot = refs[:8], *refs[8:]
     gather_window(place, shards, window)
     own[...] = window[:, 2 * ROW : 2 * ROW + OWN]
     for cells, total in convolve(window, moved, weights, 64):
         mid[:, cells] = total
+    c = place[C]
+    cot[at(c, 32), :] = cot_own[...]
+    cot[at(1 - c, 32), :] = cot_other[...]
+    shift = pltpu.roll(cot[...].astype(F32), jnp.where(c == 0, ROW, GWIN - ROW), 1)
+    cell = lax.broadcasted_iota(jnp.int32, shift.shape, 1)
+    inside = (cell >= ROW * (1 - c)) & (cell < GWIN - ROW * c)
+    cotangent[...] = jnp.where(inside, shift, 0.0)
 
 
 def if_inner(place, values):
@@ -217,18 +224,11 @@
     return v, square, t
 
 
-def grad_body(place, mid, near, far, bias, cot_own, cot_other, grad, sums, cot):
-    c = place[C]
-    cot[at(c, 32), :] = cot_own[...]
-    cot[at(1 - c, 32), :] = cot_other[...]
-    moved = pltpu.roll(cot[...].astype(F32), jnp.where(c == 0, ROW, GWIN - ROW), 1)
-    cell = lax.broadcasted_iota(jnp.int32, moved.shape, 1)
-    inside = (cell >= ROW * (1 - c)) & (cell < GWIN - ROW * c)
-    cotangent = jnp.where(inside, moved, 0.0)
+def grad_body(place, mid, near, far, bias, cotangent, grad, sums):
     v, square, t = gelu_parts(place, mid, near, far, bias)
     inner = 0.7978845608028654 * (1.0 + 3 * 0.044715 * square)
     slope = 0.5 * (1.0 + t) + 0.5 * v * (1.0 - t * t) * inner
-    g = (cotangent * slope).astype(BF)
+    g = (cotangent[...] * slope).astype(BF)
     grad[...] = g
     sums[...] = jnp.sum(g.astype(F32)[:, ROW : ROW + OWN], axis=1, keepdims=True)
 
@@ -291,8 +291,10 @@
     send[18:] = halves(spread)
 
 
-def near_body(place, near, own, keep, send, stack):
+def near_body(place, near, own, here_keep, here_send, keep, send, stack):
     kernel_grads(place, near[...], own, keep, send, stack)
+    keep[18:] = here_keep[...]
+    send[18:] = here_send[...]
 
 
 def far_body(place, far, own, keep, send, stack):
@@ -333,12 +335,12 @@
         input_grad[:, at(half, OWN)] = part[32:, :]
 
 
-def fold_core_body(place, here, near, far, got_here, got_near, got_far, mine, *refs):
+def fold_core_body(place, near, far, got_near, got_far, mine, *refs):
     outs, total = refs[:3], refs[3]
     x, z = place[X], place[Z]
-    total[18:36] = here[:18] + got_here[:18].astype(F32)
-    total[54:] = here[18:] + whole(got_here[18:])
-    total[pl.ds(36 * z, 18)] = near[...] + got_near[...].astype(F32)
+    total[18:36] = near[18:36] + got_near[18:36].astype(F32)
+    total[54:] = near[36:] + whole(got_near[36:])
+    total[pl.ds(36 * z, 18)] = near[:18] + got_near[:18].astype(F32)
     total[pl.ds(36 * (1 - z), 18)] = far[...] + got_far[...].astype(F32)
     mine[...] = total[:, at(x, 8), :]
     for s, out in zip(PEERS, outs, strict=True):
@@ -436,29 +438,21 @@
         room=10,
     )
     near, far = exchange(near, other_z), exchange(far, far_plane)
-    mid, own = call(
+    mid, own, cotangent = call(
         middle_body,
-        (shape(64, GWIN, dtype=F32), shape(256, OWN)),
-        windows(256),
+        (shape(64, GWIN, dtype=F32), shape(256, OWN), shape(64, GWIN, dtype=F32)),
+        windows(256) + [pltpu.VMEM((64, GWIN), BF)],
         place,
         *shards,
         *last,
         middle_weights,
+        cot_own,
+        cot_other,
         flops=2 * 192 * 768 * GWIN,
         room=12,
     )
     grad, sums = call(
-        grad_body,
-        (shape(64, GWIN), shape(64, 1, dtype=F32)),
-        [pltpu.VMEM((64, GWIN), BF)],
-        place,
-        mid,
-        near,
-        far,
-        biases,
-        cot_own,
-        cot_other,
-        room=12,
+        grad_body, (shape(64, GWIN), shape(64, 1, dtype=F32)), [], place, mid, near, far, biases, cotangent, room=12
     )
     grad_near, grad_far = exchange(grad, other_z), exchange(grad, far_plane)
     act_own, act_other = call(
@@ -483,11 +477,10 @@
             flops=2 * 576 * 256 * OWN,
             room=8,
         )
-        return keep, exchange(send, other_core)
-
-    grads = [
-        wgrad(here_body, 20, grad, own, sums), wgrad(near_body, 18, grad_near, own), wgrad(far_body, 18, grad_far, own)
-    ]
+        return keep, send
+
+    grads = wgrad(here_body, 20, grad, own, sums)
+    keeps, sends = zip(wgrad(near_body, 38, grad_near, own, *grads), wgrad(far_body, 18, grad_far, own))
     pieces = call(
         input_grad_body,
         tuple(shape(64, OWN) for _ in STEPS),
@@ -517,8 +510,9 @@
         (shape(56, 8, 128, dtype=F32),) + (shape(56, 8, 128),) * 3,
         [pltpu.VMEM((56, 32, 128), F32)],
         place,
-        *[keep for keep, _ in grads],
-        *[got for _, got in grads],
+        *keeps,
+        exchange(sends[0], other_core),
+        exchange(sends[1], other_core),
     )
     got = [exchange(value, peer_x(s)) for s, value in zip(PEERS, sends)]
     eight = shape(28, 8, 128)

time: 109 us -> 110 us (level)
  waiting for transfers between devices: 20.9 us -> 27.3 us
  starting transfers between devices: 58 us -> 52.6 us
    ppermute x35 -> x34, waiting for transfers between devices: 20.9 us -> 27.3 us  [exchange(): return lax.ppermute(value, ('depth', 'filt'), pairs(move))]
    ppermute x35 -> x34, starting transfers between devices: 58 us -> 52.6 us  [exchange(): return lax.ppermute(value, ('depth', 'filt'), pairs(move))]
  transfers between devices with their start and end apart: 35 -> 34, of which waited for: 11 -> 12; matrix products, arithmetic and copies ran while one was open for 0% -> 0% of each run, Pallas kernels for 19% -> 19%
where the time goes in v3:
time: 110 us; the launch traced here: 109 us
  starting transfers between devices  52.6 us (48%)
  waiting for transfers between devices  27.3 us (25%)
  Pallas kernels  25.9 us (24%)
    ppermute x34, starting transfers between devices, exchange(): return lax.ppermute(value, ('depth', 'filt'), pairs(move))  52.6 us
    ppermute x34, waiting for transfers between devices, exchange(): return lax.ppermute(value, ('depth', 'filt'), pairs(move))  27.3 us
    pallas_call x18, Pallas kernels, call(): pl.pallas_call(body, out_shape=outs, in_specs=[SMEM] + [HBM if i in hbm_i...  25.9 us
  transfers between devices with their start and end apart: 34, of which 12 were waited for; matrix products, arithmetic and copies ran while one was open for 0% of the time, Pallas kernels for 19%

profile of v3, /device:TPU:32, one launch (start us, length us, event | category | flops | bytes accessed | tf_op | source)
XLA Modules:
  0.0 108.8 jit_solution(6238094998222249120)
XLA Ops:
  0.7 0.7 fusion
  1.4 0.9 constant_dynamic-slice_fusion
  2.5 2.0 %collective-permute-start.8 = (bf16[28,32,128]{2,1,0:T(8,128)(2,1)S(1)}, bf16[28,32,128]{2,1,0:T(8,128)(2,1)S(1)}, u32[]{:S(2)}, u32[]{:S(2)}) collective-permute-start(bf16[28,32,128]{2,1,0:T(8,128)(2,1)S(1)} %pad_maximum_fusion), channel_id=1, source_target_pairs={{0,52},{1,53},{2,54},{3,55},{4,16},{5,17},{6,18},{7,19},{8,60},{9,... | collective-permute-start | bytes 688136 | tf_op jit(solution)/shard_map/ppermute | solution.py:86
  4.6 4.1 %collective-permute-start.1 = (bf16[32,2176]{1,0:T(8,128)(2,1)S(1)}, bf16[32,2176]{1,0:T(8,128)(2,1)S(1)}, u32[]{:S(2)}, u32[]{:S(2)}) collective-permute-start(bf16[32,2176]{1,0:T(8,128)(2,1)S(1)} %get-tuple-element.78), channel_id=1, source_target_pairs={{0,8},{1,9},{2,10},{3,11},{4,0},{5,1},{6,2},{7,3},{8,12},{9,13},{1... | collective-permute-start | bytes 417800 | tf_op jit(solution)/shard_map/ppermute | solution.py:86
  8.7 1.9 %collective-permute-start = (bf16[32,2176]{1,0:T(8,128)(2,1)S(1)}, bf16[32,2176]{1,0:T(8,128)(2,1)S(1)}, u32[]{:S(2)}, u32[]{:S(2)}) collective-permute-start(bf16[32,2176]{1,0:T(8,128)(2,1)S(1)} %get-tuple-element.79), channel_id=1, source_target_pairs={{0,0},{1,1},{2,2},{3,3},{4,8},{5,9},{6,10},{7,11},{8,4},{9,5},{10,... | collective-permute-start | bytes 417800 | tf_op jit(solution)/shard_map/ppermute | solution.py:86
  11.3 1.6 %collective-permute-start.3 = (bf16[32,2176]{1,0:T(8,128)(2,1)S(1)}, bf16[32,2176]{1,0:T(8,128)(2,1)S(1)}, u32[]{:S(2)}, u32[]{:S(2)}) collective-permute-start(bf16[32,2176]{1,0:T(8,128)(2,1)S(1)} %collective-permute-done.1.refs_1_), channel_id=1, source_target_pairs={{0,1},{1,0},{2,3},{3,2},{4,5},{5,4},{6,7},{7,6},{8,9},{9,8},{10,11... | collective-permute-start | bytes 417800 | tf_op jit(solution)/shard_map/ppermute | solution.py:86
  12.9 2.2 %collective-permute-done.refs_0_ = bf16[32,2176]{1,0:T(8,128)(2,1)S(1)} collective-permute-done((bf16[32,2176]{1,0:T(8,128)(2,1)S(1)}, bf16[32,2176]{1,0:T(8,128)(2,1)S(1)}, u32[]{:S(2)}, u32[]{:S(2)}) %collective-permute-start) | collective-permute-done | bytes 139296 | tf_op jit(solution)/shard_map/ppermute | solution.py:86
  15.1 3.0 %collective-permute-start.4 = (bf16[32,2176]{1,0:T(8,128)(2,1)S(1)}, bf16[32,2176]{1,0:T(8,128)(2,1)S(1)}, u32[]{:S(2)}, u32[]{:S(2)}) collective-permute-start(bf16[32,2176]{1,0:T(8,128)(2,1)S(1)} %collective-permute-done.refs_0_), channel_id=1, source_target_pairs={{0,3},{1,2},{2,1},{3,0},{4,7},{5,6},{6,5},{7,4},{8,11},{9,10},{10,... | collective-permute-start | bytes 417800 | tf_op jit(solution)/shard_map/ppermute | solution.py:86
  18.7 2.7 %collective-permute-start.7 = (bf16[32,2176]{1,0:T(8,128)(2,1)S(1)}, bf16[32,2176]{1,0:T(8,128)(2,1)S(1)}, u32[]{:S(2)}, u32[]{:S(2)}) collective-permute-start(bf16[32,2176]{1,0:T(8,128)(2,1)S(1)} %collective-permute-done.3.refs_3_), channel_id=1, source_target_pairs={{0,3},{1,2},{2,1},{3,0},{4,7},{5,6},{6,5},{7,4},{8,11},{9,10},{10,... | collective-permute-start | bytes 417800 | tf_op jit(solution)/shard_map/ppermute | solution.py:86
  21.3 1.4 %collective-permute-done.4.refs_4_ = bf16[32,2176]{1,0:T(8,128)(2,1)S(1)} collective-permute-done((bf16[32,2176]{1,0:T(8,128)(2,1)S(1)}, bf16[32,2176]{1,0:T(8,128)(2,1)S(1)}, u32[]{:S(2)}, u32[]{:S(2)}) %collective-permute-start.4) | collective-permute-done | bytes 139296 | tf_op jit(solution)/shard_map/ppermute | solution.py:86
  23.1 1.8 %shard_map.75 = (bf16[384,576]{1,0:T(8,128)(2,1)S(1)}, bf16[384,192]{1,0:T(8,128)(2,1)S(1)}, bf16[192,768]{1,0:T(8,128)(2,1)S(1)}, bf16[256,1728]{1,0:T(8,128)(2,1)S(1)}, f32[64,128]{1,0:T(8,128)S(1)}) custom-call(s32[5]{0:T(128)S(1)} %stack.27.place, bf16[27,32,256]{2,1,0:T(8,128)(2,1)S(1)} %copy-done, ...), custom_call_target="tpu_custom_call" | custom-call | bytes 2000000 | tf_op jit(solution)/shard_map/pallas_call | solution.py:94
  24.9 2.8 %shard_map.77.part = f32[128,2176]{1,0:T(8,128)S(1)} custom-call(s32[5]{0:T(128)S(1)} %stack.27.place, bf16[32,2176]{1,0:T(8,128)(2,1)S(1)} %collective-permute-done.refs_0_, bf16[32,2176]{1,0:T(8,128)(2,1)S(1)} %collective-permute-done.1.refs_1_, bf16[32,2176]{1,0:T(8,128)(2,1)S(1)} %collective-permute-done.2.refs_2_, ...), custom_call_target="tpu_custom_call" | custom-call | flops 962592768 | bytes 2000000 | tf_op jit(solution)/shard_map/pallas_call | solution.py:94
  27.8 1.6 %shard_map.78 = (bf16[64,2176]{1,0:T(8,128)(2,1)S(1)}, bf16[64,2176]{1,0:T(8,128)(2,1)S(1)}) custom-call(s32[5]{0:T(128)S(1)} %stack.27.place, bf16[32,2176]{1,0:T(8,128)(2,1)S(1)} %collective-permute-done.6.refs_6_.one, bf16[32,2176]{1,0:T(8,128)(2,1)S(1)} %collective-permute-done.7.refs_7_.two, bf16[384,192]{1,0:T(8,128)(2,1)S(1)} %get-tuple-element.42.weights, ...), custom_call_target="tpu_custom_call" | custom-call | flops 320864256 | bytes 2000000 | tf_op jit(solution)/shard_map/pallas_call | solution.py:94
  29.5 1.6 %collective-permute-start.12 = (bf16[64,2176]{1,0:T(8,128)(2,1)S(1)}, bf16[64,2176]{1,0:T(8,128)(2,1)S(1)}, u32[]{:S(2)}, u32[]{:S(2)}) collective-permute-start(bf16[64,2176]{1,0:T(8,128)(2,1)S(1)} %get-tuple-element.44), channel_id=1, source_target_pairs={{0,4},{1,5},{2,6},{3,7},{4,0},{5,1},{6,2},{7,3},{8,12},{9,13},{10,... | collective-permute-start | bytes 835592 | tf_op jit(solution)/shard_map/ppermute | solution.py:86
  31.1 1.0 collective-permute-start.13
  32.1 4.3 %collective-permute-start.11 = (bf16[32,2176]{1,0:T(8,128)(2,1)S(1)}, bf16[32,2176]{1,0:T(8,128)(2,1)S(1)}, u32[]{:S(2)}, u32[]{:S(2)}) collective-permute-start(bf16[32,2176]{1,0:T(8,128)(2,1)S(1)} %get-tuple-element.76), channel_id=1, source_target_pairs={{0,8},{1,9},{2,10},{3,11},{4,0},{5,1},{6,2},{7,3},{8,12},{9,13},{1... | collective-permute-start | bytes 417800 | tf_op jit(solution)/shard_map/ppermute | solution.py:86
  36.5 2.1 %collective-permute-start.10 = (bf16[32,2176]{1,0:T(8,128)(2,1)S(1)}, bf16[32,2176]{1,0:T(8,128)(2,1)S(1)}, u32[]{:S(2)}, u32[]{:S(2)}) collective-permute-start(bf16[32,2176]{1,0:T(8,128)(2,1)S(1)} %get-tuple-element.77), channel_id=1, source_target_pairs={{0,0},{1,1},{2,2},{3,3},{4,8},{5,9},{6,10},{7,11},{8,4},{9,5},{10,... | collective-permute-start | bytes 417800 | tf_op jit(solution)/shard_map/ppermute | solution.py:86
  39.1 3.8 %collective-permute-done.10.refs_9_ = bf16[32,2176]{1,0:T(8,128)(2,1)S(1)} collective-permute-done((bf16[32,2176]{1,0:T(8,128)(2,1)S(1)}, bf16[32,2176]{1,0:T(8,128)(2,1)S(1)}, u32[]{:S(2)}, u32[]{:S(2)}) %collective-permute-start.10) | collective-permute-done | bytes 139296 | tf_op jit(solution)/shard_map/ppermute | solution.py:86
  42.8 2.7 %shard_map.76 = (f32[64,2176]{1,0:T(8,128)S(1)}, bf16[256,2048]{1,0:T(8,128)(2,1)S(1)}, f32[64,2176]{1,0:T(8,128)S(1)}) custom-call(s32[5]{0:T(128)S(1)} %stack.27.place, bf16[32,2176]{1,0:T(8,128)(2,1)S(1)} %collective-permute-done.refs_0_, bf16[32,2176]{1,0:T(8,128)(2,1)S(1)} %collective-permute-done.1.refs_1_, ...), custom_call_target="tpu_custom_call" | custom-call | flops 641728512 | bytes 2000000 | tf_op jit(solution)/shard_map/pallas_call | solution.py:94
  45.6 1.2 %shard_map.79 = (bf16[64,2176]{1,0:T(8,128)(2,1)S(1)}, f32[64,1]{1,0:T(8,128)S(1)}) custom-call(s32[5]{0:T(128)S(1)} %stack.27.place, f32[64,2176]{1,0:T(8,128)S(1)} %get-tuple-element.41.mid, bf16[64,2176]{1,0:T(8,128)(2,1)S(1)} %collective-permute-done.12.near, bf16[64,2176]{1,0:T(8,128)(2,1)S(1)} %collective-permute-done.13.far, ...), custom_call_target="tpu_custom_call" | custom-call | bytes 2000000 | tf_op jit(solution)/shard_map/pallas_call | solution.py:94
  46.9 1.5 %shard_map.84 = (f32[20,32,128]{2,1,0:T(8,128)S(1)}, bf16[20,32,128]{2,1,0:T(8,128)(2,1)S(1)}) custom-call(s32[5]{0:T(128)S(1)} %stack.27.place, bf16[64,2176]{1,0:T(8,128)(2,1)S(1)} %get-tuple-element.48.here, bf16[256,2048]{1,0:T(8,128)(2,1)S(1)} %get-tuple-element.60.own, f32[64,1]{1,0:T(8,128)S(1)} %get-tuple-element.61.sums), custom_call_target="tpu_custom_call" | custom-call | flops 603979776 | bytes 2000000 | tf_op jit(solution)/shard_map/pallas_call | solution.py:94
  48.5 5.6 %collective-permute-done.14.near = bf16[64,2176]{1,0:T(8,128)(2,1)S(1)} collective-permute-done((bf16[64,2176]{1,0:T(8,128)(2,1)S(1)}, bf16[64,2176]{1,0:T(8,128)(2,1)S(1)}, u32[]{:S(2)}, u32[]{:S(2)}) %collective-permute-start.14) | collective-permute-done | bytes 278560 | tf_op jit(solution)/shard_map/ppermute | solution.py:86
  54.0 1.5 %shard_map.85 = (f32[38,32,128]{2,1,0:T(8,128)S(1)}, bf16[38,32,128]{2,1,0:T(8,128)(2,1)S(1)}) custom-call(s32[5]{0:T(128)S(1)} %stack.27.place, bf16[64,2176]{1,0:T(8,128)(2,1)S(1)} %collective-permute-done.14.near, bf16[256,2048]{1,0:T(8,128)(2,1)S(1)} %get-tuple-element.60.own, f32[20,32,128]{2,1,0:T(8,128)S(1)} %get-tuple-element.62.here_keep, ...), custom_call_target="tpu_custom_call" | custom-call | flops 603979776 | bytes 2000000 | tf_op jit(solution)/shard_map/pallas_call | solution.py:94
  55.7 1.6 %shard_map.86 = (f32[18,32,128]{2,1,0:T(8,128)S(1)}, bf16[18,32,128]{2,1,0:T(8,128)(2,1)S(1)}) custom-call(s32[5]{0:T(128)S(1)} %stack.27.place, bf16[64,2176]{1,0:T(8,128)(2,1)S(1)} %collective-permute-done.15.far, bf16[256,2048]{1,0:T(8,128)(2,1)S(1)} %get-tuple-element.60.own), custom_call_target="tpu_custom_call" | custom-call | flops 603979776 | bytes 2000000 | tf_op jit(solution)/shard_map/pallas_call | solution.py:94
  57.8 1.0 collective-permute-done.22.got_far
  58.8 0.8 shard_map.87
  59.7 1.5 %collective-permute-start.24 = (bf16[56,8,128]{2,1,0:T(8,128)(2,1)S(1)}, bf16[56,8,128]{2,1,0:T(8,128)(2,1)S(1)}, u32[]{:S(2)}, u32[]{:S(2)}) collective-permute-start(bf16[56,8,128]{2,1,0:T(8,128)(2,1)S(1)} %get-tuple-element.70), channel_id=1, source_target_pairs={{0,192},{1,193},{2,194},{3,195},{4,196},{5,197},{6,198},{7,199},{8... | collective-permute-start | bytes 344072 | tf_op jit(solution)/shard_map/ppermute | solution.py:86
  61.3 2.5 %collective-permute-start.25 = (bf16[56,8,128]{2,1,0:T(8,128)(2,1)S(1)}, bf16[56,8,128]{2,1,0:T(8,128)(2,1)S(1)}, u32[]{:S(2)}, u32[]{:S(2)}) collective-permute-start(bf16[56,8,128]{2,1,0:T(8,128)(2,1)S(1)} %get-tuple-element.71), channel_id=1, source_target_pairs={{0,128},{1,129},{2,130},{3,131},{4,132},{5,133},{6,134},{7,135},{8... | collective-permute-start | bytes 344072 | tf_op jit(solution)/shard_map/ppermute | solution.py:86
  63.8 3.2 %shard_map.80 = (bf16[64,2048]{1,0:T(8,128)(2,1)S(1)}, bf16[64,2048]{1,0:T(8,128)(2,1)S(1)}, bf16[64,2048]{1,0:T(8,128)(2,1)S(1)}, bf16[64,2048]{1,0:T(8,128)(2,1)S(1)}) custom-call(s32[5]{0:T(128)S(1)} %stack.27.place, bf16[64,2176]{1,0:T(8,128)(2,1)S(1)} %collective-permute-done.14.near, bf16[64,2176]{1,0:T(8,128)(2,1)S(1)} %get-tuple-element.48.here, ...), custom_call_target="tpu_custom_call" | custom-call | flops 1811939328 | bytes 2000000 | tf_op jit(solution)/shard_map/pallas_call | solution.py:94
  67.0 1.0 collective-permute-start.16
  68.1 2.2 %collective-permute-start.17 = (bf16[64,2048]{1,0:T(8,128)(2,1)S(1)}, bf16[64,2048]{1,0:T(8,128)(2,1)S(1)}, u32[]{:S(2)}, u32[]{:S(2)}) collective-permute-start(bf16[64,2048]{1,0:T(8,128)(2,1)S(1)} %get-tuple-element.52), channel_id=1, source_target_pairs={{0,3},{1,2},{2,1},{3,0},{4,7},{5,6},{6,5},{7,4},{8,11},{9,10},{10,... | collective-permute-start | bytes 786440 | tf_op jit(solution)/shard_map/ppermute | solution.py:86
  70.2 1.0 collective-permute-start.18
  71.9 0.8 collective-permute-start.27
  72.6 4.1 %collective-permute-start.28 = (bf16[28,8,128]{2,1,0:T(8,128)(2,1)S(1)}, bf16[28,8,128]{2,1,0:T(8,128)(2,1)S(1)}, u32[]{:S(2)}, u32[]{:S(2)}) collective-permute-start(bf16[28,8,128]{2,1,0:T(8,128)(2,1)S(1)} %get-tuple-element.73), channel_id=1, source_target_pairs={{0,20},{1,21},{2,22},{3,23},{4,16},{5,17},{6,18},{7,19},{8,28},{9,... | collective-permute-start | bytes 172040 | tf_op jit(solution)/shard_map/ppermute | solution.py:86
  77.3 3.0 %collective-permute-start.26 = (bf16[28,8,128]{2,1,0:T(8,128)(2,1)S(1)}, bf16[28,8,128]{2,1,0:T(8,128)(2,1)S(1)}, u32[]{:S(2)}, u32[]{:S(2)}) collective-permute-start(bf16[28,8,128]{2,1,0:T(8,128)(2,1)S(1)} %get-tuple-element.73), channel_id=1, source_target_pairs={{0,4},{1,5},{2,6},{3,7},{4,0},{5,1},{6,2},{7,3},{8,12},{9,13},{10,... | collective-permute-start | bytes 172040 | tf_op jit(solution)/shard_map/ppermute | solution.py:86
  80.4 2.2 %collective-permute-done.26.from_z = bf16[28,8,128]{2,1,0:T(8,128)(2,1)S(1)} collective-permute-done((bf16[28,8,128]{2,1,0:T(8,128)(2,1)S(1)}, bf16[28,8,128]{2,1,0:T(8,128)(2,1)S(1)}, u32[]{:S(2)}, u32[]{:S(2)}) %collective-permute-start.26) | collective-permute-done | bytes 57376 | tf_op jit(solution)/shard_map/ppermute | solution.py:86
  83.2 2.7 %collective-permute-start.29 = (bf16[28,8,128]{2,1,0:T(8,128)(2,1)S(1)}, bf16[28,8,128]{2,1,0:T(8,128)(2,1)S(1)}, u32[]{:S(2)}, u32[]{:S(2)}) collective-permute-start(bf16[28,8,128]{2,1,0:T(8,128)(2,1)S(1)} %shard_map.89.mine), channel_id=1, source_target_pairs={{0,48},{1,49},{2,50},{3,51},{4,52},{5,53},{6,54},{7,55},{8,56},{9,... | collective-permute-start | bytes 172040 | tf_op jit(solution)/shard_map/ppermute | solution.py:86
  85.9 3.6 %collective-permute-done.29.got = bf16[28,8,128]{2,1,0:T(8,128)(2,1)S(1)} collective-permute-done((bf16[28,8,128]{2,1,0:T(8,128)(2,1)S(1)}, bf16[28,8,128]{2,1,0:T(8,128)(2,1)S(1)}, u32[]{:S(2)}, u32[]{:S(2)}) %collective-permute-start.29) | collective-permute-done | bytes 57376 | tf_op jit(solution)/shard_map/ppermute | solution.py:86
  90.1 0.9 collective-permute-start.32
  91.1 2.1 %collective-permute-start.31 = (bf16[28,8,128]{2,1,0:T(8,128)(2,1)S(1)}, bf16[28,8,128]{2,1,0:T(8,128)(2,1)S(1)}, u32[]{:S(2)}, u32[]{:S(2)}) collective-permute-start(bf16[28,8,128]{2,1,0:T(8,128)(2,1)S(1)} %shard_map.90.refs_0_), channel_id=1, source_target_pairs={{0,192},{1,193},{2,194},{3,195},{4,196},{5,197},{6,198},{7,199},{8... | collective-permute-start | bytes 172040 | tf_op jit(solution)/shard_map/ppermute | solution.py:86
  93.7 1.0 shard_map.81
  94.7 0.7 shard_map.82
  95.4 1.9 %collective-permute-start.19 = (bf16[64,2048]{1,0:T(8,128)(2,1)S(1)}, bf16[64,2048]{1,0:T(8,128)(2,1)S(1)}, u32[]{:S(2)}, u32[]{:S(2)}) collective-permute-start(bf16[64,2048]{1,0:T(8,128)(2,1)S(1)} %get-tuple-element.56), channel_id=1, source_target_pairs={{0,0},{1,1},{2,2},{3,3},{4,8},{5,9},{6,10},{7,11},{8,4},{9,5},{10,... | collective-permute-start | bytes 786440 | tf_op jit(solution)/shard_map/ppermute | solution.py:86
  98.0 1.9 %collective-permute-start.33 = (bf16[28,32,128]{2,1,0:T(8,128)(2,1)S(1)}, bf16[28,32,128]{2,1,0:T(8,128)(2,1)S(1)}, u32[]{:S(2)}, u32[]{:S(2)}) collective-permute-start(bf16[28,32,128]{2,1,0:T(8,128)(2,1)S(1)} %shard_map.91.mine), channel_id=1, source_target_pairs={{0,8},{1,9},{2,10},{3,11},{4,12},{5,13},{6,14},{7,15},{8,0},{9,1},... | collective-permute-start | bytes 688136 | tf_op jit(solution)/shard_map/ppermute | solution.py:86
  99.9 5.2 %collective-permute-done.19.direct = bf16[64,2048]{1,0:T(8,128)(2,1)S(1)} collective-permute-done((bf16[64,2048]{1,0:T(8,128)(2,1)S(1)}, bf16[64,2048]{1,0:T(8,128)(2,1)S(1)}, u32[]{:S(2)}, u32[]{:S(2)}) %collective-permute-start.19) | collective-permute-done | bytes 262176 | tf_op jit(solution)/shard_map/ppermute | solution.py:86
  105.2 0.7 collective-permute-done.20.crossed
  105.9 1.4 %shard_map.83 = (bf16[32,4096]{1,0:T(8,128)(2,1)}, bf16[32,4096]{1,0:T(8,128)(2,1)}) custom-call(s32[5]{0:T(128)S(1)} %stack.27.place, bf16[64,2048]{1,0:T(8,128)(2,1)S(1)} %collective-permute-done.19.direct, bf16[64,2048]{1,0:T(8,128)(2,1)S(1)} %collective-permute-done.20.crossed), custom_call_target="tpu_custom_call" | custom-call | bytes 2000000 | tf_op jit(solution)/shard_map/pallas_call | solution.py:94
  107.2 1.6 %shard_map.92 = (f32[27,32,256]{2,1,0:T(8,128)}, f32[1,32]{1,0:T(1,128)}) custom-call(s32[5]{0:T(128)S(1)} %stack.27.place, bf16[28,32,128]{2,1,0:T(8,128)(2,1)S(1)} %shard_map.91.mine, bf16[28,32,128]{2,1,0:T(8,128)(2,1)S(1)} %collective-permute-done.33.other), custom_call_target="tpu_custom_call" | custom-call | bytes 2000000 | tf_op jit(solution)/shard_map/pallas_call | solution.py:94
  (54 shorter events, 6.9 us)
Async XLA Ops:
  0.6 22.5 %copy-start.1 = (f32[32]{0:T(128)S(1)}, f32[32]{0:T(128)}, u32[]{:S(2)}) copy-start(f32[32]{0:T(128)} %param.6) | copy-start | bytes 388
  0.6 22.5 %copy-start = (bf16[27,32,256]{2,1,0:T(8,128)(2,1)S(1)}, bf16[27,32,256]{2,1,0:T(8,128)(2,1)}, u32[]{:S(2)}) copy-start(bf16[27,32,256]{2,1,0:T(8,128)(2,1)} %mine.1) | copy-start | bytes 1327108
  0.7 3.9 %copy-start.2 = (bf16[32,1,4096]{2,0,1:T(8,128)(2,1)S(1)}, bf16[32,1,4096]{2,0,1:T(8,128)(2,1)}, u32[]{:S(2)}) copy-start(bf16[32,1,4096]{2,0,1:T(8,128)(2,1)} %param.4) | copy-start | bytes 786436
  2.5 8.1 %collective-permute-start.8 = (bf16[28,32,128]{2,1,0:T(8,128)(2,1)S(1)}, bf16[28,32,128]{2,1,0:T(8,128)(2,1)S(1)}, u32[]{:S(2)}, u32[]{:S(2)}) collective-permute-start(bf16[28,32,128]{2,1,0:T(8,128)(2,1)S(1)} %pad_maximum_fusion), channel_id=1, source_target_pairs={{0,52},{1,53},{2,54},{3,55},{4,16},{5,17},{6,18},{7,19},{8,60},{9,... | collective-permute-start | bytes 688136 | tf_op jit(solution)/shard_map/ppermute | solution.py:86
  4.6 6.7 %collective-permute-start.1 = (bf16[32,2176]{1,0:T(8,128)(2,1)S(1)}, bf16[32,2176]{1,0:T(8,128)(2,1)S(1)}, u32[]{:S(2)}, u32[]{:S(2)}) collective-permute-start(bf16[32,2176]{1,0:T(8,128)(2,1)S(1)} %get-tuple-element.78), channel_id=1, source_target_pairs={{0,8},{1,9},{2,10},{3,11},{4,0},{5,1},{6,2},{7,3},{8,12},{9,13},{1... | collective-permute-start | bytes 417800 | tf_op jit(solution)/shard_map/ppermute | solution.py:86
  8.7 6.4 %collective-permute-start = (bf16[32,2176]{1,0:T(8,128)(2,1)S(1)}, bf16[32,2176]{1,0:T(8,128)(2,1)S(1)}, u32[]{:S(2)}, u32[]{:S(2)}) collective-permute-start(bf16[32,2176]{1,0:T(8,128)(2,1)S(1)} %get-tuple-element.79), channel_id=1, source_target_pairs={{0,0},{1,1},{2,2},{3,3},{4,8},{5,9},{6,10},{7,11},{8,4},{9,5},{10,... | collective-permute-start | bytes 417800 | tf_op jit(solution)/shard_map/ppermute | solution.py:86
  10.6 12.5 %collective-permute-start.9 = (bf16[28,32,128]{2,1,0:T(8,128)(2,1)S(1)}, bf16[28,32,128]{2,1,0:T(8,128)(2,1)S(1)}, u32[]{:S(2)}, u32[]{:S(2)}) collective-permute-start(bf16[28,32,128]{2,1,0:T(8,128)(2,1)S(1)} %collective-permute-done.8.partner), channel_id=1, source_target_pairs={{0,8},{1,9},{2,10},{3,11},{4,12},{5,13},{6,14},{7,15},{8,0},{9,1},... | collective-permute-start | bytes 688136 | tf_op jit(solution)/shard_map/ppermute | solution.py:86
  11.3 7.4 %collective-permute-start.3 = (bf16[32,2176]{1,0:T(8,128)(2,1)S(1)}, bf16[32,2176]{1,0:T(8,128)(2,1)S(1)}, u32[]{:S(2)}, u32[]{:S(2)}) collective-permute-start(bf16[32,2176]{1,0:T(8,128)(2,1)S(1)} %collective-permute-done.1.refs_1_), channel_id=1, source_target_pairs={{0,1},{1,0},{2,3},{3,2},{4,5},{5,4},{6,7},{7,6},{8,9},{9,8},{10,11... | collective-permute-start | bytes 417800 | tf_op jit(solution)/shard_map/ppermute | solution.py:86
  15.1 7.7 %collective-permute-start.4 = (bf16[32,2176]{1,0:T(8,128)(2,1)S(1)}, bf16[32,2176]{1,0:T(8,128)(2,1)S(1)}, u32[]{:S(2)}, u32[]{:S(2)}) collective-permute-start(bf16[32,2176]{1,0:T(8,128)(2,1)S(1)} %collective-permute-done.refs_0_), channel_id=1, source_target_pairs={{0,3},{1,2},{2,1},{3,0},{4,7},{5,6},{6,5},{7,4},{8,11},{9,10},{10,... | collective-permute-start | bytes 417800 | tf_op jit(solution)/shard_map/ppermute | solution.py:86
  18.1 6.9 %collective-permute-start.5 = (bf16[32,2176]{1,0:T(8,128)(2,1)S(1)}, bf16[32,2176]{1,0:T(8,128)(2,1)S(1)}, u32[]{:S(2)}, u32[]{:S(2)}) collective-permute-start(bf16[32,2176]{1,0:T(8,128)(2,1)S(1)} %collective-permute-done.1.refs_1_), channel_id=1, source_target_pairs={{0,3},{1,2},{2,1},{3,0},{4,7},{5,6},{6,5},{7,4},{8,11},{9,10},{10,... | collective-permute-start | bytes 417800 | tf_op jit(solution)/shard_map/ppermute | solution.py:86
  18.3 6.6 %collective-permute-start.2 = (bf16[32,2176]{1,0:T(8,128)(2,1)S(1)}, bf16[32,2176]{1,0:T(8,128)(2,1)S(1)}, u32[]{:S(2)}, u32[]{:S(2)}) collective-permute-start(bf16[32,2176]{1,0:T(8,128)(2,1)S(1)} %collective-permute-done.refs_0_), channel_id=1, source_target_pairs={{0,1},{1,0},{2,3},{3,2},{4,5},{5,4},{6,7},{7,6},{8,9},{9,8},{10,11... | collective-permute-start | bytes 417800 | tf_op jit(solution)/shard_map/ppermute | solution.py:86
  18.7 9.1 %collective-permute-start.7 = (bf16[32,2176]{1,0:T(8,128)(2,1)S(1)}, bf16[32,2176]{1,0:T(8,128)(2,1)S(1)}, u32[]{:S(2)}, u32[]{:S(2)}) collective-permute-start(bf16[32,2176]{1,0:T(8,128)(2,1)S(1)} %collective-permute-done.3.refs_3_), channel_id=1, source_target_pairs={{0,3},{1,2},{2,1},{3,0},{4,7},{5,6},{6,5},{7,4},{8,11},{9,10},{10,... | collective-permute-start | bytes 417800 | tf_op jit(solution)/shard_map/ppermute | solution.py:86
  22.7 5.1 %collective-permute-start.6 = (bf16[32,2176]{1,0:T(8,128)(2,1)S(1)}, bf16[32,2176]{1,0:T(8,128)(2,1)S(1)}, u32[]{:S(2)}, u32[]{:S(2)}) collective-permute-start(bf16[32,2176]{1,0:T(8,128)(2,1)S(1)} %collective-permute-done.4.refs_4_), channel_id=1, source_target_pairs={{0,1},{1,0},{2,3},{3,2},{4,5},{5,4},{6,7},{7,6},{8,9},{9,8},{10,11... | collective-permute-start | bytes 417800 | tf_op jit(solution)/shard_map/ppermute | solution.py:86
  27.8 4.3 %copy-start.3 = (bf16[32,1,4096]{2,0,1:T(8,128)(2,1)S(1)}, bf16[32,1,4096]{2,0,1:T(8,128)(2,1)}, u32[]{:S(2)}) copy-start(bf16[32,1,4096]{2,0,1:T(8,128)(2,1)} %param.7) | copy-start | bytes 786436
  29.5 16.1 %collective-permute-start.12 = (bf16[64,2176]{1,0:T(8,128)(2,1)S(1)}, bf16[64,2176]{1,0:T(8,128)(2,1)S(1)}, u32[]{:S(2)}, u32[]{:S(2)}) collective-permute-start(bf16[64,2176]{1,0:T(8,128)(2,1)S(1)} %get-tuple-element.44), channel_id=1, source_target_pairs={{0,4},{1,5},{2,6},{3,7},{4,0},{5,1},{6,2},{7,3},{8,12},{9,13},{10,... | collective-permute-start | bytes 835592 | tf_op jit(solution)/shard_map/ppermute | solution.py:86
  31.1 14.5 %collective-permute-start.13 = (bf16[64,2176]{1,0:T(8,128)(2,1)S(1)}, bf16[64,2176]{1,0:T(8,128)(2,1)S(1)}, u32[]{:S(2)}, u32[]{:S(2)}) collective-permute-start(bf16[64,2176]{1,0:T(8,128)(2,1)S(1)} %get-tuple-element.45), channel_id=1, source_target_pairs={{0,244},{1,245},{2,246},{3,247},{4,16},{5,17},{6,18},{7,19},{8,252... | collective-permute-start | bytes 835592 | tf_op jit(solution)/shard_map/ppermute | solution.py:86
  32.1 6.9 %collective-permute-start.11 = (bf16[32,2176]{1,0:T(8,128)(2,1)S(1)}, bf16[32,2176]{1,0:T(8,128)(2,1)S(1)}, u32[]{:S(2)}, u32[]{:S(2)}) collective-permute-start(bf16[32,2176]{1,0:T(8,128)(2,1)S(1)} %get-tuple-element.76), channel_id=1, source_target_pairs={{0,8},{1,9},{2,10},{3,11},{4,0},{5,1},{6,2},{7,3},{8,12},{9,13},{1... | collective-permute-start | bytes 417800 | tf_op jit(solution)/shard_map/ppermute | solution.py:86
  36.5 6.4 %collective-permute-start.10 = (bf16[32,2176]{1,0:T(8,128)(2,1)S(1)}, bf16[32,2176]{1,0:T(8,128)(2,1)S(1)}, u32[]{:S(2)}, u32[]{:S(2)}) collective-permute-start(bf16[32,2176]{1,0:T(8,128)(2,1)S(1)} %get-tuple-element.77), channel_id=1, source_target_pairs={{0,0},{1,1},{2,2},{3,3},{4,8},{5,9},{6,10},{7,11},{8,4},{9,5},{10,... | collective-permute-start | bytes 417800 | tf_op jit(solution)/shard_map/ppermute | solution.py:86
  46.8 7.3 %collective-permute-start.14 = (bf16[64,2176]{1,0:T(8,128)(2,1)S(1)}, bf16[64,2176]{1,0:T(8,128)(2,1)S(1)}, u32[]{:S(2)}, u32[]{:S(2)}) collective-permute-start(bf16[64,2176]{1,0:T(8,128)(2,1)S(1)} %get-tuple-element.48.here), channel_id=1, source_target_pairs={{0,4},{1,5},{2,6},{3,7},{4,0},{5,1},{6,2},{7,3},{8,12},{9,13},{10,... | collective-permute-start | bytes 835592 | tf_op jit(solution)/shard_map/ppermute | solution.py:86
  46.8 8.9 %collective-permute-start.15 = (bf16[64,2176]{1,0:T(8,128)(2,1)S(1)}, bf16[64,2176]{1,0:T(8,128)(2,1)S(1)}, u32[]{:S(2)}, u32[]{:S(2)}) collective-permute-start(bf16[64,2176]{1,0:T(8,128)(2,1)S(1)} %get-tuple-element.48.here), channel_id=1, source_target_pairs={{0,244},{1,245},{2,246},{3,247},{4,16},{5,17},{6,18},{7,19},{8,252... | collective-permute-start | bytes 835592 | tf_op jit(solution)/shard_map/ppermute | solution.py:86
  55.6 3.3 %collective-permute-start.21 = (bf16[38,32,128]{2,1,0:T(8,128)(2,1)S(1)}, bf16[38,32,128]{2,1,0:T(8,128)(2,1)S(1)}, u32[]{:S(2)}, u32[]{:S(2)}) collective-permute-start(bf16[38,32,128]{2,1,0:T(8,128)(2,1)S(1)} %get-tuple-element.66), channel_id=1, source_target_pairs={{0,8},{1,9},{2,10},{3,11},{4,12},{5,13},{6,14},{7,15},{8,0},{9,1},... | collective-permute-start | bytes 933896 | tf_op jit(solution)/shard_map/ppermute | solution.py:86
  57.2 1.6 %collective-permute-start.22 = (bf16[18,32,128]{2,1,0:T(8,128)(2,1)S(1)}, bf16[18,32,128]{2,1,0:T(8,128)(2,1)S(1)}, u32[]{:S(2)}, u32[]{:S(2)}) collective-permute-start(bf16[18,32,128]{2,1,0:T(8,128)(2,1)S(1)} %get-tuple-element.67), channel_id=1, source_target_pairs={{0,8},{1,9},{2,10},{3,11},{4,12},{5,13},{6,14},{7,15},{8,0},{9,1},... | collective-permute-start | bytes 442376 | tf_op jit(solution)/shard_map/ppermute | solution.py:86
  59.6 10.6 %collective-permute-start.23 = (bf16[56,8,128]{2,1,0:T(8,128)(2,1)S(1)}, bf16[56,8,128]{2,1,0:T(8,128)(2,1)S(1)}, u32[]{:S(2)}, u32[]{:S(2)}) collective-permute-start(bf16[56,8,128]{2,1,0:T(8,128)(2,1)S(1)} %get-tuple-element.69), channel_id=1, source_target_pairs={{0,64},{1,65},{2,66},{3,67},{4,68},{5,69},{6,70},{7,71},{8,72},{9,... | collective-permute-start | bytes 344072 | tf_op jit(solution)/shard_map/ppermute | solution.py:86
  59.7 11.5 %collective-permute-start.24 = (bf16[56,8,128]{2,1,0:T(8,128)(2,1)S(1)}, bf16[56,8,128]{2,1,0:T(8,128)(2,1)S(1)}, u32[]{:S(2)}, u32[]{:S(2)}) collective-permute-start(bf16[56,8,128]{2,1,0:T(8,128)(2,1)S(1)} %get-tuple-element.70), channel_id=1, source_target_pairs={{0,192},{1,193},{2,194},{3,195},{4,196},{5,197},{6,198},{7,199},{8... | collective-permute-start | bytes 344072 | tf_op jit(solution)/shard_map/ppermute | solution.py:86
  61.3 9.9 %collective-permute-start.25 = (bf16[56,8,128]{2,1,0:T(8,128)(2,1)S(1)}, bf16[56,8,128]{2,1,0:T(8,128)(2,1)S(1)}, u32[]{:S(2)}, u32[]{:S(2)}) collective-permute-start(bf16[56,8,128]{2,1,0:T(8,128)(2,1)S(1)} %get-tuple-element.71), channel_id=1, source_target_pairs={{0,128},{1,129},{2,130},{3,131},{4,132},{5,133},{6,134},{7,135},{8... | collective-permute-start | bytes 344072 | tf_op jit(solution)/shard_map/ppermute | solution.py:86
  67.0 26.2 %collective-permute-start.16 = (bf16[64,2048]{1,0:T(8,128)(2,1)S(1)}, bf16[64,2048]{1,0:T(8,128)(2,1)S(1)}, u32[]{:S(2)}, u32[]{:S(2)}) collective-permute-start(bf16[64,2048]{1,0:T(8,128)(2,1)S(1)} %get-tuple-element.51), channel_id=1, source_target_pairs={{0,1},{1,0},{2,3},{3,2},{4,5},{5,4},{6,7},{7,6},{8,9},{9,8},{10,11... | collective-permute-start | bytes 786440 | tf_op jit(solution)/shard_map/ppermute | solution.py:86
  68.1 26.6 %collective-permute-start.17 = (bf16[64,2048]{1,0:T(8,128)(2,1)S(1)}, bf16[64,2048]{1,0:T(8,128)(2,1)S(1)}, u32[]{:S(2)}, u32[]{:S(2)}) collective-permute-start(bf16[64,2048]{1,0:T(8,128)(2,1)S(1)} %get-tuple-element.52), channel_id=1, source_target_pairs={{0,3},{1,2},{2,1},{3,0},{4,7},{5,6},{6,5},{7,4},{8,11},{9,10},{10,... | collective-permute-start | bytes 786440 | tf_op jit(solution)/shard_map/ppermute | solution.py:86
  70.2 24.4 %collective-permute-start.18 = (bf16[64,2048]{1,0:T(8,128)(2,1)S(1)}, bf16[64,2048]{1,0:T(8,128)(2,1)S(1)}, u32[]{:S(2)}, u32[]{:S(2)}) collective-permute-start(bf16[64,2048]{1,0:T(8,128)(2,1)S(1)} %get-tuple-element.53), channel_id=1, source_target_pairs={{0,2},{1,3},{2,0},{3,1},{4,6},{5,7},{6,4},{7,5},{8,10},{9,11},{10,... | collective-permute-start | bytes 786440 | tf_op jit(solution)/shard_map/ppermute | solution.py:86
  71.9 5.5 %collective-permute-start.27 = (bf16[28,8,128]{2,1,0:T(8,128)(2,1)S(1)}, bf16[28,8,128]{2,1,0:T(8,128)(2,1)S(1)}, u32[]{:S(2)}, u32[]{:S(2)}) collective-permute-start(bf16[28,8,128]{2,1,0:T(8,128)(2,1)S(1)} %get-tuple-element.72.mine), channel_id=1, source_target_pairs={{0,16},{1,17},{2,18},{3,19},{4,20},{5,21},{6,22},{7,23},{8,24},{9,... | collective-permute-start | bytes 172040 | tf_op jit(solution)/shard_map/ppermute | solution.py:86
  72.6 7.8 %collective-permute-start.28 = (bf16[28,8,128]{2,1,0:T(8,128)(2,1)S(1)}, bf16[28,8,128]{2,1,0:T(8,128)(2,1)S(1)}, u32[]{:S(2)}, u32[]{:S(2)}) collective-permute-start(bf16[28,8,128]{2,1,0:T(8,128)(2,1)S(1)} %get-tuple-element.73), channel_id=1, source_target_pairs={{0,20},{1,21},{2,22},{3,23},{4,16},{5,17},{6,18},{7,19},{8,28},{9,... | collective-permute-start | bytes 172040 | tf_op jit(solution)/shard_map/ppermute | solution.py:86
  77.3 5.2 %collective-permute-start.26 = (bf16[28,8,128]{2,1,0:T(8,128)(2,1)S(1)}, bf16[28,8,128]{2,1,0:T(8,128)(2,1)S(1)}, u32[]{:S(2)}, u32[]{:S(2)}) collective-permute-start(bf16[28,8,128]{2,1,0:T(8,128)(2,1)S(1)} %get-tuple-element.73), channel_id=1, source_target_pairs={{0,4},{1,5},{2,6},{3,7},{4,0},{5,1},{6,2},{7,3},{8,12},{9,13},{10,... | collective-permute-start | bytes 172040 | tf_op jit(solution)/shard_map/ppermute | solution.py:86
  83.2 6.3 %collective-permute-start.29 = (bf16[28,8,128]{2,1,0:T(8,128)(2,1)S(1)}, bf16[28,8,128]{2,1,0:T(8,128)(2,1)S(1)}, u32[]{:S(2)}, u32[]{:S(2)}) collective-permute-start(bf16[28,8,128]{2,1,0:T(8,128)(2,1)S(1)} %shard_map.89.mine), channel_id=1, source_target_pairs={{0,48},{1,49},{2,50},{3,51},{4,52},{5,53},{6,54},{7,55},{8,56},{9,... | collective-permute-start | bytes 172040 | tf_op jit(solution)/shard_map/ppermute | solution.py:86
  90.1 7.3 %collective-permute-start.32 = (bf16[28,8,128]{2,1,0:T(8,128)(2,1)S(1)}, bf16[28,8,128]{2,1,0:T(8,128)(2,1)S(1)}, u32[]{:S(2)}, u32[]{:S(2)}) collective-permute-start(bf16[28,8,128]{2,1,0:T(8,128)(2,1)S(1)} %shard_map.90.refs_0_), channel_id=1, source_target_pairs={{0,128},{1,129},{2,130},{3,131},{4,132},{5,133},{6,134},{7,135},{8... | collective-permute-start | bytes 172040 | tf_op jit(solution)/shard_map/ppermute | solution.py:86
  91.1 6.3 %collective-permute-start.31 = (bf16[28,8,128]{2,1,0:T(8,128)(2,1)S(1)}, bf16[28,8,128]{2,1,0:T(8,128)(2,1)S(1)}, u32[]{:S(2)}, u32[]{:S(2)}) collective-permute-start(bf16[28,8,128]{2,1,0:T(8,128)(2,1)S(1)} %shard_map.90.refs_0_), channel_id=1, source_target_pairs={{0,192},{1,193},{2,194},{3,195},{4,196},{5,197},{6,198},{7,199},{8... | collective-permute-start | bytes 172040 | tf_op jit(solution)/shard_map/ppermute | solution.py:86
  93.2 4.2 %collective-permute-start.30 = (bf16[28,8,128]{2,1,0:T(8,128)(2,1)S(1)}, bf16[28,8,128]{2,1,0:T(8,128)(2,1)S(1)}, u32[]{:S(2)}, u32[]{:S(2)}) collective-permute-start(bf16[28,8,128]{2,1,0:T(8,128)(2,1)S(1)} %shard_map.90.refs_0_), channel_id=1, source_target_pairs={{0,64},{1,65},{2,66},{3,67},{4,68},{5,69},{6,70},{7,71},{8,72},{9,... | collective-permute-start | bytes 172040 | tf_op jit(solution)/shard_map/ppermute | solution.py:86
  95.4 9.8 %collective-permute-start.19 = (bf16[64,2048]{1,0:T(8,128)(2,1)S(1)}, bf16[64,2048]{1,0:T(8,128)(2,1)S(1)}, u32[]{:S(2)}, u32[]{:S(2)}) collective-permute-start(bf16[64,2048]{1,0:T(8,128)(2,1)S(1)} %get-tuple-element.56), channel_id=1, source_target_pairs={{0,0},{1,1},{2,2},{3,3},{4,8},{5,9},{6,10},{7,11},{8,4},{9,5},{10,... | collective-permute-start | bytes 786440 | tf_op jit(solution)/shard_map/ppermute | solution.py:86
  97.3 8.6 %collective-permute-start.20 = (bf16[64,2048]{1,0:T(8,128)(2,1)S(1)}, bf16[64,2048]{1,0:T(8,128)(2,1)S(1)}, u32[]{:S(2)}, u32[]{:S(2)}) collective-permute-start(bf16[64,2048]{1,0:T(8,128)(2,1)S(1)} %get-tuple-element.57), channel_id=1, source_target_pairs={{0,4},{1,5},{2,6},{3,7},{4,12},{5,13},{6,14},{7,15},{8,0},{9,1},{1... | collective-permute-start | bytes 786440 | tf_op jit(solution)/shard_map/ppermute | solution.py:86
  98.0 9.2 %collective-permute-start.33 = (bf16[28,32,128]{2,1,0:T(8,128)(2,1)S(1)}, bf16[28,32,128]{2,1,0:T(8,128)(2,1)S(1)}, u32[]{:S(2)}, u32[]{:S(2)}) collective-permute-start(bf16[28,32,128]{2,1,0:T(8,128)(2,1)S(1)} %shard_map.91.mine), channel_id=1, source_target_pairs={{0,8},{1,9},{2,10},{3,11},{4,12},{5,13},{6,14},{7,15},{8,0},{9,1},... | collective-permute-start | bytes 688136 | tf_op jit(solution)/shard_map/ppermute | solution.py:86
